TPU v7x, 32 devices: a whole 2x2x4 slice. The times are simulated.
32 devices in a mesh: dp: 8 (over z, x), obj: 4 (over y, core).
Axes of the slice: x: 2, y: 2, z: 4, core: 2. Of those that a mesh axis runs over, the one named last changes fastest.
Arguments:
- object_field: float32 [2, 2048, 2048], P(None, 'dp', 'obj'), may hold values from -6 to 6
- probe_modes: float32 [4, 2, 256, 256], replicated, may hold values from -3 to 3
- amplitude: float32 [192, 256, 256], P(('dp', 'obj')), may hold values from 0.3 to 5
- offsets: int32 [192, 2], P(('dp', 'obj')), may hold values from -128 to 1919, as said below
Outputs:
- object_out: float32 [2, 2048, 2048], P(None, 'dp', 'obj')
- probe_out: float32 [4, 2, 256, 256], replicated
Inputs may be any that keep to these rules, and one draw needn't show every extreme that they name: `offsets`: the position in slot n of a device's 6 slots has its patch centre (offset plus 256 / 2 in both coordinates) inside that device's tile of 256 x 512 object pixels; on every device one position's centre is the tile's first pixel and one is its last pixel.
All inputs are finite; a program needn't handle non-finite values.
Results may differ from a plain program's by a relative error of at most 0.003.
Values may be sent and summed in bfloat16 or wider, within the bound.
No kernel may reach another device: no remote copies, remote signals or barrier semaphores. Data moves between devices by JAX's collectives and lax.ppermute only.
A program may use at most 128 MiB of HBM per device.

v0:
```python
import jax
import jax.numpy as jnp
from jax import lax
from jax.experimental import pallas as pl
from jax.experimental.pallas import tpu as pltpu
from jax.sharding import PartitionSpec as P


ITERS = 2


EPSILON = 1e-06


LANES = 128


def swap_bit(values, axis, bit):
    return lax.ppermute(values, axis, [(i, i ^ bit) for i in range(lax.axis_size(axis))])


def neighbours(before, after, axis):
    count = lax.axis_size(axis)
    odd = lax.axis_index(axis) % 2 == 1
    inner = [(i, i ^ 1) for i in range(count)]
    outer = [(i, i + 1) for i in range(1, count - 1, 2)]
    outer = outer + [(target, source) for source, target in outer]
    from_outer = lax.ppermute(jnp.where(odd, after, before), axis, outer)
    from_inner = lax.ppermute(jnp.where(odd, before, after), axis, inner)
    previous = jnp.where(odd, from_inner, from_outer)
    following = jnp.where(odd, from_outer, from_inner)
    return previous, following


def dft_tables(length):
    counter = jnp.arange(length, dtype=jnp.int32)
    phase_steps = counter[:, None] * counter[None, :] % length
    angle_grid = phase_steps.astype(jnp.float32) * (2.0 * jnp.pi / length)
    norm_factor = 1.0 / jnp.sqrt(jnp.float32(length))
    real_table = (jnp.cos(angle_grid) * norm_factor).astype(jnp.bfloat16)
    imag_table = (-jnp.sin(angle_grid) * norm_factor).astype(jnp.bfloat16)
    return (real_table, imag_table)


def split_tables(length):
    real_table, imag_table = dft_tables(length)
    half = length // 2
    lefts = []
    for first in (0, 1):
        re = real_table[first::2, :half]
        im = imag_table[first::2, :half]
        lefts.append(
            jnp.concatenate(
                [jnp.concatenate([re, -im], axis=1), jnp.concatenate([im, re], axis=1)], axis=0
            )
        )
    return jnp.stack(lefts + [lefts[0].T, lefts[1].T])


def even_odd(values):
    side = values.shape[-1]
    order = jnp.concatenate([jnp.arange(0, side, 2), jnp.arange(1, side, 2)])
    pick = (jnp.arange(side)[:, None] == order[None, :]).astype(jnp.float32)
    right = jnp.einsum(
        "brc,ck->brk", values, pick, precision=lax.Precision.HIGHEST,
        preferred_element_type=jnp.float32,
    )
    return jnp.einsum(
        "rk,brc->bkc", pick, right, precision=lax.Precision.HIGHEST,
        preferred_element_type=jnp.float32,
    )


def mm(left, right):
    return jnp.dot(left, right, preferred_element_type=jnp.float32)


def propagate_body(
    rows_ref, cols_ref, tile_ref, above_ref, below_ref, left_ref, right_ref, probe_ref, amp_ref,
    table_ref, grad_ref, rim_ref, probe_grad_ref, ext_f32, patch_ref, far_ref, acc_ref, scale_ref,
):
    modes = probe_ref.shape[0]
    side = probe_ref.shape[2]
    half = side // 2
    step = pl.program_id(0)
    tiles = ext_f32.shape[1]
    edge = half // LANES
    tile_rows = tile_ref.shape[1]

    @pl.when(step == 0)
    def _():
        for part in range(2):
            for tile in range(tiles):
                if tile < edge:
                    at = slice(tile * LANES, (tile + 1) * LANES)
                    ext_f32[part, tile] = left_ref[part, :, at].astype(jnp.float32)
                elif tile >= tiles - edge:
                    at = slice((tile - tiles + edge) * LANES, (tile - tiles + edge + 1) * LANES)
                    ext_f32[part, tile] = right_ref[part, :, at].astype(jnp.float32)
                else:
                    at = slice((tile - edge) * LANES, (tile - edge + 1) * LANES)
                    ext_f32[part, tile, :half] = above_ref[part, :, at].astype(jnp.float32)
                    ext_f32[part, tile, half : half + tile_rows] = tile_ref[
                        part, :, at
                    ].astype(jnp.float32)
                    ext_f32[part, tile, half + tile_rows :] = below_ref[part, :, at].astype(
                        jnp.float32
                    )
        acc_ref[...] = jnp.zeros(acc_ref.shape, jnp.float32)
        probe_grad_ref[...] = jnp.zeros(probe_grad_ref.shape, jnp.float32)
        power = jnp.zeros((side, side), jnp.float32)
        for mode in range(modes):
            for part in range(2):
                values = probe_ref[mode, part].astype(jnp.float32)
                power += values * values
        scale_ref[0] = 1.0 / (jnp.max(power) + EPSILON)

    row = rows_ref[step]
    col = cols_ref[step]
    tile0 = col // LANES
    lane0 = col % LANES
    width = side // LANES
    lane = lax.broadcasted_iota(jnp.int32, (side, LANES), 1)
    left_part = lane < LANES - lane0
    for part in range(2):
        rolled = [
            pltpu.roll(
                ext_f32[part, tile0 + j, pl.ds(row, side), :], (LANES - lane0) % LANES, 1
            )
            for j in range(width + 1)
        ]
        for j in range(width):
            patch_ref[part, :, j * LANES : (j + 1) * LANES] = jnp.where(
                left_part, rolled[j], rolled[j + 1]
            )

    table_le = table_ref[0]
    table_lo = table_ref[1]
    table_re = table_ref[2]
    table_ro = table_ref[3]
    power_e = jnp.zeros((side, half), jnp.float32)
    power_o = jnp.zeros((side, half), jnp.float32)
    for mode in range(modes):
        wave = []
        for rows in (slice(0, half), slice(half, side)):
            qr = probe_ref[mode, 0, rows, :].astype(jnp.float32)
            qi = probe_ref[mode, 1, rows, :].astype(jnp.float32)
            pr = patch_ref[0, rows, :]
            pi = patch_ref[1, rows, :]
            wave.append((qr * pr - qi * pi, qr * pi + qi * pr))
        (lo_re, lo_im), (hi_re, hi_im) = wave
        sums = jnp.concatenate(
            [(lo_re + hi_re).astype(jnp.bfloat16), (lo_im + hi_im).astype(jnp.bfloat16)], axis=0
        )
        diffs = jnp.concatenate(
            [(lo_re - hi_re).astype(jnp.bfloat16), (lo_im - hi_im).astype(jnp.bfloat16)], axis=0
        )
        evens, odds = [], []
        for half_field in (mm(table_le, sums), mm(table_lo, diffs)):
            re_lo, re_hi = half_field[:half, :half], half_field[:half, half:]
            im_lo, im_hi = half_field[half:, :half], half_field[half:, half:]
            evens.append(
                jnp.concatenate(
                    [(re_lo + re_hi).astype(jnp.bfloat16), (im_lo + im_hi).astype(jnp.bfloat16)],
                    axis=1,
                )
            )
            odds.append(
                jnp.concatenate(
                    [(re_lo - re_hi).astype(jnp.bfloat16), (im_lo - im_hi).astype(jnp.bfloat16)],
                    axis=1,
                )
            )
        far_e = mm(jnp.concatenate(evens, axis=0), table_re)
        far_o = mm(jnp.concatenate(odds, axis=0), table_ro)
        far_ref[mode, 0] = far_e
        far_ref[mode, 1] = far_o
        power_e += far_e[:, :half] * far_e[:, :half] + far_e[:, half:] * far_e[:, half:]
        power_o += far_o[:, :half] * far_o[:, :half] + far_o[:, half:] * far_o[:, half:]

    ratio_e = amp_ref[0, :, :half] * lax.rsqrt(jnp.maximum(power_e, 1.0)) - 1.0
    ratio_o = amp_ref[0, :, half:] * lax.rsqrt(jnp.maximum(power_o, 1.0)) - 1.0

    obj = [[None, None], [None, None]]
    for mode in range(modes):
        far_e = far_ref[mode, 0]
        far_o = far_ref[mode, 1]
        diff_e = jnp.concatenate(
            [
                (far_e[:, :half] * ratio_e).astype(jnp.bfloat16),
                (far_e[:, half:] * ratio_e).astype(jnp.bfloat16),
            ],
            axis=1,
        )
        diff_o = jnp.concatenate(
            [
                (far_o[:, :half] * ratio_o).astype(jnp.bfloat16),
                (far_o[:, half:] * ratio_o).astype(jnp.bfloat16),
            ],
            axis=1,
        )
        u = mm(diff_e, table_le)
        v = mm(diff_o, table_lo)
        total = (u + v).astype(jnp.bfloat16)
        gap = (u - v).astype(jnp.bfloat16)
        backs = []
        for rows in (slice(0, half), slice(half, side)):
            backs.append(
                jnp.concatenate(
                    [
                        jnp.concatenate([total[rows, :half], gap[rows, :half]], axis=1),
                        jnp.concatenate([total[rows, half:], gap[rows, half:]], axis=1),
                    ],
                    axis=0,
                )
            )
        p = mm(table_re, backs[0])
        q = mm(table_ro, backs[1])
        for index, sign in ((0, 1), (1, -1)):
            rows = slice(index * half, (index + 1) * half)
            if sign > 0:
                chi_re = p[:half] + q[:half]
                chi_im = p[half:] + q[half:]
            else:
                chi_re = p[:half] - q[:half]
                chi_im = p[half:] - q[half:]
            qr = probe_ref[mode, 0, rows, :].astype(jnp.float32)
            qi = probe_ref[mode, 1, rows, :].astype(jnp.float32)
            pr = patch_ref[0, rows, :]
            pi = patch_ref[1, rows, :]
            term_re = qr * chi_re + qi * chi_im
            term_im = qr * chi_im - qi * chi_re
            if mode == 0:
                obj[index] = [term_re, term_im]
            else:
                obj[index][0] += term_re
                obj[index][1] += term_im
            probe_grad_ref[mode, 0, rows, :] += pr * chi_re + pi * chi_im
            probe_grad_ref[mode, 1, rows, :] += pr * chi_im - pi * chi_re

    lane_h = lax.broadcasted_iota(jnp.int32, (half, LANES), 1)
    right_part = lane_h >= lane0
    scale = scale_ref[0]
    for index in range(2):
        for part in range(2):
            values = obj[index][part] * scale
            rolled = [
                pltpu.roll(values[:, j * LANES : (j + 1) * LANES], lane0, 1) for j in range(width)
            ]
            where = pl.ds(row + index * half, half)
            for j in range(width + 1):
                above = rolled[j] if j < width else jnp.zeros_like(rolled[0])
                below = rolled[j - 1] if j > 0 else jnp.zeros_like(rolled[0])
                acc_ref[part, tile0 + j, where, :] += jnp.where(right_part, above, below)

    @pl.when(step == pl.num_programs(0) - 1)
    def _():
        for part in range(2):
            for tile in range(tiles):
                values = acc_ref[part, tile]
                if tile < edge:
                    at = slice(tile * LANES, (tile + 1) * LANES)
                    rim_ref[0, part, :, at] = values.astype(rim_ref.dtype)
                elif tile >= tiles - edge:
                    at = slice((tile - tiles + edge) * LANES, (tile - tiles + edge + 1) * LANES)
                    rim_ref[1, part, :, at] = values.astype(rim_ref.dtype)
                else:
                    at = slice((tile - edge) * LANES, (tile - edge + 1) * LANES)
                    grad_ref[part, :, at] = values


def propagate(rows, cols, pieces, probe_low, amplitude, tables):
    count = rows.shape[0]
    modes, _, side, _ = probe_low.shape
    half = side // 2
    tile_rows, tile_cols = pieces[0].shape[1:]
    ext_rows = tile_rows + side
    tiles = (tile_cols + side) // LANES

    def whole(*shape):
        return pl.BlockSpec(
            shape, lambda i, *_: (0,) * len(shape), pipeline_mode=pl.Buffered(1)
        )

    return pl.pallas_call(
        propagate_body,
        out_shape=(
            jax.ShapeDtypeStruct((2, ext_rows, tile_cols), jnp.float32),
            jax.ShapeDtypeStruct((2, 2, ext_rows, half), jnp.bfloat16),
            jax.ShapeDtypeStruct((modes, 2, side, side), jnp.float32),
        ),
        grid_spec=pltpu.PrefetchScalarGridSpec(
            num_scalar_prefetch=2,
            grid=(count,),
            in_specs=[whole(*piece.shape) for piece in pieces]
            + [
                whole(*probe_low.shape),
                pl.BlockSpec((1, side, side), lambda i, *_: (i, 0, 0)),
                whole(*tables.shape),
            ],
            out_specs=(
                whole(2, ext_rows, tile_cols),
                whole(2, 2, ext_rows, half),
                whole(modes, 2, side, side),
            ),
            scratch_shapes=[
                pltpu.VMEM((2, tiles, ext_rows, LANES), jnp.float32),
                pltpu.VMEM((2, side, side), jnp.float32),
                pltpu.VMEM((modes, 2, side, side), jnp.float32),
                pltpu.VMEM((2, tiles, ext_rows, LANES), jnp.float32),
                pltpu.SMEM((1,), jnp.float32),
            ],
        ),
        name="propagate",
    )(rows, cols, *pieces, probe_low, amplitude, tables)


def exchange_steps():
    steps = []
    bit = 1
    while bit < lax.axis_size("obj"):
        steps.append(("obj", bit, jnp.bfloat16))
        bit *= 2
    bit = 2
    while bit < lax.axis_size("dp"):
        steps.append(("dp", bit, jnp.bfloat16))
        bit *= 2
    if lax.axis_size("dp") > 1:
        steps.append(("dp", 1, jnp.float32))
    return steps


def halve(values, axis, bit):
    rows = values.shape[0] // 2
    upper = (lax.axis_index(axis) // bit) % 2
    keep = lax.dynamic_slice_in_dim(values, upper * rows, rows, 0)
    send = lax.dynamic_slice_in_dim(values, (1 - upper) * rows, rows, 0)
    return keep, send


def sum_to_share(values):
    for axis, bit, kind in exchange_steps():
        keep, send = halve(values, axis, bit)
        got = swap_bit(send.astype(kind), axis, bit)
        values = keep + got.astype(values.dtype)
    return values


def own_share(values):
    for axis, bit, _ in exchange_steps():
        values = halve(values, axis, bit)[0]
    return values


def join_shares(values):
    steps = exchange_steps()
    for index in range(len(steps) - 1, -1, -1):
        axis, bit, _ = steps[index]
        got = swap_bit(values, axis, bit)
        lower = (lax.axis_index(axis) // bit) % 2 == 0
        values = jnp.concatenate(
            [jnp.where(lower, values, got), jnp.where(lower, got, values)], axis=0
        )
    return values


def fold_rims(grad, rims, half, tile_rows, tile_cols):
    left, right = rims[0], rims[1]
    from_left, from_right = neighbours(left, right, "obj")
    wide = jnp.zeros((2, grad.shape[1], tile_cols - 2 * half), from_left.dtype)
    total = grad + jnp.concatenate([from_left, wide, from_right], axis=2).astype(jnp.float32)
    low = total.astype(jnp.bfloat16)
    from_above, from_below = neighbours(low[:, :half], low[:, -half:], "dp")
    tall = jnp.zeros((2, tile_rows - 2 * half, tile_cols), from_above.dtype)
    inner = total[:, half : half + tile_rows]
    return inner + jnp.concatenate([from_above, tall, from_below], axis=1).astype(jnp.float32)


def gather_rims(tile, half):
    above, below = neighbours(tile[:, :half], tile[:, -half:], "dp")
    first = jnp.concatenate([above[:, :, :half], tile[:, :, :half], below[:, :, :half]], axis=1)
    last = jnp.concatenate([above[:, :, -half:], tile[:, :, -half:], below[:, :, -half:]], axis=1)
    left, right = neighbours(first, last, "obj")
    return tile, above, below, left, right


def shards(object_field, probe_modes, amplitude, offsets):
    side = probe_modes.shape[2]
    half = side // 2
    tile_rows = object_field.shape[1]
    tile_cols = object_field.shape[2]
    count = offsets.shape[0]
    devices = lax.axis_size("dp") * lax.axis_size("obj")
    total_positions = count * devices
    tables = split_tables(side)
    amplitude = even_odd(amplitude)
    top_rows = offsets[:, 0] - lax.axis_index("dp") * tile_rows + half
    left_cols = offsets[:, 1] - lax.axis_index("obj") * tile_cols + half
    current = object_field
    probe_low = probe_modes.astype(jnp.bfloat16)
    probe_share = own_share(probe_modes.reshape(-1, side))
    pieces = gather_rims(current.astype(jnp.bfloat16), half)
    for turn in range(ITERS):
        grad, rims, probe_terms = propagate(
            top_rows, left_cols, pieces, probe_low, amplitude, tables
        )
        current = current + fold_rims(grad, rims, half, tile_rows, tile_cols)
        summed = sum_to_share(probe_terms.reshape(-1, side))
        probe_share = probe_share + summed / total_positions
        if turn + 1 < ITERS:
            pieces = gather_rims(current.astype(jnp.bfloat16), half)
            probe_low = join_shares(probe_share.astype(jnp.bfloat16)).reshape(
                probe_modes.shape
            )
        else:
            probe = join_shares(probe_share).reshape(probe_modes.shape)
    return (current, probe)


def solution(mesh):
    in_specs = (P(None, "dp", "obj"), P(), P(("dp", "obj"), None, None), P(("dp", "obj"), None))
    out_specs = (P(None, "dp", "obj"), P())
    return jax.shard_map(shards, mesh=mesh, in_specs=in_specs, out_specs=out_specs, check_vma=False)
```

profile of v0, /device:TPU:8, one launch (start us, length us, event | category | flops | bytes accessed | tf_op | source)
XLA Modules:
  0.0 239.9 jit_solution(17170942447655748176)
XLA Ops:
  2.9 3.3 %collective-permute-start.1 = (bf16[2,128,512]{2,1,0:T(8,128)(2,1)}, bf16[2,128,512]{2,1,0:T(8,128)(2,1)S(1)}, u32[]{:S(2)}, u32[]{:S(2)}) collective-permute-start(bf16[2,128,512]{2,1,0:T(8,128)(2,1)} %get-tuple-element.64), channel_id=1, source_target_pairs={{4,8},{12,16},{20,24},{8,4},{16,12},{24,20},{5,9},{13,17},{21,25},... | collective-permute-start | bytes 786440 | tf_op jit(solution)/shard_map/ppermute | solution.py:28
  15.6 2.2 fusion.2.amp_ref
  20.7 2.9 %collective-permute-start.2 = (bf16[2,512,128]{2,1,0:T(8,128)(2,1)S(1)}, bf16[2,512,128]{2,1,0:T(8,128)(2,1)}, u32[]{:S(2)}, u32[]{:S(2)}) collective-permute-start(bf16[2,512,128]{2,1,0:T(8,128)(2,1)S(1)} %get-tuple-element.59), channel_id=1, source_target_pairs={{0,1},{1,0},{2,3},{3,2},{4,5},{5,4},{6,7},{7,6},{8,9},{9,8},{10,11... | collective-permute-start | bytes 786440 | tf_op jit(solution)/shard_map/ppermute | solution.py:29
  24.5 2.7 %convert_element_type.115.probe_ref = bf16[4,2,256,256]{3,2,1,0:T(8,128)(2,1)} convert(f32[4,2,256,256]{3,2,1,0:T(8,128)} %param.5) | non-fusion elementwise | flops 524288 | bytes 3145728 | tf_op jit(solution)/shard_map/convert_element_type | solution.py:400
  27.7 1.8 broadcast_select_fusion.16
  29.5 26.3 %propagate.2 = (f32[2,512,512]{2,1,0:T(8,128)}, bf16[2,2,512,128]{3,2,1,0:T(8,128)(2,1)}, f32[4,2,256,256]{3,2,1,0:T(8,128)}) custom-call(s32[6]{0:T(128)} %get-tuple-element.89.rows_ref, s32[6]{0:T(128)} %get-tuple-element.88.cols_ref, bf16[2,256,512]{2,1,0:T(8,128)(2,1)} %copy-done.4, bf16[2,128,512]{2,1,0:T(8,128)(2,1)} %copy-done.13, ...), custom_call_target="tpu_custom_call" | custom-call | tf_op jit(solution)/shard_map/propagate/pallas_call | solution.py:285
  62.3 7.6 %collective-permute-start.13 = (bf16[512,256]{1,0:T(8,128)(2,1)S(1)}, bf16[512,256]{1,0:T(8,128)(2,1)S(1)}, u32[]{:S(2)}, u32[]{:S(2)}) collective-permute-start(bf16[512,256]{1,0:T(8,128)(2,1)S(1)} %dynamic-slice_convert_fusion.3), channel_id=1, source_target_pairs={{0,2},{1,3},{2,0},{3,1},{4,6},{5,7},{6,4},{7,5},{8,10},{9,11},{10,... | collective-permute-start | bytes 786440 | tf_op jit(solution)/shard_map/ppermute | solution.py:19
  70.4 6.5 %collective-permute-done.13 = bf16[512,256]{1,0:T(8,128)(2,1)S(1)} collective-permute-done((bf16[512,256]{1,0:T(8,128)(2,1)S(1)}, bf16[512,256]{1,0:T(8,128)(2,1)S(1)}, u32[]{:S(2)}, u32[]{:S(2)}) %collective-permute-start.13) | collective-permute-done | bytes 262176 | tf_op jit(solution)/shard_map/ppermute | solution.py:19
  77.1 2.0 collective-permute-start.6
  79.1 3.4 %collective-permute-start.7 = (bf16[2,128,512]{2,1,0:T(8,128)(2,1)S(1)}, bf16[2,128,512]{2,1,0:T(8,128)(2,1)S(1)}, u32[]{:S(2)}, u32[]{:S(2)}) collective-permute-start(bf16[2,128,512]{2,1,0:T(8,128)(2,1)S(1)} %get-tuple-element.29), channel_id=1, source_target_pairs={{4,8},{12,16},{20,24},{8,4},{16,12},{24,20},{5,9},{13,17},{21,25},... | collective-permute-start | bytes 786440 | tf_op jit(solution)/shard_map/ppermute | solution.py:28
  82.6 2.6 %collective-permute-start.15 = (bf16[128,256]{1,0:T(8,128)(2,1)S(1)}, bf16[128,256]{1,0:T(8,128)(2,1)S(1)}, u32[]{:S(2)}, u32[]{:S(2)}) collective-permute-start(bf16[128,256]{1,0:T(8,128)(2,1)S(1)} %dynamic-slice_convert_fusion.7), channel_id=1, source_target_pairs={{0,16},{4,20},{8,24},{12,28},{16,0},{20,4},{24,8},{28,12},{1,17},{... | collective-permute-start | bytes 196616 | tf_op jit(solution)/shard_map/ppermute | solution.py:19
  85.3 5.6 %collective-permute-done.6 = bf16[2,128,512]{2,1,0:T(8,128)(2,1)S(1)} collective-permute-done((bf16[2,128,512]{2,1,0:T(8,128)(2,1)S(1)}, bf16[2,128,512]{2,1,0:T(8,128)(2,1)S(1)}, u32[]{:S(2)}, u32[]{:S(2)}) %collective-permute-start.6) | collective-permute-done | bytes 262176 | tf_op jit(solution)/shard_map/ppermute | solution.py:29
  93.0 3.4 %collective-permute-done.16 = f32[64,256]{1,0:T(8,128)S(1)} collective-permute-done((f32[64,256]{1,0:T(8,128)S(1)}, f32[64,256]{1,0:T(8,128)S(1)}, u32[]{:S(2)}, u32[]{:S(2)}) %collective-permute-start.16) | collective-permute-done | bytes 65568 | tf_op jit(solution)/shard_map/ppermute | solution.py:19
  98.0 3.3 %collective-permute-done.17 = bf16[64,256]{1,0:T(8,128)(2,1)S(1)} collective-permute-done((bf16[64,256]{1,0:T(8,128)(2,1)S(1)}, bf16[64,256]{1,0:T(8,128)(2,1)S(1)}, u32[]{:S(2)}, u32[]{:S(2)}) %collective-permute-start.17) | collective-permute-done | bytes 32800 | tf_op jit(solution)/shard_map/ppermute | solution.py:19
  103.1 3.2 %collective-permute-start.9 = (bf16[2,128,512]{2,1,0:T(8,128)(2,1)S(1)}, bf16[2,128,512]{2,1,0:T(8,128)(2,1)S(1)}, u32[]{:S(2)}, u32[]{:S(2)}) collective-permute-start(bf16[2,128,512]{2,1,0:T(8,128)(2,1)S(1)} %get-tuple-element.48), channel_id=1, source_target_pairs={{4,8},{12,16},{20,24},{8,4},{16,12},{24,20},{5,9},{13,17},{21,25},... | collective-permute-start | bytes 786440 | tf_op jit(solution)/shard_map/ppermute | solution.py:28
  108.7 3.7 %collective-permute-done.9 = bf16[2,128,512]{2,1,0:T(8,128)(2,1)S(1)} collective-permute-done((bf16[2,128,512]{2,1,0:T(8,128)(2,1)S(1)}, bf16[2,128,512]{2,1,0:T(8,128)(2,1)S(1)}, u32[]{:S(2)}, u32[]{:S(2)}) %collective-permute-start.9) | collective-permute-done | bytes 262176 | tf_op jit(solution)/shard_map/ppermute | solution.py:28
  112.4 3.1 %collective-permute-done.8 = bf16[2,128,512]{2,1,0:T(8,128)(2,1)S(1)} collective-permute-done((bf16[2,128,512]{2,1,0:T(8,128)(2,1)S(1)}, bf16[2,128,512]{2,1,0:T(8,128)(2,1)S(1)}, u32[]{:S(2)}, u32[]{:S(2)}) %collective-permute-start.8) | collective-permute-done | bytes 262176 | tf_op jit(solution)/shard_map/ppermute | solution.py:29
  116.2 5.9 %collective-permute-done.20 = bf16[512,256]{1,0:T(8,128)(2,1)S(1)} collective-permute-done((bf16[512,256]{1,0:T(8,128)(2,1)S(1)}, bf16[512,256]{1,0:T(8,128)(2,1)S(1)}, u32[]{:S(2)}, u32[]{:S(2)}) %collective-permute-start.20) | collective-permute-done | bytes 262176 | tf_op jit(solution)/shard_map/ppermute | solution.py:19
  128.1 1.9 broadcast_select_fusion.10
  132.3 26.4 %propagate.3 = (f32[2,512,512]{2,1,0:T(8,128)}, bf16[2,2,512,128]{3,2,1,0:T(8,128)(2,1)}, f32[4,2,256,256]{3,2,1,0:T(8,128)}) custom-call(s32[6]{0:T(128)} %get-tuple-element.89.rows_ref, s32[6]{0:T(128)} %get-tuple-element.88.cols_ref, bf16[2,256,512]{2,1,0:T(8,128)(2,1)} %copy-done.5, bf16[2,128,512]{2,1,0:T(8,128)(2,1)} %copy-done.11, ...), custom_call_target="tpu_custom_call" | custom-call | tf_op jit(solution)/shard_map/propagate/pallas_call | solution.py:285
  160.0 4.3 %collective-permute-start.26 = (bf16[1024,256]{1,0:T(8,128)(2,1)S(1)}, bf16[1024,256]{1,0:T(8,128)(2,1)S(1)}, u32[]{:S(2)}, u32[]{:S(2)}) collective-permute-start(bf16[1024,256]{1,0:T(8,128)(2,1)S(1)} %dynamic-slice_convert_fusion), channel_id=1, source_target_pairs={{0,1},{1,0},{2,3},{3,2},{4,5},{5,4},{6,7},{7,6},{8,9},{9,8},{10,11... | collective-permute-start | bytes 1572872 | tf_op jit(solution)/shard_map/ppermute | solution.py:19
  167.6 8.3 %collective-permute-done.27 = bf16[512,256]{1,0:T(8,128)(2,1)S(1)} collective-permute-done((bf16[512,256]{1,0:T(8,128)(2,1)S(1)}, bf16[512,256]{1,0:T(8,128)(2,1)S(1)}, u32[]{:S(2)}, u32[]{:S(2)}) %collective-permute-start.27) | collective-permute-done | bytes 262176 | tf_op jit(solution)/shard_map/ppermute | solution.py:19
  176.1 5.0 %collective-permute-done.28 = bf16[256,256]{1,0:T(8,128)(2,1)S(1)} collective-permute-done((bf16[256,256]{1,0:T(8,128)(2,1)S(1)}, bf16[256,256]{1,0:T(8,128)(2,1)S(1)}, u32[]{:S(2)}, u32[]{:S(2)}) %collective-permute-start.28) | collective-permute-done | bytes 131104 | tf_op jit(solution)/shard_map/ppermute | solution.py:19
  182.4 3.9 %collective-permute-done.29 = bf16[128,256]{1,0:T(8,128)(2,1)S(1)} collective-permute-done((bf16[128,256]{1,0:T(8,128)(2,1)S(1)}, bf16[128,256]{1,0:T(8,128)(2,1)S(1)}, u32[]{:S(2)}, u32[]{:S(2)}) %collective-permute-start.29) | collective-permute-done | bytes 65568 | tf_op jit(solution)/shard_map/ppermute | solution.py:19
  187.4 3.5 %collective-permute-done.30 = f32[64,256]{1,0:T(8,128)S(1)} collective-permute-done((f32[64,256]{1,0:T(8,128)S(1)}, f32[64,256]{1,0:T(8,128)S(1)}, u32[]{:S(2)}, u32[]{:S(2)}) %collective-permute-start.30) | collective-permute-done | bytes 65568 | tf_op jit(solution)/shard_map/ppermute | solution.py:19
  191.9 3.3 %collective-permute-done.31 = f32[64,256]{1,0:T(8,128)S(1)} collective-permute-done((f32[64,256]{1,0:T(8,128)S(1)}, f32[64,256]{1,0:T(8,128)S(1)}, u32[]{:S(2)}, u32[]{:S(2)}) %collective-permute-start.31) | collective-permute-done | bytes 65568 | tf_op jit(solution)/shard_map/ppermute | solution.py:19
  195.3 1.9 collective-permute-start.32
  197.2 5.4 %collective-permute-done.32 = f32[128,256]{1,0:T(8,128)S(1)} collective-permute-done((f32[128,256]{1,0:T(8,128)S(1)}, f32[128,256]{1,0:T(8,128)S(1)}, u32[]{:S(2)}, u32[]{:S(2)}) %collective-permute-start.32) | collective-permute-done | bytes 131104 | tf_op jit(solution)/shard_map/ppermute | solution.py:19
  203.7 5.4 %collective-permute-done.33 = f32[256,256]{1,0:T(8,128)S(1)} collective-permute-done((f32[256,256]{1,0:T(8,128)S(1)}, f32[256,256]{1,0:T(8,128)S(1)}, u32[]{:S(2)}, u32[]{:S(2)}) %collective-permute-start.33) | collective-permute-done | bytes 262176 | tf_op jit(solution)/shard_map/ppermute | solution.py:19
  209.9 12.2 %collective-permute-done.34 = f32[512,256]{1,0:T(8,128)S(1)} collective-permute-done((f32[512,256]{1,0:T(8,128)S(1)}, f32[512,256]{1,0:T(8,128)S(1)}, u32[]{:S(2)}, u32[]{:S(2)}) %collective-permute-start.34) | collective-permute-done | bytes 524320 | tf_op jit(solution)/shard_map/ppermute | solution.py:19
  223.5 4.3 %collective-permute-start.25 = (bf16[2,128,512]{2,1,0:T(8,128)(2,1)S(1)}, bf16[2,128,512]{2,1,0:T(8,128)(2,1)S(1)}, u32[]{:S(2)}, u32[]{:S(2)}) collective-permute-start(bf16[2,128,512]{2,1,0:T(8,128)(2,1)S(1)} %get-tuple-element.25), channel_id=1, source_target_pairs={{4,8},{12,16},{20,24},{8,4},{16,12},{24,20},{5,9},{13,17},{21,25},... | collective-permute-start | bytes 786440 | tf_op jit(solution)/shard_map/ppermute | solution.py:28
  227.8 9.0 %collective-permute-done.24 = bf16[2,128,512]{2,1,0:T(8,128)(2,1)S(1)} collective-permute-done((bf16[2,128,512]{2,1,0:T(8,128)(2,1)S(1)}, bf16[2,128,512]{2,1,0:T(8,128)(2,1)S(1)}, u32[]{:S(2)}, u32[]{:S(2)}) %collective-permute-start.24) | collective-permute-done | bytes 262176 | tf_op jit(solution)/shard_map/ppermute | solution.py:29
  (160 shorter events, 53.9 us)
Async XLA Ops:
  2.9 15.2 %collective-permute-start.1 = (bf16[2,128,512]{2,1,0:T(8,128)(2,1)}, bf16[2,128,512]{2,1,0:T(8,128)(2,1)S(1)}, u32[]{:S(2)}, u32[]{:S(2)}) collective-permute-start(bf16[2,128,512]{2,1,0:T(8,128)(2,1)} %get-tuple-element.64), channel_id=1, source_target_pairs={{4,8},{12,16},{20,24},{8,4},{16,12},{24,20},{5,9},{13,17},{21,25},... | collective-permute-start | bytes 786440 | tf_op jit(solution)/shard_map/ppermute | solution.py:28
  6.2 13.4 %collective-permute-start = (bf16[2,128,512]{2,1,0:T(8,128)(2,1)S(1)}, bf16[2,128,512]{2,1,0:T(8,128)(2,1)S(1)}, u32[]{:S(2)}, u32[]{:S(2)}) collective-permute-start(bf16[2,128,512]{2,1,0:T(8,128)(2,1)S(1)} %get-tuple-element.65), channel_id=1, source_target_pairs={{0,4},{4,0},{8,12},{12,8},{16,20},{20,16},{24,28},{28,24},{1,5},{5... | collective-permute-start | bytes 786440 | tf_op jit(solution)/shard_map/ppermute | solution.py:29
  19.8 7.9 %collective-permute-start.3 = (bf16[2,512,128]{2,1,0:T(8,128)(2,1)S(1)}, bf16[2,512,128]{2,1,0:T(8,128)(2,1)S(1)}, u32[]{:S(2)}, u32[]{:S(2)}) collective-permute-start(bf16[2,512,128]{2,1,0:T(8,128)(2,1)S(1)} %get-tuple-element.58), channel_id=1, source_target_pairs={{1,2},{2,1},{5,6},{6,5},{9,10},{10,9},{13,14},{14,13},{17,18},{18,... | collective-permute-start | bytes 786440 | tf_op jit(solution)/shard_map/ppermute | solution.py:28
  20.7 7.0 %collective-permute-start.2 = (bf16[2,512,128]{2,1,0:T(8,128)(2,1)S(1)}, bf16[2,512,128]{2,1,0:T(8,128)(2,1)}, u32[]{:S(2)}, u32[]{:S(2)}) collective-permute-start(bf16[2,512,128]{2,1,0:T(8,128)(2,1)S(1)} %get-tuple-element.59), channel_id=1, source_target_pairs={{0,1},{1,0},{2,3},{3,2},{4,5},{5,4},{6,7},{7,6},{8,9},{9,8},{10,11... | collective-permute-start | bytes 786440 | tf_op jit(solution)/shard_map/ppermute | solution.py:29
  57.1 3.8 %collective-permute-start.12 = (bf16[1024,256]{1,0:T(8,128)(2,1)S(1)}, bf16[1024,256]{1,0:T(8,128)(2,1)S(1)}, u32[]{:S(2)}, u32[]{:S(2)}) collective-permute-start(bf16[1024,256]{1,0:T(8,128)(2,1)S(1)} %dynamic-slice_convert_fusion.1), channel_id=1, source_target_pairs={{0,1},{1,0},{2,3},{3,2},{4,5},{5,4},{6,7},{7,6},{8,9},{9,8},{10,11... | collective-permute-start | bytes 1572872 | tf_op jit(solution)/shard_map/ppermute | solution.py:19
  62.3 14.6 %collective-permute-start.13 = (bf16[512,256]{1,0:T(8,128)(2,1)S(1)}, bf16[512,256]{1,0:T(8,128)(2,1)S(1)}, u32[]{:S(2)}, u32[]{:S(2)}) collective-permute-start(bf16[512,256]{1,0:T(8,128)(2,1)S(1)} %dynamic-slice_convert_fusion.3), channel_id=1, source_target_pairs={{0,2},{1,3},{2,0},{3,1},{4,6},{5,7},{6,4},{7,5},{8,10},{9,11},{10,... | collective-permute-start | bytes 786440 | tf_op jit(solution)/shard_map/ppermute | solution.py:19
  77.0 5.6 %collective-permute-start.14 = (bf16[256,256]{1,0:T(8,128)(2,1)S(1)}, bf16[256,256]{1,0:T(8,128)(2,1)S(1)}, u32[]{:S(2)}, u32[]{:S(2)}) collective-permute-start(bf16[256,256]{1,0:T(8,128)(2,1)S(1)} %dynamic-slice_convert_fusion.5), channel_id=1, source_target_pairs={{0,8},{4,12},{8,0},{12,4},{16,24},{20,28},{24,16},{28,20},{1,9},{5... | collective-permute-start | bytes 393224 | tf_op jit(solution)/shard_map/ppermute | solution.py:19
  77.1 13.8 %collective-permute-start.6 = (bf16[2,128,512]{2,1,0:T(8,128)(2,1)S(1)}, bf16[2,128,512]{2,1,0:T(8,128)(2,1)S(1)}, u32[]{:S(2)}, u32[]{:S(2)}) collective-permute-start(bf16[2,128,512]{2,1,0:T(8,128)(2,1)S(1)} %get-tuple-element.28), channel_id=1, source_target_pairs={{0,4},{4,0},{8,12},{12,8},{16,20},{20,16},{24,28},{28,24},{1,5},{5... | collective-permute-start | bytes 786440 | tf_op jit(solution)/shard_map/ppermute | solution.py:29
  79.1 11.8 %collective-permute-start.7 = (bf16[2,128,512]{2,1,0:T(8,128)(2,1)S(1)}, bf16[2,128,512]{2,1,0:T(8,128)(2,1)S(1)}, u32[]{:S(2)}, u32[]{:S(2)}) collective-permute-start(bf16[2,128,512]{2,1,0:T(8,128)(2,1)S(1)} %get-tuple-element.29), channel_id=1, source_target_pairs={{4,8},{12,16},{20,24},{8,4},{16,12},{24,20},{5,9},{13,17},{21,25},... | collective-permute-start | bytes 786440 | tf_op jit(solution)/shard_map/ppermute | solution.py:28
  82.6 9.5 %collective-permute-start.15 = (bf16[128,256]{1,0:T(8,128)(2,1)S(1)}, bf16[128,256]{1,0:T(8,128)(2,1)S(1)}, u32[]{:S(2)}, u32[]{:S(2)}) collective-permute-start(bf16[128,256]{1,0:T(8,128)(2,1)S(1)} %dynamic-slice_convert_fusion.7), channel_id=1, source_target_pairs={{0,16},{4,20},{8,24},{12,28},{16,0},{20,4},{24,8},{28,12},{1,17},{... | collective-permute-start | bytes 196616 | tf_op jit(solution)/shard_map/ppermute | solution.py:19
  92.1 4.3 %collective-permute-start.16 = (f32[64,256]{1,0:T(8,128)S(1)}, f32[64,256]{1,0:T(8,128)S(1)}, u32[]{:S(2)}, u32[]{:S(2)}) collective-permute-start(f32[64,256]{1,0:T(8,128)S(1)} %constant_dynamic-slice_fusion.1), channel_id=1, source_target_pairs={{0,4},{4,0},{8,12},{12,8},{16,20},{20,16},{24,28},{28,24},{1,5},{5... | collective-permute-start | bytes 196616 | tf_op jit(solution)/shard_map/ppermute | solution.py:19
  97.4 4.0 %collective-permute-start.17 = (bf16[64,256]{1,0:T(8,128)(2,1)S(1)}, bf16[64,256]{1,0:T(8,128)(2,1)S(1)}, u32[]{:S(2)}, u32[]{:S(2)}) collective-permute-start(bf16[64,256]{1,0:T(8,128)(2,1)S(1)} %get-tuple-element.16), channel_id=1, source_target_pairs={{0,4},{4,0},{8,12},{12,8},{16,20},{20,16},{24,28},{28,24},{1,5},{5... | collective-permute-start | bytes 98312 | tf_op jit(solution)/shard_map/ppermute | solution.py:19
  101.4 5.9 %collective-permute-start.18 = (bf16[128,256]{1,0:T(8,128)(2,1)S(1)}, bf16[128,256]{1,0:T(8,128)(2,1)S(1)}, u32[]{:S(2)}, u32[]{:S(2)}) collective-permute-start(bf16[128,256]{1,0:T(8,128)(2,1)S(1)} %pad_maximum_fusion.14), channel_id=1, source_target_pairs={{0,16},{4,20},{8,24},{12,28},{16,0},{20,4},{24,8},{28,12},{1,17},{... | collective-permute-start | bytes 196616 | tf_op jit(solution)/shard_map/ppermute | solution.py:19
  103.1 9.3 %collective-permute-start.9 = (bf16[2,128,512]{2,1,0:T(8,128)(2,1)S(1)}, bf16[2,128,512]{2,1,0:T(8,128)(2,1)S(1)}, u32[]{:S(2)}, u32[]{:S(2)}) collective-permute-start(bf16[2,128,512]{2,1,0:T(8,128)(2,1)S(1)} %get-tuple-element.48), channel_id=1, source_target_pairs={{4,8},{12,16},{20,24},{8,4},{16,12},{24,20},{5,9},{13,17},{21,25},... | collective-permute-start | bytes 786440 | tf_op jit(solution)/shard_map/ppermute | solution.py:28
  106.3 9.2 %collective-permute-start.8 = (bf16[2,128,512]{2,1,0:T(8,128)(2,1)S(1)}, bf16[2,128,512]{2,1,0:T(8,128)(2,1)S(1)}, u32[]{:S(2)}, u32[]{:S(2)}) collective-permute-start(bf16[2,128,512]{2,1,0:T(8,128)(2,1)S(1)} %get-tuple-element.49), channel_id=1, source_target_pairs={{0,4},{4,0},{8,12},{12,8},{16,20},{20,16},{24,28},{28,24},{1,5},{5... | collective-permute-start | bytes 786440 | tf_op jit(solution)/shard_map/ppermute | solution.py:29
  107.3 8.2 %collective-permute-start.19 = (bf16[256,256]{1,0:T(8,128)(2,1)S(1)}, bf16[256,256]{1,0:T(8,128)(2,1)S(1)}, u32[]{:S(2)}, u32[]{:S(2)}) collective-permute-start(bf16[256,256]{1,0:T(8,128)(2,1)S(1)} %pad_maximum_fusion.12), channel_id=1, source_target_pairs={{0,8},{4,12},{8,0},{12,4},{16,24},{20,28},{24,16},{28,20},{1,9},{5... | collective-permute-start | bytes 393224 | tf_op jit(solution)/shard_map/ppermute | solution.py:19
  115.7 6.4 %collective-permute-start.20 = (bf16[512,256]{1,0:T(8,128)(2,1)S(1)}, bf16[512,256]{1,0:T(8,128)(2,1)S(1)}, u32[]{:S(2)}, u32[]{:S(2)}) collective-permute-start(bf16[512,256]{1,0:T(8,128)(2,1)S(1)} %pad_maximum_fusion.10), channel_id=1, source_target_pairs={{0,2},{1,3},{2,0},{3,1},{4,6},{5,7},{6,4},{7,5},{8,10},{9,11},{10,... | collective-permute-start | bytes 786440 | tf_op jit(solution)/shard_map/ppermute | solution.py:19
  123.0 7.0 %collective-permute-start.21 = (bf16[1024,256]{1,0:T(8,128)(2,1)}, bf16[1024,256]{1,0:T(8,128)(2,1)}, u32[]{:S(2)}, u32[]{:S(2)}) collective-permute-start(bf16[1024,256]{1,0:T(8,128)(2,1)} %pad_maximum_fusion.4), channel_id=1, source_target_pairs={{0,1},{1,0},{2,3},{3,2},{4,5},{5,4},{6,7},{7,6},{8,9},{9,8},{10,11... | collective-permute-start | bytes 1572872 | tf_op jit(solution)/shard_map/ppermute | solution.py:19
  160.0 5.9 %collective-permute-start.26 = (bf16[1024,256]{1,0:T(8,128)(2,1)S(1)}, bf16[1024,256]{1,0:T(8,128)(2,1)S(1)}, u32[]{:S(2)}, u32[]{:S(2)}) collective-permute-start(bf16[1024,256]{1,0:T(8,128)(2,1)S(1)} %dynamic-slice_convert_fusion), channel_id=1, source_target_pairs={{0,1},{1,0},{2,3},{3,2},{4,5},{5,4},{6,7},{7,6},{8,9},{9,8},{10,11... | collective-permute-start | bytes 1572872 | tf_op jit(solution)/shard_map/ppermute | solution.py:19
  167.2 8.7 %collective-permute-start.27 = (bf16[512,256]{1,0:T(8,128)(2,1)S(1)}, bf16[512,256]{1,0:T(8,128)(2,1)S(1)}, u32[]{:S(2)}, u32[]{:S(2)}) collective-permute-start(bf16[512,256]{1,0:T(8,128)(2,1)S(1)} %dynamic-slice_convert_fusion.2), channel_id=1, source_target_pairs={{0,2},{1,3},{2,0},{3,1},{4,6},{5,7},{6,4},{7,5},{8,10},{9,11},{10,... | collective-permute-start | bytes 786440 | tf_op jit(solution)/shard_map/ppermute | solution.py:19
  176.0 5.0 %collective-permute-start.28 = (bf16[256,256]{1,0:T(8,128)(2,1)S(1)}, bf16[256,256]{1,0:T(8,128)(2,1)S(1)}, u32[]{:S(2)}, u32[]{:S(2)}) collective-permute-start(bf16[256,256]{1,0:T(8,128)(2,1)S(1)} %dynamic-slice_convert_fusion.4), channel_id=1, source_target_pairs={{0,8},{4,12},{8,0},{12,4},{16,24},{20,28},{24,16},{28,20},{1,9},{5... | collective-permute-start | bytes 393224 | tf_op jit(solution)/shard_map/ppermute | solution.py:19
  181.1 5.2 %collective-permute-start.29 = (bf16[128,256]{1,0:T(8,128)(2,1)S(1)}, bf16[128,256]{1,0:T(8,128)(2,1)S(1)}, u32[]{:S(2)}, u32[]{:S(2)}) collective-permute-start(bf16[128,256]{1,0:T(8,128)(2,1)S(1)} %dynamic-slice_convert_fusion.6), channel_id=1, source_target_pairs={{0,16},{4,20},{8,24},{12,28},{16,0},{20,4},{24,8},{28,12},{1,17},{... | collective-permute-start | bytes 196616 | tf_op jit(solution)/shard_map/ppermute | solution.py:19
  186.3 4.5 %collective-permute-start.30 = (f32[64,256]{1,0:T(8,128)S(1)}, f32[64,256]{1,0:T(8,128)S(1)}, u32[]{:S(2)}, u32[]{:S(2)}) collective-permute-start(f32[64,256]{1,0:T(8,128)S(1)} %constant_dynamic-slice_fusion), channel_id=1, source_target_pairs={{0,4},{4,0},{8,12},{12,8},{16,20},{20,16},{24,28},{28,24},{1,5},{5... | collective-permute-start | bytes 196616 | tf_op jit(solution)/shard_map/ppermute | solution.py:19
  190.9 4.3 %collective-permute-start.31 = (f32[64,256]{1,0:T(8,128)S(1)}, f32[64,256]{1,0:T(8,128)S(1)}, u32[]{:S(2)}, u32[]{:S(2)}) collective-permute-start(f32[64,256]{1,0:T(8,128)S(1)} %multiply_add_fusion), channel_id=1, source_target_pairs={{0,4},{4,0},{8,12},{12,8},{16,20},{20,16},{24,28},{28,24},{1,5},{5... | collective-permute-start | bytes 196616 | tf_op jit(solution)/shard_map/ppermute | solution.py:19
  195.3 7.3 %collective-permute-start.32 = (f32[128,256]{1,0:T(8,128)S(1)}, f32[128,256]{1,0:T(8,128)S(1)}, u32[]{:S(2)}, u32[]{:S(2)}) collective-permute-start(f32[128,256]{1,0:T(8,128)S(1)} %pad_maximum_fusion.13), channel_id=1, source_target_pairs={{0,16},{4,20},{8,24},{12,28},{16,0},{20,4},{24,8},{28,12},{1,17},{... | collective-permute-start | bytes 393224 | tf_op jit(solution)/shard_map/ppermute | solution.py:19
  202.6 6.4 %collective-permute-start.33 = (f32[256,256]{1,0:T(8,128)S(1)}, f32[256,256]{1,0:T(8,128)S(1)}, u32[]{:S(2)}, u32[]{:S(2)}) collective-permute-start(f32[256,256]{1,0:T(8,128)S(1)} %pad_maximum_fusion.11), channel_id=1, source_target_pairs={{0,8},{4,12},{8,0},{12,4},{16,24},{20,28},{24,16},{28,20},{1,9},{5... | collective-permute-start | bytes 786440 | tf_op jit(solution)/shard_map/ppermute | solution.py:19
  202.8 6.7 %collective-permute-start.22 = (bf16[2,512,128]{2,1,0:T(8,128)(2,1)S(1)}, bf16[2,512,128]{2,1,0:T(8,128)(2,1)S(1)}, u32[]{:S(2)}, u32[]{:S(2)}) collective-permute-start(bf16[2,512,128]{2,1,0:T(8,128)(2,1)S(1)} %get-tuple-element.36), channel_id=1, source_target_pairs={{0,1},{1,0},{2,3},{3,2},{4,5},{5,4},{6,7},{7,6},{8,9},{9,8},{10,11... | collective-permute-start | bytes 786440 | tf_op jit(solution)/shard_map/ppermute | solution.py:29
  202.9 6.6 %collective-permute-start.23 = (bf16[2,512,128]{2,1,0:T(8,128)(2,1)S(1)}, bf16[2,512,128]{2,1,0:T(8,128)(2,1)S(1)}, u32[]{:S(2)}, u32[]{:S(2)}) collective-permute-start(bf16[2,512,128]{2,1,0:T(8,128)(2,1)S(1)} %get-tuple-element.37), channel_id=1, source_target_pairs={{1,2},{2,1},{5,6},{6,5},{9,10},{10,9},{13,14},{14,13},{17,18},{18,... | collective-permute-start | bytes 786440 | tf_op jit(solution)/shard_map/ppermute | solution.py:28
  209.2 12.9 %collective-permute-start.34 = (f32[512,256]{1,0:T(8,128)S(1)}, f32[512,256]{1,0:T(8,128)S(1)}, u32[]{:S(2)}, u32[]{:S(2)}) collective-permute-start(f32[512,256]{1,0:T(8,128)S(1)} %pad_maximum_fusion.5), channel_id=1, source_target_pairs={{0,2},{1,3},{2,0},{3,1},{4,6},{5,7},{6,4},{7,5},{8,10},{9,11},{10,... | collective-permute-start | bytes 1572872 | tf_op jit(solution)/shard_map/ppermute | solution.py:19
  222.3 16.0 %collective-permute-start.35 = (f32[1024,256]{1,0:T(8,128)S(1)}, f32[1024,256]{1,0:T(8,128)S(1)}, u32[]{:S(2)}, u32[]{:S(2)}) collective-permute-start(f32[1024,256]{1,0:T(8,128)S(1)} %pad_maximum_fusion.2), channel_id=1, source_target_pairs={{0,1},{1,0},{2,3},{3,2},{4,5},{5,4},{6,7},{7,6},{8,9},{9,8},{10,11... | collective-permute-start | bytes 3145736 | tf_op jit(solution)/shard_map/ppermute | solution.py:19
  222.4 14.4 %collective-permute-start.24 = (bf16[2,128,512]{2,1,0:T(8,128)(2,1)S(1)}, bf16[2,128,512]{2,1,0:T(8,128)(2,1)S(1)}, u32[]{:S(2)}, u32[]{:S(2)}) collective-permute-start(bf16[2,128,512]{2,1,0:T(8,128)(2,1)S(1)} %get-tuple-element.24), channel_id=1, source_target_pairs={{0,4},{4,0},{8,12},{12,8},{16,20},{20,16},{24,28},{28,24},{1,5},{5... | collective-permute-start | bytes 786440 | tf_op jit(solution)/shard_map/ppermute | solution.py:29
  223.5 13.3 %collective-permute-start.25 = (bf16[2,128,512]{2,1,0:T(8,128)(2,1)S(1)}, bf16[2,128,512]{2,1,0:T(8,128)(2,1)S(1)}, u32[]{:S(2)}, u32[]{:S(2)}) collective-permute-start(bf16[2,128,512]{2,1,0:T(8,128)(2,1)S(1)} %get-tuple-element.25), channel_id=1, source_target_pairs={{4,8},{12,16},{20,24},{8,4},{16,12},{24,20},{5,9},{13,17},{21,25},... | collective-permute-start | bytes 786440 | tf_op jit(solution)/shard_map/ppermute | solution.py:28
  (20 other events, 213.6 us)
where the time goes:
time: 242 us; the launch traced here: 240 us
  waiting for transfers between devices  94.2 us (39%)
  starting transfers between devices  53.2 us (22%)
  Pallas kernels  52.7 us (22%)
  other arithmetic  26.7 us (11%)
  local copies, waits for them, and re-layouts  8.27 us (3%)
  matrix products  3.17 us (1%)
    ppermute x20, waiting for transfers between devices, swap_bit(): lax.ppermute(values, axis, [(i, i ^ bit) for i in range(lax.axis_size(axi...  69.4 us
    pallas_call x2, Pallas kernels, propagate(): pl.pallas_call(propagate_body, out_shape=(jax.ShapeDtypeStruct((2, ext_ro...  52.7 us
    ppermute x20, starting transfers between devices, swap_bit(): lax.ppermute(values, axis, [(i, i ^ bit) for i in range(lax.axis_size(axi...  25.3 us
    ppermute x8, waiting for transfers between devices, neighbours(): from_inner = lax.ppermute(jnp.where(odd, before, after), axis, inner)  21.1 us
    ppermute x8, starting transfers between devices, neighbours(): from_outer = lax.ppermute(jnp.where(odd, after, before), axis, outer)  18 us
    ppermute x8, starting transfers between devices, neighbours(): from_inner = lax.ppermute(jnp.where(odd, before, after), axis, inner)  9.94 us
  transfers between devices with their start and end apart: 36, of which 22 were waited for; matrix products, arithmetic and copies ran while one was open for 9% of the time, Pallas kernels for 0%

commit v1 on v0

v1 whole, which is shorter than its diff:
```python
import jax
import jax.numpy as jnp
import numpy as np
from jax import lax
from jax.experimental import pallas as pl
from jax.experimental.pallas import tpu as pltpu
from jax.sharding import PartitionSpec as P


ITERS = 2


EPSILON = 1e-06


LANES = 128


def swap_bit(values, axis, bit):
    return lax.ppermute(values, axis, [(i, i ^ bit) for i in range(lax.axis_size(axis))])


def shift_both(before, after, axis):
    up = [(i, i + 1) for i in range(lax.axis_size(axis) - 1)]
    previous = lax.ppermute(after, axis, up)
    following = lax.ppermute(before, axis, [(target, source) for source, target in up])
    return previous, following


def swap_both(outer, inner, axis):
    count = lax.axis_size(axis)
    inner_pairs = [(i, i ^ 1) for i in range(count)]
    outer_pairs = [(i, i + 1) for i in range(1, count - 1, 2)]
    outer_pairs = outer_pairs + [(target, source) for source, target in outer_pairs]
    outer = lax.ppermute(outer, axis, outer_pairs)
    inner = lax.ppermute(inner, axis, inner_pairs)
    return outer, inner


def pick(condition, first, second):
    return jnp.where(condition, first, second), jnp.where(condition, second, first)


def dft_tables(length):
    counter = np.arange(length, dtype=np.int32)
    phase_steps = counter[:, None] * counter[None, :] % length
    angle_grid = phase_steps.astype(np.float32) * np.float32(2.0 * np.pi / length)
    norm_factor = np.float32(1.0) / np.sqrt(np.float32(length))
    return (np.cos(angle_grid) * norm_factor, -np.sin(angle_grid) * norm_factor)


def split_tables(length):
    real_table, imag_table = dft_tables(length)
    half = length // 2
    lefts = []
    for first in (0, 1):
        re = real_table[first::2, :half]
        im = imag_table[first::2, :half]
        lefts.append(np.block([[re, -im], [im, re]]))
    return jnp.asarray(np.stack(lefts + [lefts[0].T, lefts[1].T]), jnp.bfloat16)


def even_odd(values):
    side = values.shape[-1]
    order = np.concatenate([np.arange(0, side, 2), np.arange(1, side, 2)])
    pick = jnp.asarray(np.arange(side)[:, None] == order[None, :], jnp.float32)
    right = jnp.einsum(
        "brc,ck->brk", values, pick, precision=lax.Precision.HIGHEST,
        preferred_element_type=jnp.float32,
    )
    return jnp.einsum(
        "rk,brc->bkc", pick, right, precision=lax.Precision.HIGHEST,
        preferred_element_type=jnp.float32,
    )


def mm(left, right):
    return jnp.dot(left, right, preferred_element_type=jnp.float32)


def propagate_body(
    rows_ref, cols_ref, flag_ref, tile_ref, above_ref, below_ref, outer_ref, inner_ref, own_ref,
    other_ref, amp_ref, table_ref, grad_ref, rim_outer_ref, rim_inner_ref, keep_ref, send_ref,
    ext_f32, patch_ref, far_ref, acc_ref, probe_ref, probe_acc, scale_ref,
):
    modes, _, side, _ = probe_ref.shape
    half = side // 2
    step = pl.program_id(0)
    tiles = ext_f32.shape[1]
    edge = half // LANES
    tile_rows = tile_ref.shape[1]
    odd = flag_ref[0]
    upper = flag_ref[1]
    share = modes // 2

    @pl.when(step == 0)
    def _():
        probe_ref[pl.ds(upper * share, share)] = own_ref[...].astype(jnp.float32)
        probe_ref[pl.ds((1 - upper) * share, share)] = other_ref[...].astype(jnp.float32)
        for part in range(2):
            for tile in range(edge):
                at = slice(tile * LANES, (tile + 1) * LANES)
                last = (tiles - edge) * odd + tile
                first = (tiles - edge) * (1 - odd) + tile
                ext_f32[part, last] = outer_ref[part, :, at].astype(jnp.float32)
                ext_f32[part, first] = inner_ref[part, :, at].astype(jnp.float32)
            for tile in range(edge, tiles - edge):
                at = slice((tile - edge) * LANES, (tile - edge + 1) * LANES)
                ext_f32[part, tile, :half] = above_ref[part, :, at].astype(jnp.float32)
                ext_f32[part, tile, half : half + tile_rows] = tile_ref[part, :, at].astype(
                    jnp.float32
                )
                ext_f32[part, tile, half + tile_rows :] = below_ref[part, :, at].astype(
                    jnp.float32
                )
        acc_ref[...] = jnp.zeros(acc_ref.shape, jnp.float32)
        probe_acc[...] = jnp.zeros(probe_acc.shape, jnp.float32)
        power = jnp.zeros((side, side), jnp.float32)
        for mode in range(modes):
            for part in range(2):
                values = probe_ref[mode, part]
                power += values * values
        scale_ref[0] = 1.0 / (jnp.max(power) + EPSILON)

    row = rows_ref[step]
    col = cols_ref[step]
    tile0 = col // LANES
    lane0 = col % LANES
    width = side // LANES
    lane = lax.broadcasted_iota(jnp.int32, (side, LANES), 1)
    left_part = lane < LANES - lane0
    for part in range(2):
        rolled = [
            pltpu.roll(
                ext_f32[part, tile0 + j, pl.ds(row, side), :], (LANES - lane0) % LANES, 1
            )
            for j in range(width + 1)
        ]
        for j in range(width):
            patch_ref[part, :, j * LANES : (j + 1) * LANES] = jnp.where(
                left_part, rolled[j], rolled[j + 1]
            )

    table_le = table_ref[0]
    table_lo = table_ref[1]
    table_re = table_ref[2]
    table_ro = table_ref[3]
    power_e = jnp.zeros((side, half), jnp.float32)
    power_o = jnp.zeros((side, half), jnp.float32)
    for mode in range(modes):
        wave = []
        for rows in (slice(0, half), slice(half, side)):
            qr = probe_ref[mode, 0, rows, :]
            qi = probe_ref[mode, 1, rows, :]
            pr = patch_ref[0, rows, :]
            pi = patch_ref[1, rows, :]
            wave.append((qr * pr - qi * pi, qr * pi + qi * pr))
        (lo_re, lo_im), (hi_re, hi_im) = wave
        sums = jnp.concatenate(
            [(lo_re + hi_re).astype(jnp.bfloat16), (lo_im + hi_im).astype(jnp.bfloat16)], axis=0
        )
        diffs = jnp.concatenate(
            [(lo_re - hi_re).astype(jnp.bfloat16), (lo_im - hi_im).astype(jnp.bfloat16)], axis=0
        )
        evens, odds = [], []
        for half_field in (mm(table_le, sums), mm(table_lo, diffs)):
            re_lo, re_hi = half_field[:half, :half], half_field[:half, half:]
            im_lo, im_hi = half_field[half:, :half], half_field[half:, half:]
            evens.append(
                jnp.concatenate(
                    [(re_lo + re_hi).astype(jnp.bfloat16), (im_lo + im_hi).astype(jnp.bfloat16)],
                    axis=1,
                )
            )
            odds.append(
                jnp.concatenate(
                    [(re_lo - re_hi).astype(jnp.bfloat16), (im_lo - im_hi).astype(jnp.bfloat16)],
                    axis=1,
                )
            )
        far_e = mm(jnp.concatenate(evens, axis=0), table_re)
        far_o = mm(jnp.concatenate(odds, axis=0), table_ro)
        far_ref[mode, 0] = far_e
        far_ref[mode, 1] = far_o
        power_e += far_e[:, :half] * far_e[:, :half] + far_e[:, half:] * far_e[:, half:]
        power_o += far_o[:, :half] * far_o[:, :half] + far_o[:, half:] * far_o[:, half:]

    ratio_e = amp_ref[0, :, :half] * lax.rsqrt(jnp.maximum(power_e, 1.0)) - 1.0
    ratio_o = amp_ref[0, :, half:] * lax.rsqrt(jnp.maximum(power_o, 1.0)) - 1.0

    obj = [[None, None], [None, None]]
    for mode in range(modes):
        far_e = far_ref[mode, 0]
        far_o = far_ref[mode, 1]
        diff_e = jnp.concatenate(
            [
                (far_e[:, :half] * ratio_e).astype(jnp.bfloat16),
                (far_e[:, half:] * ratio_e).astype(jnp.bfloat16),
            ],
            axis=1,
        )
        diff_o = jnp.concatenate(
            [
                (far_o[:, :half] * ratio_o).astype(jnp.bfloat16),
                (far_o[:, half:] * ratio_o).astype(jnp.bfloat16),
            ],
            axis=1,
        )
        u = mm(diff_e, table_le)
        v = mm(diff_o, table_lo)
        total = (u + v).astype(jnp.bfloat16)
        gap = (u - v).astype(jnp.bfloat16)
        backs = []
        for rows in (slice(0, half), slice(half, side)):
            backs.append(
                jnp.concatenate(
                    [
                        jnp.concatenate([total[rows, :half], gap[rows, :half]], axis=1),
                        jnp.concatenate([total[rows, half:], gap[rows, half:]], axis=1),
                    ],
                    axis=0,
                )
            )
        p = mm(table_re, backs[0])
        q = mm(table_ro, backs[1])
        for index, sign in ((0, 1), (1, -1)):
            rows = slice(index * half, (index + 1) * half)
            if sign > 0:
                chi_re = p[:half] + q[:half]
                chi_im = p[half:] + q[half:]
            else:
                chi_re = p[:half] - q[:half]
                chi_im = p[half:] - q[half:]
            qr = probe_ref[mode, 0, rows, :]
            qi = probe_ref[mode, 1, rows, :]
            pr = patch_ref[0, rows, :]
            pi = patch_ref[1, rows, :]
            term_re = qr * chi_re + qi * chi_im
            term_im = qr * chi_im - qi * chi_re
            if mode == 0:
                obj[index] = [term_re, term_im]
            else:
                obj[index][0] += term_re
                obj[index][1] += term_im
            probe_acc[mode, 0, rows, :] += pr * chi_re + pi * chi_im
            probe_acc[mode, 1, rows, :] += pr * chi_im - pi * chi_re

    lane_h = lax.broadcasted_iota(jnp.int32, (half, LANES), 1)
    right_part = lane_h >= lane0
    scale = scale_ref[0]
    for index in range(2):
        for part in range(2):
            values = obj[index][part] * scale
            rolled = [
                pltpu.roll(values[:, j * LANES : (j + 1) * LANES], lane0, 1) for j in range(width)
            ]
            where = pl.ds(row + index * half, half)
            for j in range(width + 1):
                above = rolled[j] if j < width else jnp.zeros_like(rolled[0])
                below = rolled[j - 1] if j > 0 else jnp.zeros_like(rolled[0])
                acc_ref[part, tile0 + j, where, :] += jnp.where(right_part, above, below)

    @pl.when(step == pl.num_programs(0) - 1)
    def _():
        keep_ref[...] = probe_acc[pl.ds(upper * share, share)]
        send_ref[...] = probe_acc[pl.ds((1 - upper) * share, share)].astype(send_ref.dtype)
        for part in range(2):
            for tile in range(edge):
                at = slice(tile * LANES, (tile + 1) * LANES)
                last = (tiles - edge) * odd + tile
                first = (tiles - edge) * (1 - odd) + tile
                rim_outer_ref[part, :, at] = acc_ref[part, last].astype(rim_outer_ref.dtype)
                rim_inner_ref[part, :, at] = acc_ref[part, first].astype(rim_inner_ref.dtype)
            for tile in range(edge, tiles - edge):
                at = slice((tile - edge) * LANES, (tile - edge + 1) * LANES)
                grad_ref[part, :, at] = acc_ref[part, tile]


def propagate(rows, cols, flags, pieces, probe_parts, amplitude, tables):
    count = rows.shape[0]
    share, _, side, _ = probe_parts[0].shape
    modes = 2 * share
    half = side // 2
    tile_rows, tile_cols = pieces[0].shape[1:]
    ext_rows = tile_rows + side
    tiles = (tile_cols + side) // LANES

    def whole(*shape):
        return pl.BlockSpec(
            shape, lambda i, *_: (0,) * len(shape), pipeline_mode=pl.Buffered(1)
        )

    outs = (
        jax.ShapeDtypeStruct((2, ext_rows, tile_cols), jnp.float32),
        jax.ShapeDtypeStruct((2, ext_rows, half), jnp.bfloat16),
        jax.ShapeDtypeStruct((2, ext_rows, half), jnp.bfloat16),
        jax.ShapeDtypeStruct((share, 2, side, side), jnp.float32),
        jax.ShapeDtypeStruct((share, 2, side, side), jnp.bfloat16),
    )
    return pl.pallas_call(
        propagate_body,
        out_shape=outs,
        grid_spec=pltpu.PrefetchScalarGridSpec(
            num_scalar_prefetch=3,
            grid=(count,),
            in_specs=[whole(*piece.shape) for piece in pieces]
            + [whole(*part.shape) for part in probe_parts]
            + [
                pl.BlockSpec((1, side, side), lambda i, *_: (i, 0, 0)),
                whole(*tables.shape),
            ],
            out_specs=tuple(whole(*out.shape) for out in outs),
            scratch_shapes=[
                pltpu.VMEM((2, tiles, ext_rows, LANES), jnp.float32),
                pltpu.VMEM((2, side, side), jnp.float32),
                pltpu.VMEM((modes, 2, side, side), jnp.float32),
                pltpu.VMEM((2, tiles, ext_rows, LANES), jnp.float32),
                pltpu.VMEM((modes, 2, side, side), jnp.float32),
                pltpu.VMEM((modes, 2, side, side), jnp.float32),
                pltpu.SMEM((1,), jnp.float32),
            ],
        ),
        name="propagate",
    )(rows, cols, flags, *pieces, *probe_parts, amplitude, tables)


def exchange_steps():
    steps = []
    bit = 1
    while bit < lax.axis_size("obj"):
        steps.append(("obj", bit))
        bit *= 2
    bit = 2
    while bit < lax.axis_size("dp"):
        steps.append(("dp", bit))
        bit *= 2
    return steps


def upper_of(axis, bit):
    return (lax.axis_index(axis) // bit) % 2


def halve(values, axis, bit):
    rows = values.shape[0] // 2
    upper = upper_of(axis, bit)
    keep = lax.dynamic_slice_in_dim(values, upper * rows, rows, 0)
    send = lax.dynamic_slice_in_dim(values, (1 - upper) * rows, rows, 0)
    return keep, send


def sum_to_share(keep, send):
    for index, (axis, bit) in enumerate(exchange_steps()):
        if index > 0:
            keep, send = halve(values, axis, bit)
        got = swap_bit(send.astype(jnp.bfloat16), axis, bit)
        values = keep + got.astype(keep.dtype)
    got = swap_bit(values, "dp", 1)
    return values + got


def own_share(values):
    for axis, bit in exchange_steps():
        values = halve(values, axis, bit)[0]
    return values


def join_shares(values):
    steps = exchange_steps()
    for index in range(len(steps) - 1, -1, -1):
        axis, bit = steps[index]
        got = swap_bit(values, axis, bit)
        if index == 0:
            return values, got
        values = jnp.concatenate(pick(upper_of(axis, bit) == 0, values, got), axis=0)


def fold_rims(current, grad, rim_outer, rim_inner, half):
    tile_rows, tile_cols = current.shape[1:]
    odd = lax.axis_index("obj") % 2 == 1
    outer, inner = swap_both(rim_outer, rim_inner, "obj")
    left, right = pick(odd, inner, outer)
    wide = jnp.zeros((2, grad.shape[1], tile_cols - 2 * half), left.dtype)
    total = grad + jnp.concatenate([left, wide, right], axis=2).astype(jnp.float32)
    low = total.astype(jnp.bfloat16)
    first, last = low[:, :half], low[:, -half:]
    above, below = shift_both(first, last, "dp")
    tall = jnp.zeros((2, tile_rows - 2 * half, tile_cols), above.dtype)
    rows = jnp.concatenate([above, tall, below], axis=1).astype(jnp.float32)
    current = current + (total[:, half : half + tile_rows] + rows)
    return current, current.astype(jnp.bfloat16)


def gather_rims(tile, half):
    low = lambda values: values.astype(jnp.bfloat16)
    above, below = shift_both(low(tile[:, :half]), low(tile[:, -half:]), "dp")
    tile = low(tile)
    first = jnp.concatenate([above[:, :, :half], tile[:, :, :half], below[:, :, :half]], axis=1)
    last = jnp.concatenate([above[:, :, -half:], tile[:, :, -half:], below[:, :, -half:]], axis=1)
    odd = lax.axis_index("obj") % 2 == 1
    outer, inner = swap_both(*pick(odd, last, first), "obj")
    return tile, above, below, outer, inner


def shards(object_field, probe_modes, amplitude, offsets):
    modes, _, side, _ = probe_modes.shape
    half = side // 2
    tile_rows = object_field.shape[1]
    tile_cols = object_field.shape[2]
    count = offsets.shape[0]
    devices = lax.axis_size("dp") * lax.axis_size("obj")
    total_positions = count * devices
    tables = split_tables(side)
    amplitude = even_odd(amplitude)
    top_rows = offsets[:, 0] - lax.axis_index("dp") * tile_rows + half
    left_cols = offsets[:, 1] - lax.axis_index("obj") * tile_cols + half
    upper = upper_of("obj", 1)
    flags = jnp.stack([lax.axis_index("obj") % 2, upper])
    split = (modes // 2, 2, side, side)
    current = object_field
    probe_parts = [
        half_modes.astype(jnp.bfloat16).reshape(split)
        for half_modes in halve(probe_modes.reshape(-1, side), "obj", 1)
    ]
    probe_share = own_share(probe_modes.reshape(-1, side))
    pieces = gather_rims(current, half)
    for turn in range(ITERS):
        grad, rim_outer, rim_inner, keep, send = propagate(
            top_rows, left_cols, flags, pieces, probe_parts, amplitude, tables
        )
        current, low_tile = fold_rims(current, grad, rim_outer, rim_inner, half)
        summed = sum_to_share(keep.reshape(-1, side), send.reshape(-1, side))
        probe_share = probe_share + summed / total_positions
        if turn + 1 < ITERS:
            pieces = gather_rims(low_tile, half)
            low_share = probe_share.astype(jnp.bfloat16)
            parts = join_shares(low_share)
            probe_parts = [part.reshape(split) for part in parts]
        else:
            rest = (probe_share - low_share.astype(jnp.float32)).astype(jnp.bfloat16)
            parts = [
                part.astype(jnp.float32) + more.astype(jnp.float32)
                for part, more in zip(parts, join_shares(rest))
            ]
            parts = pick(upper == 0, *parts)
            probe = jnp.concatenate(parts, axis=0).reshape(probe_modes.shape)
    return (current, probe)


def solution(mesh):
    in_specs = (P(None, "dp", "obj"), P(), P(("dp", "obj"), None, None), P(("dp", "obj"), None))
    out_specs = (P(None, "dp", "obj"), P())
    return jax.shard_map(shards, mesh=mesh, in_specs=in_specs, out_specs=out_specs, check_vma=False)
```

time: 242 us -> 211 us (0.87)
  waiting for transfers between devices: 94.2 us -> 55.6 us
  starting transfers between devices: 53.2 us -> 67 us
  other arithmetic: 26.7 us -> 19.9 us
    ppermute x20 -> x18, waiting for transfers between devices: 69.4 us -> 41 us  [swap_bit(): lax.ppermute(values, axis, [(i, i ^ bit) for i in range(lax.axis_size(axi...]
    ppermute x20 -> x18, starting transfers between devices: 25.3 us -> 37.2 us  [swap_bit(): lax.ppermute(values, axis, [(i, i ^ bit) for i in range(lax.axis_size(axi...]
    ppermute x16, waiting for transfers between devices: 24.8 us -> 14.6 us  [the longest x4 8.24 us: shift_both(): previous = lax.ppermute(after, axis, up)]
    select_n x26 -> x11, other arithmetic: 9.34 us -> 2.11 us  [the longest x9 1.89 us: pick(): jnp.where(condition, first, second)]
    slice x9 -> x10, local copies, waits for them, and re-layouts: 4.81 us -> 1.89 us  [the longest x2 1.63 us: fold_rims(): first, last = (low[:, :half], low[:, -half:])]
    unnamed x32 -> x50, local copies, waits for them, and re-layouts: 0.52 us -> 3.21 us
    convert_element_type x6 -> x4, other arithmetic: 7.27 us -> 4.67 us  [the longest x1 1.61 us: fold_rims(): return (current, current.astype(jnp.bfloat16))]
    convert_element_type x2, other arithmetic: 0.78 us -> 3.34 us  [fold_rims(): low = total.astype(jnp.bfloat16)]
  transfers between devices with their start and end apart: 36 -> 34, of which waited for: 22 -> 19; matrix products, arithmetic and copies ran while one was open for 9% -> 11% of each run, Pallas kernels for 0% -> 0%
where the time goes in v1:
time: 211 us; the launch traced here: 210 us
  starting transfers between devices  67 us (32%)
  waiting for transfers between devices  55.6 us (26%)
  Pallas kernels  52.7 us (25%)
  other arithmetic  19.9 us (9%)
  local copies, waits for them, and re-layouts  7.89 us (4%)
  matrix products  5.38 us (3%)
    pallas_call x2, Pallas kernels, propagate(): pl.pallas_call(propagate_body, out_shape=outs, grid_spec=pltpu.PrefetchSc...  52.7 us
    ppermute x18, waiting for transfers between devices, swap_bit(): lax.ppermute(values, axis, [(i, i ^ bit) for i in range(lax.axis_size(axi...  41 us
    ppermute x18, starting transfers between devices, swap_bit(): lax.ppermute(values, axis, [(i, i ^ bit) for i in range(lax.axis_size(axi...  37.2 us
    ppermute x4, starting transfers between devices, shift_both(): lax.ppermute(before, axis, [(target, source) for source, target in up])  16.9 us
    ppermute x4, starting transfers between devices, shift_both(): previous = lax.ppermute(after, axis, up)  9.86 us
    ppermute x4, waiting for transfers between devices, shift_both(): previous = lax.ppermute(after, axis, up)  8.24 us
    ppermute x4, waiting for transfers between devices, shift_both(): lax.ppermute(before, axis, [(target, source) for source, target in up])  5.47 us
  transfers between devices with their start and end apart: 34, of which 19 were waited for; matrix products, arithmetic and copies ran while one was open for 11% of the time, Pallas kernels for 0%

profile of v1, /device:TPU:8, one launch (start us, length us, event | category | flops | bytes accessed | tf_op | source)
XLA Modules:
  0.0 209.8 jit_solution(15957901913308556103)
XLA Ops:
  2.1 3.3 %collective-permute-start.1 = (bf16[2,128,512]{2,1,0:T(8,128)(2,1)S(1)}, bf16[2,128,512]{2,1,0:T(8,128)(2,1)S(1)}, u32[]{:S(2)}, u32[]{:S(2)}) collective-permute-start(bf16[2,128,512]{2,1,0:T(8,128)(2,1)S(1)} %get-tuple-element.54), channel_id=1, source_target_pairs={{4,0},{8,4},{12,8},{16,12},{20,16},{24,20},{28,24},{5,1},{9,5},{13... | collective-permute-start | bytes 786440 | tf_op jit(solution)/shard_map/ppermute | solution.py:26
  5.4 2.6 %collective-permute-start = (bf16[2,128,512]{2,1,0:T(8,128)(2,1)S(1)}, bf16[2,128,512]{2,1,0:T(8,128)(2,1)S(1)}, u32[]{:S(2)}, u32[]{:S(2)}) collective-permute-start(bf16[2,128,512]{2,1,0:T(8,128)(2,1)S(1)} %get-tuple-element.55), channel_id=1, source_target_pairs={{0,4},{4,8},{8,12},{12,16},{16,20},{20,24},{24,28},{1,5},{5,9},{9,... | collective-permute-start | bytes 786440 | tf_op jit(solution)/shard_map/ppermute | solution.py:25
  8.0 2.7 %fusion.23 = f32[256,6,256]{2,0,1:T(8,128)S(1)} fusion(f32[256,256,1]{1,0,2:T(8,128)S(1)} %copy-done.11, f32[6,256,256]{2,1,0:T(8,128)S(1)} %copy-done), kind=kOutput, calls=%fused_computation.79 | convolution fusion | flops 1207959552 | bytes 3407872 | tf_op jit(solution)/shard_map/brc,ck->brk/dot_general | solution.py:67
  10.7 2.7 %fusion.2.amp_ref = f32[6,256,256]{2,1,0:T(8,128)} fusion(f32[256,256,1]{1,0,2:T(8,128)S(1)} %copy-done.11, f32[256,6,256]{2,0,1:T(8,128)S(1)} %fusion.23), kind=kOutput, calls=%fused_computation.5 | convolution fusion | flops 1207959552 | bytes 3407872 | tf_op jit(solution)/shard_map/rk,brc->bkc/dot_general | solution.py:71
  13.5 2.6 %dynamic-slice_convert_fusion = (bf16[1024,256]{1,0:T(8,128)(2,1)}, bf16[1024,256]{1,0:T(8,128)(2,1)}) fusion(f32[2048,256]{1,0:T(8,128)} %bitcast.32, s32[]{:T(128)S(6)} %select_n.237, s32[]{:T(128)S(6)} %select_n.236), kind=kLoop, calls=%fused_computation.14 | loop fusion | bytes 2097160 | tf_op jit(solution)/shard_map/convert_element_type | solution.py:422
  20.7 26.4 %propagate.2 = (f32[2,512,512]{2,1,0:T(8,128)}, bf16[2,512,128]{2,1,0:T(8,128)(2,1)}, bf16[2,512,128]{2,1,0:T(8,128)(2,1)}, f32[2,2,256,256]{3,2,1,0:T(8,128)}, bf16[2,2,256,256]{3,2,1,0:T(8,128)(2,1)}) custom-call(s32[6]{0:T(128)} %get-tuple-element.73.rows_ref, s32[6]{0:T(128)} %get-tuple-element.72.cols_ref, s32[2]{0:T(128)} %pad_add_fusion.flag_ref, ...), custom_call_target="tpu_custom_call" | custom-call | tf_op jit(solution)/shard_map/propagate/pallas_call | solution.py:300
  47.1 6.1 %collective-permute-start.12 = (bf16[1024,256]{1,0:T(8,128)(2,1)}, bf16[1024,256]{1,0:T(8,128)(2,1)S(1)}, u32[]{:S(2)}, u32[]{:S(2)}) collective-permute-start(bf16[1024,256]{1,0:T(8,128)(2,1)} %bitcast.34), channel_id=1, source_target_pairs={{0,1},{1,0},{2,3},{3,2},{4,5},{5,4},{6,7},{7,6},{8,9},{9,8},{10,11... | collective-permute-start | bytes 1572872 | tf_op jit(solution)/shard_map/ppermute | solution.py:20
  58.8 6.2 %collective-permute-done.13 = bf16[512,256]{1,0:T(8,128)(2,1)S(1)} collective-permute-done((bf16[512,256]{1,0:T(8,128)(2,1)S(1)}, bf16[512,256]{1,0:T(8,128)(2,1)S(1)}, u32[]{:S(2)}, u32[]{:S(2)}) %collective-permute-start.13) | collective-permute-done | bytes 262176 | tf_op jit(solution)/shard_map/ppermute | solution.py:20
  65.5 4.6 %collective-permute-done.14 = bf16[256,256]{1,0:T(8,128)(2,1)S(1)} collective-permute-done((bf16[256,256]{1,0:T(8,128)(2,1)S(1)}, bf16[256,256]{1,0:T(8,128)(2,1)S(1)}, u32[]{:S(2)}, u32[]{:S(2)}) %collective-permute-start.14) | collective-permute-done | bytes 131104 | tf_op jit(solution)/shard_map/ppermute | solution.py:20
  70.2 2.6 %collective-permute-start.15 = (bf16[128,256]{1,0:T(8,128)(2,1)S(1)}, bf16[128,256]{1,0:T(8,128)(2,1)S(1)}, u32[]{:S(2)}, u32[]{:S(2)}) collective-permute-start(bf16[128,256]{1,0:T(8,128)(2,1)S(1)} %dynamic-slice_convert_fusion.7), channel_id=1, source_target_pairs={{0,16},{4,20},{8,24},{12,28},{16,0},{20,4},{24,8},{28,12},{1,17},{... | collective-permute-start | bytes 196616 | tf_op jit(solution)/shard_map/ppermute | solution.py:20
  75.4 2.4 %collective-permute-start.16 = (f32[128,256]{1,0:T(8,128)S(1)}, f32[128,256]{1,0:T(8,128)S(1)}, u32[]{:S(2)}, u32[]{:S(2)}) collective-permute-start(f32[128,256]{1,0:T(8,128)S(1)} %convert_add_fusion.9), channel_id=1, source_target_pairs={{0,4},{4,0},{8,12},{12,8},{16,20},{20,16},{24,28},{28,24},{1,5},{5... | collective-permute-start | bytes 393224 | tf_op jit(solution)/shard_map/ppermute | solution.py:20
  80.6 4.8 %collective-permute-start.7 = (bf16[2,128,512]{2,1,0:T(8,128)(2,1)}, bf16[2,128,512]{2,1,0:T(8,128)(2,1)S(1)}, u32[]{:S(2)}, u32[]{:S(2)}) collective-permute-start(bf16[2,128,512]{2,1,0:T(8,128)(2,1)} %get-tuple-element.35), channel_id=1, source_target_pairs={{4,0},{8,4},{12,8},{16,12},{20,16},{24,20},{28,24},{5,1},{9,5},{13... | collective-permute-start | bytes 786440 | tf_op jit(solution)/shard_map/ppermute | solution.py:26
  87.1 4.3 %collective-permute-start.17 = (bf16[128,256]{1,0:T(8,128)(2,1)S(1)}, bf16[128,256]{1,0:T(8,128)(2,1)S(1)}, u32[]{:S(2)}, u32[]{:S(2)}) collective-permute-start(bf16[128,256]{1,0:T(8,128)(2,1)S(1)} %get-tuple-element.24), channel_id=1, source_target_pairs={{0,16},{4,20},{8,24},{12,28},{16,0},{20,4},{24,8},{28,12},{1,17},{... | collective-permute-start | bytes 196616 | tf_op jit(solution)/shard_map/ppermute | solution.py:20
  94.2 4.4 %collective-permute-start.9 = (bf16[2,128,512]{2,1,0:T(8,128)(2,1)S(1)}, bf16[2,128,512]{2,1,0:T(8,128)(2,1)S(1)}, u32[]{:S(2)}, u32[]{:S(2)}) collective-permute-start(bf16[2,128,512]{2,1,0:T(8,128)(2,1)S(1)} %get-tuple-element.46), channel_id=1, source_target_pairs={{4,0},{8,4},{12,8},{16,12},{20,16},{24,20},{28,24},{5,1},{9,5},{13... | collective-permute-start | bytes 786440 | tf_op jit(solution)/shard_map/ppermute | solution.py:26
  100.9 3.0 %collective-permute-start.8 = (bf16[2,128,512]{2,1,0:T(8,128)(2,1)S(1)}, bf16[2,128,512]{2,1,0:T(8,128)(2,1)S(1)}, u32[]{:S(2)}, u32[]{:S(2)}) collective-permute-start(bf16[2,128,512]{2,1,0:T(8,128)(2,1)S(1)} %get-tuple-element.47), channel_id=1, source_target_pairs={{0,4},{4,8},{8,12},{12,16},{16,20},{20,24},{24,28},{1,5},{5,9},{9,... | collective-permute-start | bytes 786440 | tf_op jit(solution)/shard_map/ppermute | solution.py:25
  106.6 3.5 %collective-permute-done.8.above_ref = bf16[2,128,512]{2,1,0:T(8,128)(2,1)S(1)} collective-permute-done((bf16[2,128,512]{2,1,0:T(8,128)(2,1)S(1)}, bf16[2,128,512]{2,1,0:T(8,128)(2,1)S(1)}, u32[]{:S(2)}, u32[]{:S(2)}) %collective-permute-start.8) | collective-permute-done | bytes 262176 | tf_op jit(solution)/shard_map/ppermute | solution.py:25
  112.7 26.4 %propagate.3 = (f32[2,512,512]{2,1,0:T(8,128)}, bf16[2,512,128]{2,1,0:T(8,128)(2,1)}, bf16[2,512,128]{2,1,0:T(8,128)(2,1)}, f32[2,2,256,256]{3,2,1,0:T(8,128)}, bf16[2,2,256,256]{3,2,1,0:T(8,128)(2,1)}) custom-call(s32[6]{0:T(128)} %get-tuple-element.73.rows_ref, s32[6]{0:T(128)} %get-tuple-element.72.cols_ref, s32[2]{0:T(128)} %pad_add_fusion.flag_ref, ...), custom_call_target="tpu_custom_call" | custom-call | tf_op jit(solution)/shard_map/propagate/pallas_call | solution.py:300
  139.1 6.5 %collective-permute-start.25 = (bf16[1024,256]{1,0:T(8,128)(2,1)}, bf16[1024,256]{1,0:T(8,128)(2,1)S(1)}, u32[]{:S(2)}, u32[]{:S(2)}) collective-permute-start(bf16[1024,256]{1,0:T(8,128)(2,1)} %bitcast.35), channel_id=1, source_target_pairs={{0,1},{1,0},{2,3},{3,2},{4,5},{5,4},{6,7},{7,6},{8,9},{9,8},{10,11... | collective-permute-start | bytes 1572872 | tf_op jit(solution)/shard_map/ppermute | solution.py:20
  149.2 8.2 %collective-permute-done.26 = bf16[512,256]{1,0:T(8,128)(2,1)S(1)} collective-permute-done((bf16[512,256]{1,0:T(8,128)(2,1)S(1)}, bf16[512,256]{1,0:T(8,128)(2,1)S(1)}, u32[]{:S(2)}, u32[]{:S(2)}) %collective-permute-start.26) | collective-permute-done | bytes 262176 | tf_op jit(solution)/shard_map/ppermute | solution.py:20
  157.5 5.0 %collective-permute-done.27 = bf16[256,256]{1,0:T(8,128)(2,1)S(1)} collective-permute-done((bf16[256,256]{1,0:T(8,128)(2,1)S(1)}, bf16[256,256]{1,0:T(8,128)(2,1)S(1)}, u32[]{:S(2)}, u32[]{:S(2)}) %collective-permute-start.27) | collective-permute-done | bytes 131104 | tf_op jit(solution)/shard_map/ppermute | solution.py:20
  162.6 2.9 %collective-permute-start.28 = (bf16[128,256]{1,0:T(8,128)(2,1)S(1)}, bf16[128,256]{1,0:T(8,128)(2,1)S(1)}, u32[]{:S(2)}, u32[]{:S(2)}) collective-permute-start(bf16[128,256]{1,0:T(8,128)(2,1)S(1)} %dynamic-slice_convert_fusion.6), channel_id=1, source_target_pairs={{0,16},{4,20},{8,24},{12,28},{16,0},{20,4},{24,8},{28,12},{1,17},{... | collective-permute-start | bytes 196616 | tf_op jit(solution)/shard_map/ppermute | solution.py:20
  165.4 2.4 %collective-permute-done.28 = bf16[128,256]{1,0:T(8,128)(2,1)S(1)} collective-permute-done((bf16[128,256]{1,0:T(8,128)(2,1)S(1)}, bf16[128,256]{1,0:T(8,128)(2,1)S(1)}, u32[]{:S(2)}, u32[]{:S(2)}) %collective-permute-start.28) | collective-permute-done | bytes 65568 | tf_op jit(solution)/shard_map/ppermute | solution.py:20
  167.8 1.9 collective-permute-start.29
  169.8 3.1 %collective-permute-done.29 = f32[128,256]{1,0:T(8,128)S(1)} collective-permute-done((f32[128,256]{1,0:T(8,128)S(1)}, f32[128,256]{1,0:T(8,128)S(1)}, u32[]{:S(2)}, u32[]{:S(2)}) %collective-permute-start.29) | collective-permute-done | bytes 131104 | tf_op jit(solution)/shard_map/ppermute | solution.py:20
  172.9 2.8 %collective-permute-start.30 = (bf16[128,256]{1,0:T(8,128)(2,1)S(1)}, bf16[128,256]{1,0:T(8,128)(2,1)S(1)}, u32[]{:S(2)}, u32[]{:S(2)}) collective-permute-start(bf16[128,256]{1,0:T(8,128)(2,1)S(1)} %subtract_convert_fusion), channel_id=1, source_target_pairs={{0,16},{4,20},{8,24},{12,28},{16,0},{20,4},{24,8},{28,12},{1,17},{... | collective-permute-start | bytes 196616 | tf_op jit(solution)/shard_map/ppermute | solution.py:20
  178.2 2.2 %collective-permute-start.31 = (bf16[256,256]{1,0:T(8,128)(2,1)S(1)}, bf16[256,256]{1,0:T(8,128)(2,1)S(1)}, u32[]{:S(2)}, u32[]{:S(2)}) collective-permute-start(bf16[256,256]{1,0:T(8,128)(2,1)S(1)} %pad_maximum_fusion.10), channel_id=1, source_target_pairs={{0,8},{4,12},{8,0},{12,4},{16,24},{20,28},{24,16},{28,20},{1,9},{5... | collective-permute-start | bytes 393224 | tf_op jit(solution)/shard_map/ppermute | solution.py:20
  180.5 3.3 %collective-permute-done.31 = bf16[256,256]{1,0:T(8,128)(2,1)S(1)} collective-permute-done((bf16[256,256]{1,0:T(8,128)(2,1)S(1)}, bf16[256,256]{1,0:T(8,128)(2,1)S(1)}, u32[]{:S(2)}, u32[]{:S(2)}) %collective-permute-start.31) | collective-permute-done | bytes 131104 | tf_op jit(solution)/shard_map/ppermute | solution.py:20
  187.5 2.4 %collective-permute-start.23 = (bf16[2,128,512]{2,1,0:T(8,128)(2,1)}, bf16[2,128,512]{2,1,0:T(8,128)(2,1)}, u32[]{:S(2)}, u32[]{:S(2)}) collective-permute-start(bf16[2,128,512]{2,1,0:T(8,128)(2,1)} %get-tuple-element.32), channel_id=1, source_target_pairs={{0,4},{4,8},{8,12},{12,16},{16,20},{20,24},{24,28},{1,5},{5,9},{9,... | collective-permute-start | bytes 786440 | tf_op jit(solution)/shard_map/ppermute | solution.py:25
  189.9 4.3 %collective-permute-start.24 = (bf16[2,128,512]{2,1,0:T(8,128)(2,1)}, bf16[2,128,512]{2,1,0:T(8,128)(2,1)}, u32[]{:S(2)}, u32[]{:S(2)}) collective-permute-start(bf16[2,128,512]{2,1,0:T(8,128)(2,1)} %get-tuple-element.33), channel_id=1, source_target_pairs={{4,0},{8,4},{12,8},{16,12},{20,16},{24,20},{28,24},{5,1},{9,5},{13... | collective-permute-start | bytes 786440 | tf_op jit(solution)/shard_map/ppermute | solution.py:26
  195.9 4.8 %collective-permute-done.23 = bf16[2,128,512]{2,1,0:T(8,128)(2,1)} collective-permute-done((bf16[2,128,512]{2,1,0:T(8,128)(2,1)}, bf16[2,128,512]{2,1,0:T(8,128)(2,1)}, u32[]{:S(2)}, u32[]{:S(2)}) %collective-permute-start.23) | collective-permute-done | bytes 262176 | tf_op jit(solution)/shard_map/ppermute | solution.py:25
  200.7 2.9 %collective-permute-done.24 = bf16[2,128,512]{2,1,0:T(8,128)(2,1)} collective-permute-done((bf16[2,128,512]{2,1,0:T(8,128)(2,1)}, bf16[2,128,512]{2,1,0:T(8,128)(2,1)}, u32[]{:S(2)}, u32[]{:S(2)}) %collective-permute-start.24) | collective-permute-done | bytes 262176 | tf_op jit(solution)/shard_map/ppermute | solution.py:26
  203.6 3.3 %fusion.5 = f32[2,256,512]{2,1,0:T(8,128)} fusion(f32[2,512,512]{2,1,0:T(8,128)} %get-tuple-element.23, bf16[2,128,512]{2,1,0:T(8,128)(2,1)} %collective-permute-done.24, bf16[2,128,512]{2,1,0:T(8,128)(2,1)} %collective-permute-done.23, f32[2,256,512]{2,1,0:T(8,128)S(1)} %copy-done.1, bf16[2,128,512]{2,1,0:T(8,128)(2,1)} %copy-done.10, ...), kind=kLoop, calls=%fused_computation.7 | loop fusion | flops 3145728 | bytes 5242880 | tf_op jit(solution)/shard_map/add | solution.py:390
  (144 shorter events, 43.9 us)
Async XLA Ops:
  2.1 15.6 %collective-permute-start.1 = (bf16[2,128,512]{2,1,0:T(8,128)(2,1)S(1)}, bf16[2,128,512]{2,1,0:T(8,128)(2,1)S(1)}, u32[]{:S(2)}, u32[]{:S(2)}) collective-permute-start(bf16[2,128,512]{2,1,0:T(8,128)(2,1)S(1)} %get-tuple-element.54), channel_id=1, source_target_pairs={{4,0},{8,4},{12,8},{16,12},{20,16},{24,20},{28,24},{5,1},{9,5},{13... | collective-permute-start | bytes 786440 | tf_op jit(solution)/shard_map/ppermute | solution.py:26
  5.4 12.3 %collective-permute-start = (bf16[2,128,512]{2,1,0:T(8,128)(2,1)S(1)}, bf16[2,128,512]{2,1,0:T(8,128)(2,1)S(1)}, u32[]{:S(2)}, u32[]{:S(2)}) collective-permute-start(bf16[2,128,512]{2,1,0:T(8,128)(2,1)S(1)} %get-tuple-element.55), channel_id=1, source_target_pairs={{0,4},{4,8},{8,12},{12,16},{16,20},{20,24},{24,28},{1,5},{5,9},{9,... | collective-permute-start | bytes 786440 | tf_op jit(solution)/shard_map/ppermute | solution.py:25
  17.9 2.0 collective-permute-start.3
  18.0 1.9 collective-permute-start.2
  47.1 7.9 %collective-permute-start.12 = (bf16[1024,256]{1,0:T(8,128)(2,1)}, bf16[1024,256]{1,0:T(8,128)(2,1)S(1)}, u32[]{:S(2)}, u32[]{:S(2)}) collective-permute-start(bf16[1024,256]{1,0:T(8,128)(2,1)} %bitcast.34), channel_id=1, source_target_pairs={{0,1},{1,0},{2,3},{3,2},{4,5},{5,4},{6,7},{7,6},{8,9},{9,8},{10,11... | collective-permute-start | bytes 1572872 | tf_op jit(solution)/shard_map/ppermute | solution.py:20
  56.3 8.7 %collective-permute-start.13 = (bf16[512,256]{1,0:T(8,128)(2,1)S(1)}, bf16[512,256]{1,0:T(8,128)(2,1)S(1)}, u32[]{:S(2)}, u32[]{:S(2)}) collective-permute-start(bf16[512,256]{1,0:T(8,128)(2,1)S(1)} %dynamic-slice_convert_fusion.3), channel_id=1, source_target_pairs={{0,2},{1,3},{2,0},{3,1},{4,6},{5,7},{6,4},{7,5},{8,10},{9,11},{10,... | collective-permute-start | bytes 786440 | tf_op jit(solution)/shard_map/ppermute | solution.py:20
  57.8 7.6 %collective-permute-start.4 = (bf16[2,512,128]{2,1,0:T(8,128)(2,1)}, bf16[2,512,128]{2,1,0:T(8,128)(2,1)S(1)}, u32[]{:S(2)}, u32[]{:S(2)}) collective-permute-start(bf16[2,512,128]{2,1,0:T(8,128)(2,1)} %get-tuple-element.13), channel_id=1, source_target_pairs={{0,1},{1,0},{2,3},{3,2},{4,5},{5,4},{6,7},{7,6},{8,9},{9,8},{10,11... | collective-permute-start | bytes 786440 | tf_op jit(solution)/shard_map/ppermute | solution.py:36
  57.9 7.5 %collective-permute-start.5 = (bf16[2,512,128]{2,1,0:T(8,128)(2,1)S(1)}, bf16[2,512,128]{2,1,0:T(8,128)(2,1)S(1)}, u32[]{:S(2)}, u32[]{:S(2)}) collective-permute-start(bf16[2,512,128]{2,1,0:T(8,128)(2,1)S(1)} %copy-done.22), channel_id=1, source_target_pairs={{1,2},{2,1},{5,6},{6,5},{9,10},{10,9},{13,14},{14,13},{17,18},{18,... | collective-permute-start | bytes 786440 | tf_op jit(solution)/shard_map/ppermute | solution.py:35
  65.1 5.0 %collective-permute-start.14 = (bf16[256,256]{1,0:T(8,128)(2,1)S(1)}, bf16[256,256]{1,0:T(8,128)(2,1)S(1)}, u32[]{:S(2)}, u32[]{:S(2)}) collective-permute-start(bf16[256,256]{1,0:T(8,128)(2,1)S(1)} %dynamic-slice_convert_fusion.5), channel_id=1, source_target_pairs={{0,8},{4,12},{8,0},{12,4},{16,24},{20,28},{24,16},{28,20},{1,9},{5... | collective-permute-start | bytes 393224 | tf_op jit(solution)/shard_map/ppermute | solution.py:20
  70.2 5.2 %collective-permute-start.15 = (bf16[128,256]{1,0:T(8,128)(2,1)S(1)}, bf16[128,256]{1,0:T(8,128)(2,1)S(1)}, u32[]{:S(2)}, u32[]{:S(2)}) collective-permute-start(bf16[128,256]{1,0:T(8,128)(2,1)S(1)} %dynamic-slice_convert_fusion.7), channel_id=1, source_target_pairs={{0,16},{4,20},{8,24},{12,28},{16,0},{20,4},{24,8},{28,12},{1,17},{... | collective-permute-start | bytes 196616 | tf_op jit(solution)/shard_map/ppermute | solution.py:20
  75.4 10.0 %collective-permute-start.16 = (f32[128,256]{1,0:T(8,128)S(1)}, f32[128,256]{1,0:T(8,128)S(1)}, u32[]{:S(2)}, u32[]{:S(2)}) collective-permute-start(f32[128,256]{1,0:T(8,128)S(1)} %convert_add_fusion.9), channel_id=1, source_target_pairs={{0,4},{4,0},{8,12},{12,8},{16,20},{20,16},{24,28},{28,24},{1,5},{5... | collective-permute-start | bytes 393224 | tf_op jit(solution)/shard_map/ppermute | solution.py:20
  78.7 12.7 %collective-permute-start.6 = (bf16[2,128,512]{2,1,0:T(8,128)(2,1)}, bf16[2,128,512]{2,1,0:T(8,128)(2,1)S(1)}, u32[]{:S(2)}, u32[]{:S(2)}) collective-permute-start(bf16[2,128,512]{2,1,0:T(8,128)(2,1)} %get-tuple-element.34), channel_id=1, source_target_pairs={{0,4},{4,8},{8,12},{12,16},{16,20},{20,24},{24,28},{1,5},{5,9},{9,... | collective-permute-start | bytes 786440 | tf_op jit(solution)/shard_map/ppermute | solution.py:25
  80.6 11.8 %collective-permute-start.7 = (bf16[2,128,512]{2,1,0:T(8,128)(2,1)}, bf16[2,128,512]{2,1,0:T(8,128)(2,1)S(1)}, u32[]{:S(2)}, u32[]{:S(2)}) collective-permute-start(bf16[2,128,512]{2,1,0:T(8,128)(2,1)} %get-tuple-element.35), channel_id=1, source_target_pairs={{4,0},{8,4},{12,8},{16,12},{20,16},{24,20},{28,24},{5,1},{9,5},{13... | collective-permute-start | bytes 786440 | tf_op jit(solution)/shard_map/ppermute | solution.py:26
  87.1 7.0 %collective-permute-start.17 = (bf16[128,256]{1,0:T(8,128)(2,1)S(1)}, bf16[128,256]{1,0:T(8,128)(2,1)S(1)}, u32[]{:S(2)}, u32[]{:S(2)}) collective-permute-start(bf16[128,256]{1,0:T(8,128)(2,1)S(1)} %get-tuple-element.24), channel_id=1, source_target_pairs={{0,16},{4,20},{8,24},{12,28},{16,0},{20,4},{24,8},{28,12},{1,17},{... | collective-permute-start | bytes 196616 | tf_op jit(solution)/shard_map/ppermute | solution.py:20
  94.1 5.0 %collective-permute-start.18 = (bf16[256,256]{1,0:T(8,128)(2,1)S(1)}, bf16[256,256]{1,0:T(8,128)(2,1)S(1)}, u32[]{:S(2)}, u32[]{:S(2)}) collective-permute-start(bf16[256,256]{1,0:T(8,128)(2,1)S(1)} %pad_maximum_fusion.9), channel_id=1, source_target_pairs={{0,8},{4,12},{8,0},{12,4},{16,24},{20,28},{24,16},{28,20},{1,9},{5... | collective-permute-start | bytes 393224 | tf_op jit(solution)/shard_map/ppermute | solution.py:20
  94.2 9.7 %collective-permute-start.9 = (bf16[2,128,512]{2,1,0:T(8,128)(2,1)S(1)}, bf16[2,128,512]{2,1,0:T(8,128)(2,1)S(1)}, u32[]{:S(2)}, u32[]{:S(2)}) collective-permute-start(bf16[2,128,512]{2,1,0:T(8,128)(2,1)S(1)} %get-tuple-element.46), channel_id=1, source_target_pairs={{4,0},{8,4},{12,8},{16,12},{20,16},{24,20},{28,24},{5,1},{9,5},{13... | collective-permute-start | bytes 786440 | tf_op jit(solution)/shard_map/ppermute | solution.py:26
  99.2 6.4 %collective-permute-start.19 = (bf16[512,256]{1,0:T(8,128)(2,1)S(1)}, bf16[512,256]{1,0:T(8,128)(2,1)S(1)}, u32[]{:S(2)}, u32[]{:S(2)}) collective-permute-start(bf16[512,256]{1,0:T(8,128)(2,1)S(1)} %pad_maximum_fusion.7), channel_id=1, source_target_pairs={{0,2},{1,3},{2,0},{3,1},{4,6},{5,7},{6,4},{7,5},{8,10},{9,11},{10,... | collective-permute-start | bytes 786440 | tf_op jit(solution)/shard_map/ppermute | solution.py:20
  100.9 9.2 %collective-permute-start.8 = (bf16[2,128,512]{2,1,0:T(8,128)(2,1)S(1)}, bf16[2,128,512]{2,1,0:T(8,128)(2,1)S(1)}, u32[]{:S(2)}, u32[]{:S(2)}) collective-permute-start(bf16[2,128,512]{2,1,0:T(8,128)(2,1)S(1)} %get-tuple-element.47), channel_id=1, source_target_pairs={{0,4},{4,8},{8,12},{12,16},{16,20},{20,24},{24,28},{1,5},{5,9},{9,... | collective-permute-start | bytes 786440 | tf_op jit(solution)/shard_map/ppermute | solution.py:25
  106.6 5.2 %collective-permute-start.20 = (bf16[1024,256]{1,0:T(8,128)(2,1)S(1)}, bf16[1024,256]{1,0:T(8,128)(2,1)}, u32[]{:S(2)}, u32[]{:S(2)}) collective-permute-start(bf16[1024,256]{1,0:T(8,128)(2,1)S(1)} %pad_maximum_fusion.1), channel_id=1, source_target_pairs={{0,1},{1,0},{2,3},{3,2},{4,5},{5,4},{6,7},{7,6},{8,9},{9,8},{10,11... | collective-permute-start | bytes 1572872 | tf_op jit(solution)/shard_map/ppermute | solution.py:20
  139.1 8.2 %collective-permute-start.25 = (bf16[1024,256]{1,0:T(8,128)(2,1)}, bf16[1024,256]{1,0:T(8,128)(2,1)S(1)}, u32[]{:S(2)}, u32[]{:S(2)}) collective-permute-start(bf16[1024,256]{1,0:T(8,128)(2,1)} %bitcast.35), channel_id=1, source_target_pairs={{0,1},{1,0},{2,3},{3,2},{4,5},{5,4},{6,7},{7,6},{8,9},{9,8},{10,11... | collective-permute-start | bytes 1572872 | tf_op jit(solution)/shard_map/ppermute | solution.py:20
  148.7 8.7 %collective-permute-start.26 = (bf16[512,256]{1,0:T(8,128)(2,1)S(1)}, bf16[512,256]{1,0:T(8,128)(2,1)S(1)}, u32[]{:S(2)}, u32[]{:S(2)}) collective-permute-start(bf16[512,256]{1,0:T(8,128)(2,1)S(1)} %dynamic-slice_convert_fusion.2), channel_id=1, source_target_pairs={{0,2},{1,3},{2,0},{3,1},{4,6},{5,7},{6,4},{7,5},{8,10},{9,11},{10,... | collective-permute-start | bytes 786440 | tf_op jit(solution)/shard_map/ppermute | solution.py:20
  157.5 5.0 %collective-permute-start.27 = (bf16[256,256]{1,0:T(8,128)(2,1)S(1)}, bf16[256,256]{1,0:T(8,128)(2,1)S(1)}, u32[]{:S(2)}, u32[]{:S(2)}) collective-permute-start(bf16[256,256]{1,0:T(8,128)(2,1)S(1)} %dynamic-slice_convert_fusion.4), channel_id=1, source_target_pairs={{0,8},{4,12},{8,0},{12,4},{16,24},{20,28},{24,16},{28,20},{1,9},{5... | collective-permute-start | bytes 393224 | tf_op jit(solution)/shard_map/ppermute | solution.py:20
  162.6 5.3 %collective-permute-start.28 = (bf16[128,256]{1,0:T(8,128)(2,1)S(1)}, bf16[128,256]{1,0:T(8,128)(2,1)S(1)}, u32[]{:S(2)}, u32[]{:S(2)}) collective-permute-start(bf16[128,256]{1,0:T(8,128)(2,1)S(1)} %dynamic-slice_convert_fusion.6), channel_id=1, source_target_pairs={{0,16},{4,20},{8,24},{12,28},{16,0},{20,4},{24,8},{28,12},{1,17},{... | collective-permute-start | bytes 196616 | tf_op jit(solution)/shard_map/ppermute | solution.py:20
  167.8 5.0 %collective-permute-start.29 = (f32[128,256]{1,0:T(8,128)S(1)}, f32[128,256]{1,0:T(8,128)S(1)}, u32[]{:S(2)}, u32[]{:S(2)}) collective-permute-start(f32[128,256]{1,0:T(8,128)S(1)} %convert_add_fusion.8), channel_id=1, source_target_pairs={{0,4},{4,0},{8,12},{12,8},{16,20},{20,16},{24,28},{28,24},{1,5},{5... | collective-permute-start | bytes 393224 | tf_op jit(solution)/shard_map/ppermute | solution.py:20
  172.9 5.2 %collective-permute-start.30 = (bf16[128,256]{1,0:T(8,128)(2,1)S(1)}, bf16[128,256]{1,0:T(8,128)(2,1)S(1)}, u32[]{:S(2)}, u32[]{:S(2)}) collective-permute-start(bf16[128,256]{1,0:T(8,128)(2,1)S(1)} %subtract_convert_fusion), channel_id=1, source_target_pairs={{0,16},{4,20},{8,24},{12,28},{16,0},{20,4},{24,8},{28,12},{1,17},{... | collective-permute-start | bytes 196616 | tf_op jit(solution)/shard_map/ppermute | solution.py:20
  175.7 4.7 %collective-permute-start.21 = (bf16[2,512,128]{2,1,0:T(8,128)(2,1)S(1)}, bf16[2,512,128]{2,1,0:T(8,128)(2,1)S(1)}, u32[]{:S(2)}, u32[]{:S(2)}) collective-permute-start(bf16[2,512,128]{2,1,0:T(8,128)(2,1)S(1)} %copy-done.24), channel_id=1, source_target_pairs={{0,1},{1,0},{2,3},{3,2},{4,5},{5,4},{6,7},{7,6},{8,9},{9,8},{10,11... | collective-permute-start | bytes 786440 | tf_op jit(solution)/shard_map/ppermute | solution.py:36
  175.7 4.7 %collective-permute-start.22 = (bf16[2,512,128]{2,1,0:T(8,128)(2,1)S(1)}, bf16[2,512,128]{2,1,0:T(8,128)(2,1)S(1)}, u32[]{:S(2)}, u32[]{:S(2)}) collective-permute-start(bf16[2,512,128]{2,1,0:T(8,128)(2,1)S(1)} %copy-done.23), channel_id=1, source_target_pairs={{1,2},{2,1},{5,6},{6,5},{9,10},{10,9},{13,14},{14,13},{17,18},{18,... | collective-permute-start | bytes 786440 | tf_op jit(solution)/shard_map/ppermute | solution.py:35
  178.2 5.5 %collective-permute-start.31 = (bf16[256,256]{1,0:T(8,128)(2,1)S(1)}, bf16[256,256]{1,0:T(8,128)(2,1)S(1)}, u32[]{:S(2)}, u32[]{:S(2)}) collective-permute-start(bf16[256,256]{1,0:T(8,128)(2,1)S(1)} %pad_maximum_fusion.10), channel_id=1, source_target_pairs={{0,8},{4,12},{8,0},{12,4},{16,24},{20,28},{24,16},{28,20},{1,9},{5... | collective-permute-start | bytes 393224 | tf_op jit(solution)/shard_map/ppermute | solution.py:20
  183.8 10.4 %collective-permute-start.32 = (bf16[512,256]{1,0:T(8,128)(2,1)S(1)}, bf16[512,256]{1,0:T(8,128)(2,1)S(1)}, u32[]{:S(2)}, u32[]{:S(2)}) collective-permute-start(bf16[512,256]{1,0:T(8,128)(2,1)S(1)} %pad_maximum_fusion.8), channel_id=1, source_target_pairs={{0,2},{1,3},{2,0},{3,1},{4,6},{5,7},{6,4},{7,5},{8,10},{9,11},{10,... | collective-permute-start | bytes 786440 | tf_op jit(solution)/shard_map/ppermute | solution.py:20
  187.5 13.2 %collective-permute-start.23 = (bf16[2,128,512]{2,1,0:T(8,128)(2,1)}, bf16[2,128,512]{2,1,0:T(8,128)(2,1)}, u32[]{:S(2)}, u32[]{:S(2)}) collective-permute-start(bf16[2,128,512]{2,1,0:T(8,128)(2,1)} %get-tuple-element.32), channel_id=1, source_target_pairs={{0,4},{4,8},{8,12},{12,16},{16,20},{20,24},{24,28},{1,5},{5,9},{9,... | collective-permute-start | bytes 786440 | tf_op jit(solution)/shard_map/ppermute | solution.py:25
  189.9 13.7 %collective-permute-start.24 = (bf16[2,128,512]{2,1,0:T(8,128)(2,1)}, bf16[2,128,512]{2,1,0:T(8,128)(2,1)}, u32[]{:S(2)}, u32[]{:S(2)}) collective-permute-start(bf16[2,128,512]{2,1,0:T(8,128)(2,1)} %get-tuple-element.33), channel_id=1, source_target_pairs={{4,0},{8,4},{12,8},{16,12},{20,16},{24,20},{28,24},{5,1},{9,5},{13... | collective-permute-start | bytes 786440 | tf_op jit(solution)/shard_map/ppermute | solution.py:26
  195.9 11.0 %collective-permute-start.33 = (bf16[1024,256]{1,0:T(8,128)(2,1)}, bf16[1024,256]{1,0:T(8,128)(2,1)}, u32[]{:S(2)}, u32[]{:S(2)}) collective-permute-start(bf16[1024,256]{1,0:T(8,128)(2,1)} %pad_maximum_fusion.2), channel_id=1, source_target_pairs={{0,1},{1,0},{2,3},{3,2},{4,5},{5,4},{6,7},{7,6},{8,9},{9,8},{10,11... | collective-permute-start | bytes 1572872 | tf_op jit(solution)/shard_map/ppermute | solution.py:20
  (27 other events, 224.1 us)

commit v2 on v1

--- a/solution.py
+++ b/solution.py
@@ -359,6 +359,12 @@
     return values + got
 
 
+def in_order(upper, own, other):
+    place = jnp.arange(2, dtype=jnp.int32).reshape(2, 1, 1)
+    both = jnp.where(place == upper, own[None], other[None])
+    return both.reshape(2 * own.shape[0], own.shape[1])
+
+
 def own_share(values):
     for axis, bit in exchange_steps():
         values = halve(values, axis, bit)[0]
@@ -372,7 +378,7 @@
         got = swap_bit(values, axis, bit)
         if index == 0:
             return values, got
-        values = jnp.concatenate(pick(upper_of(axis, bit) == 0, values, got), axis=0)
+        values = in_order(upper_of(axis, bit), values, got)
 
 
 def fold_rims(current, grad, rim_outer, rim_inner, half):
@@ -442,8 +448,7 @@
                 part.astype(jnp.float32) + more.astype(jnp.float32)
                 for part, more in zip(parts, join_shares(rest))
             ]
-            parts = pick(upper == 0, *parts)
-            probe = jnp.concatenate(parts, axis=0).reshape(probe_modes.shape)
+            probe = in_order(upper, *parts).reshape(probe_modes.shape)
     return (current, probe)
 
 

time: 211 us -> 220 us (1.043)
  waiting for transfers between devices: 55.6 us -> 61.8 us
  local copies, waits for them, and re-layouts: 7.89 us -> 12.3 us
    ppermute x18, starting transfers between devices: 37.2 us -> 30.6 us  [swap_bit(): lax.ppermute(values, axis, [(i, i ^ bit) for i in range(lax.axis_size(axi...]
    ppermute x4, starting transfers between devices: 0.21 us -> 6.36 us  [swap_both(): inner = lax.ppermute(inner, axis, inner_pairs)]
    select_n x0 -> x8, other arithmetic: none -> 4.04 us  [in_order(): both = jnp.where(place == upper, own[None], other[None])]
    ppermute x18, waiting for transfers between devices: 41 us -> 44.5 us  [swap_bit(): lax.ppermute(values, axis, [(i, i ^ bit) for i in range(lax.axis_size(axi...]
    ppermute x4, starting transfers between devices: 16.9 us -> 13.9 us  [shift_both(): lax.ppermute(before, axis, [(target, source) for source, target in up])]
    add x0 -> x2, other arithmetic: none -> 2.75 us  [shards(): part.astype(jnp.float32) + more.astype(jnp.float32)]
    broadcast_in_dim x0 -> x9, local copies, waits for them, and re-layouts: none -> 2.39 us  [in_order(): both = jnp.where(place == upper, own[None], other[None])]
    concatenate x7 -> x0, other arithmetic: 2.38 us -> none  [the longest x1 1.46 us: shards(): probe = jnp.concatenate(parts, axis=0).reshape(probe_modes.shape)]
where the time goes in v2:
time: 220 us; the launch traced here: 219 us
  starting transfers between devices  65.5 us (30%)
  waiting for transfers between devices  61.8 us (28%)
  Pallas kernels  52.7 us (24%)
  other arithmetic  19.6 us (9%)
  local copies, waits for them, and re-layouts  12.3 us (6%)
  matrix products  5.38 us (2%)
    pallas_call x2, Pallas kernels, propagate(): pl.pallas_call(propagate_body, out_shape=outs, grid_spec=pltpu.PrefetchSc...  52.7 us
    ppermute x18, waiting for transfers between devices, swap_bit(): lax.ppermute(values, axis, [(i, i ^ bit) for i in range(lax.axis_size(axi...  44.5 us
    ppermute x18, starting transfers between devices, swap_bit(): lax.ppermute(values, axis, [(i, i ^ bit) for i in range(lax.axis_size(axi...  30.6 us
    ppermute x4, starting transfers between devices, shift_both(): lax.ppermute(before, axis, [(target, source) for source, target in up])  13.9 us
    ppermute x4, starting transfers between devices, shift_both(): previous = lax.ppermute(after, axis, up)  12 us
    ppermute x4, waiting for transfers between devices, shift_both(): previous = lax.ppermute(after, axis, up)  9.66 us
    ppermute x4, waiting for transfers between devices, shift_both(): lax.ppermute(before, axis, [(target, source) for source, target in up])  7.61 us
    ppermute x4, starting transfers between devices, swap_both(): inner = lax.ppermute(inner, axis, inner_pairs)  6.36 us
  transfers between devices with their start and end apart: 34, of which 19 were waited for; matrix products, arithmetic and copies ran while one was open for 11% of the time, Pallas kernels for 0%

profile of v2, /device:TPU:8, one launch (start us, length us, event | category | flops | bytes accessed | tf_op | source)
XLA Modules:
  0.0 218.8 jit_solution(14502213080771152888)
XLA Ops:
  2.1 3.3 %collective-permute-start.1 = (bf16[2,128,512]{2,1,0:T(8,128)(2,1)S(1)}, bf16[2,128,512]{2,1,0:T(8,128)(2,1)S(1)}, u32[]{:S(2)}, u32[]{:S(2)}) collective-permute-start(bf16[2,128,512]{2,1,0:T(8,128)(2,1)S(1)} %get-tuple-element.50), channel_id=1, source_target_pairs={{4,0},{8,4},{12,8},{16,12},{20,16},{24,20},{28,24},{5,1},{9,5},{13... | collective-permute-start | bytes 786440 | tf_op jit(solution)/shard_map/ppermute | solution.py:26
  5.4 2.6 %collective-permute-start = (bf16[2,128,512]{2,1,0:T(8,128)(2,1)S(1)}, bf16[2,128,512]{2,1,0:T(8,128)(2,1)S(1)}, u32[]{:S(2)}, u32[]{:S(2)}) collective-permute-start(bf16[2,128,512]{2,1,0:T(8,128)(2,1)S(1)} %get-tuple-element.51), channel_id=1, source_target_pairs={{0,4},{4,8},{8,12},{12,16},{16,20},{20,24},{24,28},{1,5},{5,9},{9,... | collective-permute-start | bytes 786440 | tf_op jit(solution)/shard_map/ppermute | solution.py:25
  8.0 2.7 %fusion.21 = f32[256,6,256]{2,0,1:T(8,128)S(1)} fusion(f32[256,256,1]{1,0,2:T(8,128)S(1)} %copy-done.14, f32[6,256,256]{2,1,0:T(8,128)S(1)} %copy-done), kind=kOutput, calls=%fused_computation.72 | convolution fusion | flops 1207959552 | bytes 3407872 | tf_op jit(solution)/shard_map/brc,ck->brk/dot_general | solution.py:67
  10.7 2.7 %fusion.2.amp_ref = f32[6,256,256]{2,1,0:T(8,128)} fusion(f32[256,256,1]{1,0,2:T(8,128)S(1)} %copy-done.14, f32[256,6,256]{2,0,1:T(8,128)S(1)} %fusion.21), kind=kOutput, calls=%fused_computation.4 | convolution fusion | flops 1207959552 | bytes 3407872 | tf_op jit(solution)/shard_map/rk,brc->bkc/dot_general | solution.py:71
  13.5 2.6 %dynamic-slice_convert_fusion = (bf16[1024,256]{1,0:T(8,128)(2,1)}, bf16[1024,256]{1,0:T(8,128)(2,1)}) fusion(f32[2048,256]{1,0:T(8,128)} %bitcast.63, s32[]{:T(128)S(6)} %select_n.227, s32[]{:T(128)S(6)} %select_n.226), kind=kLoop, calls=%fused_computation.13 | loop fusion | bytes 2097160 | tf_op jit(solution)/shard_map/convert_element_type | solution.py:428
  20.6 26.4 %propagate.2 = (f32[2,512,512]{2,1,0:T(8,128)}, bf16[2,512,128]{2,1,0:T(8,128)(2,1)}, bf16[2,512,128]{2,1,0:T(8,128)(2,1)}, f32[2,2,256,256]{3,2,1,0:T(8,128)}, bf16[2,2,256,256]{3,2,1,0:T(8,128)(2,1)}) custom-call(s32[6]{0:T(128)} %get-tuple-element.61.rows_ref, s32[6]{0:T(128)} %get-tuple-element.60.cols_ref, s32[2]{0:T(128)} %pad_add_fusion.flag_ref, ...), custom_call_target="tpu_custom_call" | custom-call | tf_op jit(solution)/shard_map/propagate/pallas_call | solution.py:300
  47.0 6.2 %collective-permute-start.4 = (bf16[2,512,128]{2,1,0:T(8,128)(2,1)}, bf16[2,512,128]{2,1,0:T(8,128)(2,1)S(1)}, u32[]{:S(2)}, u32[]{:S(2)}) collective-permute-start(bf16[2,512,128]{2,1,0:T(8,128)(2,1)} %get-tuple-element.13), channel_id=1, source_target_pairs={{0,1},{1,0},{2,3},{3,2},{4,5},{5,4},{6,7},{7,6},{8,9},{9,8},{10,11... | collective-permute-start | bytes 786440 | tf_op jit(solution)/shard_map/ppermute | solution.py:36
  53.9 2.5 %collective-permute-start.12 = (bf16[1024,256]{1,0:T(8,128)(2,1)}, bf16[1024,256]{1,0:T(8,128)(2,1)S(1)}, u32[]{:S(2)}, u32[]{:S(2)}) collective-permute-start(bf16[1024,256]{1,0:T(8,128)(2,1)} %bitcast.65), channel_id=1, source_target_pairs={{0,1},{1,0},{2,3},{3,2},{4,5},{5,4},{6,7},{7,6},{8,9},{9,8},{10,11... | collective-permute-start | bytes 1572872 | tf_op jit(solution)/shard_map/ppermute | solution.py:20
  59.5 4.2 %collective-permute-start.13 = (bf16[512,256]{1,0:T(8,128)(2,1)S(1)}, bf16[512,256]{1,0:T(8,128)(2,1)S(1)}, u32[]{:S(2)}, u32[]{:S(2)}) collective-permute-start(bf16[512,256]{1,0:T(8,128)(2,1)S(1)} %dynamic-slice_convert_fusion.3), channel_id=1, source_target_pairs={{0,2},{1,3},{2,0},{3,1},{4,6},{5,7},{6,4},{7,5},{8,10},{9,11},{10,... | collective-permute-start | bytes 786440 | tf_op jit(solution)/shard_map/ppermute | solution.py:20
  64.1 6.7 %collective-permute-done.13 = bf16[512,256]{1,0:T(8,128)(2,1)S(1)} collective-permute-done((bf16[512,256]{1,0:T(8,128)(2,1)S(1)}, bf16[512,256]{1,0:T(8,128)(2,1)S(1)}, u32[]{:S(2)}, u32[]{:S(2)}) %collective-permute-start.13) | collective-permute-done | bytes 262176 | tf_op jit(solution)/shard_map/ppermute | solution.py:20
  71.3 4.4 %collective-permute-start.6 = (bf16[2,128,512]{2,1,0:T(8,128)(2,1)S(1)}, bf16[2,128,512]{2,1,0:T(8,128)(2,1)S(1)}, u32[]{:S(2)}, u32[]{:S(2)}) collective-permute-start(bf16[2,128,512]{2,1,0:T(8,128)(2,1)S(1)} %get-tuple-element.34), channel_id=1, source_target_pairs={{0,4},{4,8},{8,12},{12,16},{16,20},{20,24},{24,28},{1,5},{5,9},{9,... | collective-permute-start | bytes 786440 | tf_op jit(solution)/shard_map/ppermute | solution.py:25
  75.7 2.9 %collective-permute-start.7 = (bf16[2,128,512]{2,1,0:T(8,128)(2,1)S(1)}, bf16[2,128,512]{2,1,0:T(8,128)(2,1)S(1)}, u32[]{:S(2)}, u32[]{:S(2)}) collective-permute-start(bf16[2,128,512]{2,1,0:T(8,128)(2,1)S(1)} %get-tuple-element.35), channel_id=1, source_target_pairs={{4,0},{8,4},{12,8},{16,12},{20,16},{24,20},{28,24},{5,1},{9,5},{13... | collective-permute-start | bytes 786440 | tf_op jit(solution)/shard_map/ppermute | solution.py:26
  80.9 5.0 %collective-permute-done.6 = bf16[2,128,512]{2,1,0:T(8,128)(2,1)S(1)} collective-permute-done((bf16[2,128,512]{2,1,0:T(8,128)(2,1)S(1)}, bf16[2,128,512]{2,1,0:T(8,128)(2,1)S(1)}, u32[]{:S(2)}, u32[]{:S(2)}) %collective-permute-start.6) | collective-permute-done | bytes 262176 | tf_op jit(solution)/shard_map/ppermute | solution.py:25
  85.9 3.6 %collective-permute-done.7 = bf16[2,128,512]{2,1,0:T(8,128)(2,1)S(1)} collective-permute-done((bf16[2,128,512]{2,1,0:T(8,128)(2,1)S(1)}, bf16[2,128,512]{2,1,0:T(8,128)(2,1)S(1)}, u32[]{:S(2)}, u32[]{:S(2)}) %collective-permute-start.7) | collective-permute-done | bytes 262176 | tf_op jit(solution)/shard_map/ppermute | solution.py:26
  91.5 3.7 %collective-permute-start.9 = (bf16[2,128,512]{2,1,0:T(8,128)(2,1)}, bf16[2,128,512]{2,1,0:T(8,128)(2,1)}, u32[]{:S(2)}, u32[]{:S(2)}) collective-permute-start(bf16[2,128,512]{2,1,0:T(8,128)(2,1)} %get-tuple-element.42), channel_id=1, source_target_pairs={{4,0},{8,4},{12,8},{16,12},{20,16},{24,20},{28,24},{5,1},{9,5},{13... | collective-permute-start | bytes 786440 | tf_op jit(solution)/shard_map/ppermute | solution.py:26
  100.2 2.3 %collective-permute-start.8 = (bf16[2,128,512]{2,1,0:T(8,128)(2,1)}, bf16[2,128,512]{2,1,0:T(8,128)(2,1)S(1)}, u32[]{:S(2)}, u32[]{:S(2)}) collective-permute-start(bf16[2,128,512]{2,1,0:T(8,128)(2,1)} %get-tuple-element.43), channel_id=1, source_target_pairs={{0,4},{4,8},{8,12},{12,16},{16,20},{20,24},{24,28},{1,5},{5,9},{9,... | collective-permute-start | bytes 786440 | tf_op jit(solution)/shard_map/ppermute | solution.py:25
  106.7 2.9 %collective-permute-done.18 = bf16[256,256]{1,0:T(8,128)(2,1)S(1)} collective-permute-done((bf16[256,256]{1,0:T(8,128)(2,1)S(1)}, bf16[256,256]{1,0:T(8,128)(2,1)S(1)}, u32[]{:S(2)}, u32[]{:S(2)}) %collective-permute-start.18) | collective-permute-done | bytes 131104 | tf_op jit(solution)/shard_map/ppermute | solution.py:20
  112.8 4.1 %collective-permute-done.19 = bf16[512,256]{1,0:T(8,128)(2,1)S(1)} collective-permute-done((bf16[512,256]{1,0:T(8,128)(2,1)S(1)}, bf16[512,256]{1,0:T(8,128)(2,1)S(1)}, u32[]{:S(2)}, u32[]{:S(2)}) %collective-permute-start.19) | collective-permute-done | bytes 262176 | tf_op jit(solution)/shard_map/ppermute | solution.py:20
  120.8 26.4 %propagate.3 = (f32[2,512,512]{2,1,0:T(8,128)}, bf16[2,512,128]{2,1,0:T(8,128)(2,1)}, bf16[2,512,128]{2,1,0:T(8,128)(2,1)}, f32[2,2,256,256]{3,2,1,0:T(8,128)}, bf16[2,2,256,256]{3,2,1,0:T(8,128)(2,1)}) custom-call(s32[6]{0:T(128)} %get-tuple-element.61.rows_ref, s32[6]{0:T(128)} %get-tuple-element.60.cols_ref, s32[2]{0:T(128)} %pad_add_fusion.flag_ref, ...), custom_call_target="tpu_custom_call" | custom-call | tf_op jit(solution)/shard_map/propagate/pallas_call | solution.py:300
  147.1 6.4 %collective-permute-start.25 = (bf16[1024,256]{1,0:T(8,128)(2,1)}, bf16[1024,256]{1,0:T(8,128)(2,1)S(1)}, u32[]{:S(2)}, u32[]{:S(2)}) collective-permute-start(bf16[1024,256]{1,0:T(8,128)(2,1)} %bitcast.66), channel_id=1, source_target_pairs={{0,1},{1,0},{2,3},{3,2},{4,5},{5,4},{6,7},{7,6},{8,9},{9,8},{10,11... | collective-permute-start | bytes 1572872 | tf_op jit(solution)/shard_map/ppermute | solution.py:20
  157.0 8.3 %collective-permute-done.26 = bf16[512,256]{1,0:T(8,128)(2,1)S(1)} collective-permute-done((bf16[512,256]{1,0:T(8,128)(2,1)S(1)}, bf16[512,256]{1,0:T(8,128)(2,1)S(1)}, u32[]{:S(2)}, u32[]{:S(2)}) %collective-permute-start.26) | collective-permute-done | bytes 262176 | tf_op jit(solution)/shard_map/ppermute | solution.py:20
  167.5 3.2 %collective-permute-done.27 = bf16[256,256]{1,0:T(8,128)(2,1)S(1)} collective-permute-done((bf16[256,256]{1,0:T(8,128)(2,1)S(1)}, bf16[256,256]{1,0:T(8,128)(2,1)S(1)}, u32[]{:S(2)}, u32[]{:S(2)}) %collective-permute-start.27) | collective-permute-done | bytes 131104 | tf_op jit(solution)/shard_map/ppermute | solution.py:20
  170.8 5.2 %collective-permute-done.28 = bf16[128,256]{1,0:T(8,128)(2,1)S(1)} collective-permute-done((bf16[128,256]{1,0:T(8,128)(2,1)S(1)}, bf16[128,256]{1,0:T(8,128)(2,1)S(1)}, u32[]{:S(2)}, u32[]{:S(2)}) %collective-permute-start.28) | collective-permute-done | bytes 65568 | tf_op jit(solution)/shard_map/ppermute | solution.py:20
  176.0 4.1 %collective-permute-start.29 = (f32[128,256]{1,0:T(8,128)S(1)}, f32[128,256]{1,0:T(8,128)S(1)}, u32[]{:S(2)}, u32[]{:S(2)}) collective-permute-start(f32[128,256]{1,0:T(8,128)S(1)} %convert_add_fusion.8), channel_id=1, source_target_pairs={{0,4},{4,0},{8,12},{12,8},{16,20},{20,16},{24,28},{28,24},{1,5},{5... | collective-permute-start | bytes 393224 | tf_op jit(solution)/shard_map/ppermute | solution.py:20
  180.8 2.3 %collective-permute-done.29 = f32[128,256]{1,0:T(8,128)S(1)} collective-permute-done((f32[128,256]{1,0:T(8,128)S(1)}, f32[128,256]{1,0:T(8,128)S(1)}, u32[]{:S(2)}, u32[]{:S(2)}) %collective-permute-start.29) | collective-permute-done | bytes 131104 | tf_op jit(solution)/shard_map/ppermute | solution.py:20
  184.9 3.5 %collective-permute-done.30 = bf16[128,256]{1,0:T(8,128)(2,1)S(1)} collective-permute-done((bf16[128,256]{1,0:T(8,128)(2,1)S(1)}, bf16[128,256]{1,0:T(8,128)(2,1)S(1)}, u32[]{:S(2)}, u32[]{:S(2)}) %collective-permute-start.30) | collective-permute-done | bytes 65568 | tf_op jit(solution)/shard_map/ppermute | solution.py:20
  190.9 3.2 %collective-permute-done.31 = bf16[256,256]{1,0:T(8,128)(2,1)S(1)} collective-permute-done((bf16[256,256]{1,0:T(8,128)(2,1)S(1)}, bf16[256,256]{1,0:T(8,128)(2,1)S(1)}, u32[]{:S(2)}, u32[]{:S(2)}) %collective-permute-start.31) | collective-permute-done | bytes 131104 | tf_op jit(solution)/shard_map/ppermute | solution.py:20
  196.3 2.8 %collective-permute-start.23 = (bf16[2,128,512]{2,1,0:T(8,128)(2,1)}, bf16[2,128,512]{2,1,0:T(8,128)(2,1)S(1)}, u32[]{:S(2)}, u32[]{:S(2)}) collective-permute-start(bf16[2,128,512]{2,1,0:T(8,128)(2,1)} %get-tuple-element.32), channel_id=1, source_target_pairs={{0,4},{4,8},{8,12},{12,16},{16,20},{20,24},{24,28},{1,5},{5,9},{9,... | collective-permute-start | bytes 786440 | tf_op jit(solution)/shard_map/ppermute | solution.py:25
  199.1 4.0 %collective-permute-start.24 = (bf16[2,128,512]{2,1,0:T(8,128)(2,1)}, bf16[2,128,512]{2,1,0:T(8,128)(2,1)}, u32[]{:S(2)}, u32[]{:S(2)}) collective-permute-start(bf16[2,128,512]{2,1,0:T(8,128)(2,1)} %get-tuple-element.33), channel_id=1, source_target_pairs={{4,0},{8,4},{12,8},{16,12},{20,16},{24,20},{28,24},{5,1},{9,5},{13... | collective-permute-start | bytes 786440 | tf_op jit(solution)/shard_map/ppermute | solution.py:26
  204.9 4.0 %collective-permute-done.23 = bf16[2,128,512]{2,1,0:T(8,128)(2,1)S(1)} collective-permute-done((bf16[2,128,512]{2,1,0:T(8,128)(2,1)}, bf16[2,128,512]{2,1,0:T(8,128)(2,1)S(1)}, u32[]{:S(2)}, u32[]{:S(2)}) %collective-permute-start.23) | collective-permute-done | bytes 262176 | tf_op jit(solution)/shard_map/ppermute | solution.py:25
  208.9 2.5 %collective-permute-done.24 = bf16[2,128,512]{2,1,0:T(8,128)(2,1)} collective-permute-done((bf16[2,128,512]{2,1,0:T(8,128)(2,1)}, bf16[2,128,512]{2,1,0:T(8,128)(2,1)}, u32[]{:S(2)}, u32[]{:S(2)}) %collective-permute-start.24) | collective-permute-done | bytes 262176 | tf_op jit(solution)/shard_map/ppermute | solution.py:26
  211.4 3.1 %fusion.5 = f32[2,256,512]{2,1,0:T(8,128)} fusion(f32[2,512,512]{2,1,0:T(8,128)} %get-tuple-element.25, bf16[2,128,512]{2,1,0:T(8,128)(2,1)} %collective-permute-done.24, bf16[2,128,512]{2,1,0:T(8,128)(2,1)S(1)} %collective-permute-done.23, f32[2,256,512]{2,1,0:T(8,128)S(1)} %copy-done.1, bf16[2,128,512]{2,1,0:T(8,128)(2,1)S(1)} %copy-done.13, ...), kind=kLoop, calls=%fused_computation.6 | loop fusion | flops 3145728 | bytes 5242880 | tf_op jit(solution)/shard_map/add | solution.py:396
  (165 shorter events, 50.0 us)
Async XLA Ops:
  2.1 15.6 %collective-permute-start.1 = (bf16[2,128,512]{2,1,0:T(8,128)(2,1)S(1)}, bf16[2,128,512]{2,1,0:T(8,128)(2,1)S(1)}, u32[]{:S(2)}, u32[]{:S(2)}) collective-permute-start(bf16[2,128,512]{2,1,0:T(8,128)(2,1)S(1)} %get-tuple-element.50), channel_id=1, source_target_pairs={{4,0},{8,4},{12,8},{16,12},{20,16},{24,20},{28,24},{5,1},{9,5},{13... | collective-permute-start | bytes 786440 | tf_op jit(solution)/shard_map/ppermute | solution.py:26
  5.4 12.3 %collective-permute-start = (bf16[2,128,512]{2,1,0:T(8,128)(2,1)S(1)}, bf16[2,128,512]{2,1,0:T(8,128)(2,1)S(1)}, u32[]{:S(2)}, u32[]{:S(2)}) collective-permute-start(bf16[2,128,512]{2,1,0:T(8,128)(2,1)S(1)} %get-tuple-element.51), channel_id=1, source_target_pairs={{0,4},{4,8},{8,12},{12,16},{16,20},{20,24},{24,28},{1,5},{5,9},{9,... | collective-permute-start | bytes 786440 | tf_op jit(solution)/shard_map/ppermute | solution.py:25
  17.9 1.9 collective-permute-start.3
  18.0 1.8 collective-permute-start.2
  47.0 9.5 %collective-permute-start.4 = (bf16[2,512,128]{2,1,0:T(8,128)(2,1)}, bf16[2,512,128]{2,1,0:T(8,128)(2,1)S(1)}, u32[]{:S(2)}, u32[]{:S(2)}) collective-permute-start(bf16[2,512,128]{2,1,0:T(8,128)(2,1)} %get-tuple-element.13), channel_id=1, source_target_pairs={{0,1},{1,0},{2,3},{3,2},{4,5},{5,4},{6,7},{7,6},{8,9},{9,8},{10,11... | collective-permute-start | bytes 786440 | tf_op jit(solution)/shard_map/ppermute | solution.py:36
  53.2 3.2 %collective-permute-start.5 = (bf16[2,512,128]{2,1,0:T(8,128)(2,1)}, bf16[2,512,128]{2,1,0:T(8,128)(2,1)S(1)}, u32[]{:S(2)}, u32[]{:S(2)}) collective-permute-start(bf16[2,512,128]{2,1,0:T(8,128)(2,1)} %get-tuple-element.14), channel_id=1, source_target_pairs={{1,2},{2,1},{5,6},{6,5},{9,10},{10,9},{13,14},{14,13},{17,18},{18,... | collective-permute-start | bytes 786440 | tf_op jit(solution)/shard_map/ppermute | solution.py:35
  53.9 4.2 %collective-permute-start.12 = (bf16[1024,256]{1,0:T(8,128)(2,1)}, bf16[1024,256]{1,0:T(8,128)(2,1)S(1)}, u32[]{:S(2)}, u32[]{:S(2)}) collective-permute-start(bf16[1024,256]{1,0:T(8,128)(2,1)} %bitcast.65), channel_id=1, source_target_pairs={{0,1},{1,0},{2,3},{3,2},{4,5},{5,4},{6,7},{7,6},{8,9},{9,8},{10,11... | collective-permute-start | bytes 1572872 | tf_op jit(solution)/shard_map/ppermute | solution.py:20
  59.5 11.3 %collective-permute-start.13 = (bf16[512,256]{1,0:T(8,128)(2,1)S(1)}, bf16[512,256]{1,0:T(8,128)(2,1)S(1)}, u32[]{:S(2)}, u32[]{:S(2)}) collective-permute-start(bf16[512,256]{1,0:T(8,128)(2,1)S(1)} %dynamic-slice_convert_fusion.3), channel_id=1, source_target_pairs={{0,2},{1,3},{2,0},{3,1},{4,6},{5,7},{6,4},{7,5},{8,10},{9,11},{10,... | collective-permute-start | bytes 786440 | tf_op jit(solution)/shard_map/ppermute | solution.py:20
  70.9 7.7 %collective-permute-start.14 = (bf16[256,256]{1,0:T(8,128)(2,1)S(1)}, bf16[256,256]{1,0:T(8,128)(2,1)S(1)}, u32[]{:S(2)}, u32[]{:S(2)}) collective-permute-start(bf16[256,256]{1,0:T(8,128)(2,1)S(1)} %dynamic-slice_convert_fusion.5), channel_id=1, source_target_pairs={{0,8},{4,12},{8,0},{12,4},{16,24},{20,28},{24,16},{28,20},{1,9},{5... | collective-permute-start | bytes 393224 | tf_op jit(solution)/shard_map/ppermute | solution.py:20
  71.3 14.6 %collective-permute-start.6 = (bf16[2,128,512]{2,1,0:T(8,128)(2,1)S(1)}, bf16[2,128,512]{2,1,0:T(8,128)(2,1)S(1)}, u32[]{:S(2)}, u32[]{:S(2)}) collective-permute-start(bf16[2,128,512]{2,1,0:T(8,128)(2,1)S(1)} %get-tuple-element.34), channel_id=1, source_target_pairs={{0,4},{4,8},{8,12},{12,16},{16,20},{20,24},{24,28},{1,5},{5,9},{9,... | collective-permute-start | bytes 786440 | tf_op jit(solution)/shard_map/ppermute | solution.py:25
  75.7 13.8 %collective-permute-start.7 = (bf16[2,128,512]{2,1,0:T(8,128)(2,1)S(1)}, bf16[2,128,512]{2,1,0:T(8,128)(2,1)S(1)}, u32[]{:S(2)}, u32[]{:S(2)}) collective-permute-start(bf16[2,128,512]{2,1,0:T(8,128)(2,1)S(1)} %get-tuple-element.35), channel_id=1, source_target_pairs={{4,0},{8,4},{12,8},{16,12},{20,16},{24,20},{28,24},{5,1},{9,5},{13... | collective-permute-start | bytes 786440 | tf_op jit(solution)/shard_map/ppermute | solution.py:26
  78.7 11.1 %collective-permute-start.15 = (bf16[128,256]{1,0:T(8,128)(2,1)S(1)}, bf16[128,256]{1,0:T(8,128)(2,1)S(1)}, u32[]{:S(2)}, u32[]{:S(2)}) collective-permute-start(bf16[128,256]{1,0:T(8,128)(2,1)S(1)} %dynamic-slice_convert_fusion.7), channel_id=1, source_target_pairs={{0,16},{4,20},{8,24},{12,28},{16,0},{20,4},{24,8},{28,12},{1,17},{... | collective-permute-start | bytes 196616 | tf_op jit(solution)/shard_map/ppermute | solution.py:20
  89.8 5.5 %collective-permute-start.16 = (f32[128,256]{1,0:T(8,128)S(1)}, f32[128,256]{1,0:T(8,128)S(1)}, u32[]{:S(2)}, u32[]{:S(2)}) collective-permute-start(f32[128,256]{1,0:T(8,128)S(1)} %convert_add_fusion.9), channel_id=1, source_target_pairs={{0,4},{4,0},{8,12},{12,8},{16,20},{20,16},{24,28},{28,24},{1,5},{5... | collective-permute-start | bytes 393224 | tf_op jit(solution)/shard_map/ppermute | solution.py:20
  91.5 19.0 %collective-permute-start.9 = (bf16[2,128,512]{2,1,0:T(8,128)(2,1)}, bf16[2,128,512]{2,1,0:T(8,128)(2,1)}, u32[]{:S(2)}, u32[]{:S(2)}) collective-permute-start(bf16[2,128,512]{2,1,0:T(8,128)(2,1)} %get-tuple-element.42), channel_id=1, source_target_pairs={{4,0},{8,4},{12,8},{16,12},{20,16},{24,20},{28,24},{5,1},{9,5},{13... | collective-permute-start | bytes 786440 | tf_op jit(solution)/shard_map/ppermute | solution.py:26
  96.9 7.4 %collective-permute-start.17 = (bf16[128,256]{1,0:T(8,128)(2,1)S(1)}, bf16[128,256]{1,0:T(8,128)(2,1)S(1)}, u32[]{:S(2)}, u32[]{:S(2)}) collective-permute-start(bf16[128,256]{1,0:T(8,128)(2,1)S(1)} %get-tuple-element.26), channel_id=1, source_target_pairs={{0,16},{4,20},{8,24},{12,28},{16,0},{20,4},{24,8},{28,12},{1,17},{... | collective-permute-start | bytes 196616 | tf_op jit(solution)/shard_map/ppermute | solution.py:20
  100.2 11.8 %collective-permute-start.8 = (bf16[2,128,512]{2,1,0:T(8,128)(2,1)}, bf16[2,128,512]{2,1,0:T(8,128)(2,1)S(1)}, u32[]{:S(2)}, u32[]{:S(2)}) collective-permute-start(bf16[2,128,512]{2,1,0:T(8,128)(2,1)} %get-tuple-element.43), channel_id=1, source_target_pairs={{0,4},{4,8},{8,12},{12,16},{16,20},{20,24},{24,28},{1,5},{5,9},{9,... | collective-permute-start | bytes 786440 | tf_op jit(solution)/shard_map/ppermute | solution.py:25
  104.5 5.2 %collective-permute-start.18 = (bf16[256,256]{1,0:T(8,128)(2,1)S(1)}, bf16[256,256]{1,0:T(8,128)(2,1)S(1)}, u32[]{:S(2)}, u32[]{:S(2)}) collective-permute-start(bf16[256,256]{1,0:T(8,128)(2,1)S(1)} %bitcast_select_fusion.5), channel_id=1, source_target_pairs={{0,8},{4,12},{8,0},{12,4},{16,24},{20,28},{24,16},{28,20},{1,9},{5... | collective-permute-start | bytes 393224 | tf_op jit(solution)/shard_map/ppermute | solution.py:20
  110.4 6.4 %collective-permute-start.19 = (bf16[512,256]{1,0:T(8,128)(2,1)S(1)}, bf16[512,256]{1,0:T(8,128)(2,1)S(1)}, u32[]{:S(2)}, u32[]{:S(2)}) collective-permute-start(bf16[512,256]{1,0:T(8,128)(2,1)S(1)} %bitcast_select_fusion.3), channel_id=1, source_target_pairs={{0,2},{1,3},{2,0},{3,1},{4,6},{5,7},{6,4},{7,5},{8,10},{9,11},{10,... | collective-permute-start | bytes 786440 | tf_op jit(solution)/shard_map/ppermute | solution.py:20
  117.1 2.7 %collective-permute-start.20 = (bf16[1024,256]{1,0:T(8,128)(2,1)S(1)}, bf16[1024,256]{1,0:T(8,128)(2,1)S(1)}, u32[]{:S(2)}, u32[]{:S(2)}) collective-permute-start(bf16[1024,256]{1,0:T(8,128)(2,1)S(1)} %bitcast_select_fusion.1), channel_id=1, source_target_pairs={{0,1},{1,0},{2,3},{3,2},{4,5},{5,4},{6,7},{7,6},{8,9},{9,8},{10,11... | collective-permute-start | bytes 1572872 | tf_op jit(solution)/shard_map/ppermute | solution.py:20
  147.1 8.1 %collective-permute-start.25 = (bf16[1024,256]{1,0:T(8,128)(2,1)}, bf16[1024,256]{1,0:T(8,128)(2,1)S(1)}, u32[]{:S(2)}, u32[]{:S(2)}) collective-permute-start(bf16[1024,256]{1,0:T(8,128)(2,1)} %bitcast.66), channel_id=1, source_target_pairs={{0,1},{1,0},{2,3},{3,2},{4,5},{5,4},{6,7},{7,6},{8,9},{9,8},{10,11... | collective-permute-start | bytes 1572872 | tf_op jit(solution)/shard_map/ppermute | solution.py:20
  156.7 8.7 %collective-permute-start.26 = (bf16[512,256]{1,0:T(8,128)(2,1)S(1)}, bf16[512,256]{1,0:T(8,128)(2,1)S(1)}, u32[]{:S(2)}, u32[]{:S(2)}) collective-permute-start(bf16[512,256]{1,0:T(8,128)(2,1)S(1)} %dynamic-slice_convert_fusion.2), channel_id=1, source_target_pairs={{0,2},{1,3},{2,0},{3,1},{4,6},{5,7},{6,4},{7,5},{8,10},{9,11},{10,... | collective-permute-start | bytes 786440 | tf_op jit(solution)/shard_map/ppermute | solution.py:20
  165.4 5.3 %collective-permute-start.27 = (bf16[256,256]{1,0:T(8,128)(2,1)S(1)}, bf16[256,256]{1,0:T(8,128)(2,1)S(1)}, u32[]{:S(2)}, u32[]{:S(2)}) collective-permute-start(bf16[256,256]{1,0:T(8,128)(2,1)S(1)} %dynamic-slice_convert_fusion.4), channel_id=1, source_target_pairs={{0,8},{4,12},{8,0},{12,4},{16,24},{20,28},{24,16},{28,20},{1,9},{5... | collective-permute-start | bytes 393224 | tf_op jit(solution)/shard_map/ppermute | solution.py:20
  170.7 5.3 %collective-permute-start.28 = (bf16[128,256]{1,0:T(8,128)(2,1)S(1)}, bf16[128,256]{1,0:T(8,128)(2,1)S(1)}, u32[]{:S(2)}, u32[]{:S(2)}) collective-permute-start(bf16[128,256]{1,0:T(8,128)(2,1)S(1)} %dynamic-slice_convert_fusion.6), channel_id=1, source_target_pairs={{0,16},{4,20},{8,24},{12,28},{16,0},{20,4},{24,8},{28,12},{1,17},{... | collective-permute-start | bytes 196616 | tf_op jit(solution)/shard_map/ppermute | solution.py:20
  176.0 7.1 %collective-permute-start.29 = (f32[128,256]{1,0:T(8,128)S(1)}, f32[128,256]{1,0:T(8,128)S(1)}, u32[]{:S(2)}, u32[]{:S(2)}) collective-permute-start(f32[128,256]{1,0:T(8,128)S(1)} %convert_add_fusion.8), channel_id=1, source_target_pairs={{0,4},{4,0},{8,12},{12,8},{16,20},{20,16},{24,28},{28,24},{1,5},{5... | collective-permute-start | bytes 393224 | tf_op jit(solution)/shard_map/ppermute | solution.py:20
  180.1 4.7 %collective-permute-start.21 = (bf16[2,512,128]{2,1,0:T(8,128)(2,1)S(1)}, bf16[2,512,128]{2,1,0:T(8,128)(2,1)S(1)}, u32[]{:S(2)}, u32[]{:S(2)}) collective-permute-start(bf16[2,512,128]{2,1,0:T(8,128)(2,1)S(1)} %copy-done.30), channel_id=1, source_target_pairs={{0,1},{1,0},{2,3},{3,2},{4,5},{5,4},{6,7},{7,6},{8,9},{9,8},{10,11... | collective-permute-start | bytes 786440 | tf_op jit(solution)/shard_map/ppermute | solution.py:36
  180.2 4.7 %collective-permute-start.22 = (bf16[2,512,128]{2,1,0:T(8,128)(2,1)S(1)}, bf16[2,512,128]{2,1,0:T(8,128)(2,1)S(1)}, u32[]{:S(2)}, u32[]{:S(2)}) collective-permute-start(bf16[2,512,128]{2,1,0:T(8,128)(2,1)S(1)} %copy-done.29), channel_id=1, source_target_pairs={{1,2},{2,1},{5,6},{6,5},{9,10},{10,9},{13,14},{14,13},{17,18},{18,... | collective-permute-start | bytes 786440 | tf_op jit(solution)/shard_map/ppermute | solution.py:35
  183.1 5.2 %collective-permute-start.30 = (bf16[128,256]{1,0:T(8,128)(2,1)S(1)}, bf16[128,256]{1,0:T(8,128)(2,1)S(1)}, u32[]{:S(2)}, u32[]{:S(2)}) collective-permute-start(bf16[128,256]{1,0:T(8,128)(2,1)S(1)} %subtract_convert_fusion), channel_id=1, source_target_pairs={{0,16},{4,20},{8,24},{12,28},{16,0},{20,4},{24,8},{28,12},{1,17},{... | collective-permute-start | bytes 196616 | tf_op jit(solution)/shard_map/ppermute | solution.py:20
  188.5 5.6 %collective-permute-start.31 = (bf16[256,256]{1,0:T(8,128)(2,1)S(1)}, bf16[256,256]{1,0:T(8,128)(2,1)S(1)}, u32[]{:S(2)}, u32[]{:S(2)}) collective-permute-start(bf16[256,256]{1,0:T(8,128)(2,1)S(1)} %bitcast_select_fusion.4), channel_id=1, source_target_pairs={{0,8},{4,12},{8,0},{12,4},{16,24},{20,28},{24,16},{28,20},{1,9},{5... | collective-permute-start | bytes 393224 | tf_op jit(solution)/shard_map/ppermute | solution.py:20
  194.3 8.8 %collective-permute-start.32 = (bf16[512,256]{1,0:T(8,128)(2,1)S(1)}, bf16[512,256]{1,0:T(8,128)(2,1)S(1)}, u32[]{:S(2)}, u32[]{:S(2)}) collective-permute-start(bf16[512,256]{1,0:T(8,128)(2,1)S(1)} %bitcast_select_fusion.2), channel_id=1, source_target_pairs={{0,2},{1,3},{2,0},{3,1},{4,6},{5,7},{6,4},{7,5},{8,10},{9,11},{10,... | collective-permute-start | bytes 786440 | tf_op jit(solution)/shard_map/ppermute | solution.py:20
  196.3 12.6 %collective-permute-start.23 = (bf16[2,128,512]{2,1,0:T(8,128)(2,1)}, bf16[2,128,512]{2,1,0:T(8,128)(2,1)S(1)}, u32[]{:S(2)}, u32[]{:S(2)}) collective-permute-start(bf16[2,128,512]{2,1,0:T(8,128)(2,1)} %get-tuple-element.32), channel_id=1, source_target_pairs={{0,4},{4,8},{8,12},{12,16},{16,20},{20,24},{24,28},{1,5},{5,9},{9,... | collective-permute-start | bytes 786440 | tf_op jit(solution)/shard_map/ppermute | solution.py:25
  199.1 12.3 %collective-permute-start.24 = (bf16[2,128,512]{2,1,0:T(8,128)(2,1)}, bf16[2,128,512]{2,1,0:T(8,128)(2,1)}, u32[]{:S(2)}, u32[]{:S(2)}) collective-permute-start(bf16[2,128,512]{2,1,0:T(8,128)(2,1)} %get-tuple-element.33), channel_id=1, source_target_pairs={{4,0},{8,4},{12,8},{16,12},{20,16},{24,20},{28,24},{5,1},{9,5},{13... | collective-permute-start | bytes 786440 | tf_op jit(solution)/shard_map/ppermute | solution.py:26
  204.7 9.8 %collective-permute-start.33 = (bf16[1024,256]{1,0:T(8,128)(2,1)}, bf16[1024,256]{1,0:T(8,128)(2,1)}, u32[]{:S(2)}, u32[]{:S(2)}) collective-permute-start(bf16[1024,256]{1,0:T(8,128)(2,1)} %get-tuple-element.23), channel_id=1, source_target_pairs={{0,1},{1,0},{2,3},{3,2},{4,5},{5,4},{6,7},{7,6},{8,9},{9,8},{10,11... | collective-permute-start | bytes 1572872 | tf_op jit(solution)/shard_map/ppermute | solution.py:20
  (33 other events, 399.7 us)

commit v3 on v2

--- a/solution.py
+++ b/solution.py
@@ -78,190 +78,235 @@
     return jnp.dot(left, right, preferred_element_type=jnp.float32)
 
 
+def take_patch(ext_ref, patch_ref, row, col):
+    side = patch_ref.shape[1]
+    width = side // LANES
+    tile0 = col // LANES
+    lane0 = col % LANES
+    shift = (LANES - lane0) % LANES
+    lane = lax.broadcasted_iota(jnp.int32, (side, LANES), 1)
+    inside = lane < LANES - lane0
+    for part in range(2):
+        rolled = [
+            pltpu.roll(ext_ref[part, tile0 + j, pl.ds(row, side), :], shift, 1)
+            for j in range(width + 1)
+        ]
+        for j in range(width):
+            patch_ref[part, :, j * LANES : (j + 1) * LANES] = jnp.where(
+                inside, rolled[j], rolled[j + 1]
+            )
+
+
+def add_window(acc_ref, window_ref, row, col, scale):
+    side = window_ref.shape[1]
+    width = side // LANES
+    tile0 = col // LANES
+    lane0 = col % LANES
+    lane = lax.broadcasted_iota(jnp.int32, (side, LANES), 1)
+    inside = lane >= lane0
+    zero = jnp.zeros((side, LANES), jnp.float32)
+    for part in range(2):
+        rolled = [
+            pltpu.roll(window_ref[part, :, j * LANES : (j + 1) * LANES] * scale, lane0, 1)
+            for j in range(width)
+        ]
+        for j in range(width + 1):
+            above = rolled[j] if j < width else zero
+            below = rolled[j - 1] if j > 0 else zero
+            acc_ref[part, tile0 + j, pl.ds(row, side), :] += jnp.where(inside, above, below)
+
+
 def propagate_body(
     rows_ref, cols_ref, flag_ref, tile_ref, above_ref, below_ref, outer_ref, inner_ref, own_ref,
     other_ref, amp_ref, table_ref, grad_ref, rim_outer_ref, rim_inner_ref, keep_ref, send_ref,
-    ext_f32, patch_ref, far_ref, acc_ref, probe_ref, probe_acc, scale_ref,
+    ext_f32, patch_ref, next_ref, window_ref, acc_ref, probe_ref, probe_acc, low_ref, wide_ref,
+    far_ref, ratio_ref, scale_ref,
 ):
     modes, _, side, _ = probe_ref.shape
     half = side // 2
     step = pl.program_id(0)
+    count = pl.num_programs(0)
     tiles = ext_f32.shape[1]
     edge = half // LANES
     tile_rows = tile_ref.shape[1]
     odd = flag_ref[0]
     upper = flag_ref[1]
     share = modes // 2
+    f32 = jnp.float32
+    bf16 = jnp.bfloat16
 
     @pl.when(step == 0)
     def _():
-        probe_ref[pl.ds(upper * share, share)] = own_ref[...].astype(jnp.float32)
-        probe_ref[pl.ds((1 - upper) * share, share)] = other_ref[...].astype(jnp.float32)
+        probe_ref[pl.ds(upper * share, share)] = own_ref[...].astype(f32)
+        probe_ref[pl.ds((1 - upper) * share, share)] = other_ref[...].astype(f32)
         for part in range(2):
             for tile in range(edge):
                 at = slice(tile * LANES, (tile + 1) * LANES)
                 last = (tiles - edge) * odd + tile
                 first = (tiles - edge) * (1 - odd) + tile
-                ext_f32[part, last] = outer_ref[part, :, at].astype(jnp.float32)
-                ext_f32[part, first] = inner_ref[part, :, at].astype(jnp.float32)
+                ext_f32[part, last] = outer_ref[part, :, at].astype(f32)
+                ext_f32[part, first] = inner_ref[part, :, at].astype(f32)
             for tile in range(edge, tiles - edge):
                 at = slice((tile - edge) * LANES, (tile - edge + 1) * LANES)
-                ext_f32[part, tile, :half] = above_ref[part, :, at].astype(jnp.float32)
-                ext_f32[part, tile, half : half + tile_rows] = tile_ref[part, :, at].astype(
-                    jnp.float32
-                )
-                ext_f32[part, tile, half + tile_rows :] = below_ref[part, :, at].astype(
-                    jnp.float32
-                )
-        acc_ref[...] = jnp.zeros(acc_ref.shape, jnp.float32)
-        probe_acc[...] = jnp.zeros(probe_acc.shape, jnp.float32)
-        power = jnp.zeros((side, side), jnp.float32)
+                ext_f32[part, tile, :half] = above_ref[part, :, at].astype(f32)
+                ext_f32[part, tile, half : half + tile_rows] = tile_ref[part, :, at].astype(f32)
+                ext_f32[part, tile, half + tile_rows :] = below_ref[part, :, at].astype(f32)
+        acc_ref[...] = jnp.zeros(acc_ref.shape, f32)
+        probe_acc[...] = jnp.zeros(probe_acc.shape, f32)
+        window_ref[...] = jnp.zeros(window_ref.shape, f32)
+        power = jnp.zeros((side, side), f32)
         for mode in range(modes):
             for part in range(2):
                 values = probe_ref[mode, part]
                 power += values * values
         scale_ref[0] = 1.0 / (jnp.max(power) + EPSILON)
-
-    row = rows_ref[step]
-    col = cols_ref[step]
-    tile0 = col // LANES
-    lane0 = col % LANES
-    width = side // LANES
-    lane = lax.broadcasted_iota(jnp.int32, (side, LANES), 1)
-    left_part = lane < LANES - lane0
-    for part in range(2):
-        rolled = [
-            pltpu.roll(
-                ext_f32[part, tile0 + j, pl.ds(row, side), :], (LANES - lane0) % LANES, 1
-            )
-            for j in range(width + 1)
-        ]
-        for j in range(width):
-            patch_ref[part, :, j * LANES : (j + 1) * LANES] = jnp.where(
-                left_part, rolled[j], rolled[j + 1]
-            )
-
+        take_patch(ext_f32, next_ref, rows_ref[0], cols_ref[0])
+
+    before = jnp.maximum(step - 1, 0)
+    add_window(acc_ref, window_ref, rows_ref[before], cols_ref[before], scale_ref[0])
+    patch_ref[...] = next_ref[...]
+
+    chunk = 16
     table_le = table_ref[0]
     table_lo = table_ref[1]
     table_re = table_ref[2]
     table_ro = table_ref[3]
-    power_e = jnp.zeros((side, half), jnp.float32)
-    power_o = jnp.zeros((side, half), jnp.float32)
-    for mode in range(modes):
-        wave = []
-        for rows in (slice(0, half), slice(half, side)):
-            qr = probe_ref[mode, 0, rows, :]
-            qi = probe_ref[mode, 1, rows, :]
-            pr = patch_ref[0, rows, :]
-            pi = patch_ref[1, rows, :]
-            wave.append((qr * pr - qi * pi, qr * pi + qi * pr))
-        (lo_re, lo_im), (hi_re, hi_im) = wave
-        sums = jnp.concatenate(
-            [(lo_re + hi_re).astype(jnp.bfloat16), (lo_im + hi_im).astype(jnp.bfloat16)], axis=0
-        )
-        diffs = jnp.concatenate(
-            [(lo_re - hi_re).astype(jnp.bfloat16), (lo_im - hi_im).astype(jnp.bfloat16)], axis=0
-        )
-        evens, odds = [], []
-        for half_field in (mm(table_le, sums), mm(table_lo, diffs)):
-            re_lo, re_hi = half_field[:half, :half], half_field[:half, half:]
-            im_lo, im_hi = half_field[half:, :half], half_field[half:, half:]
-            evens.append(
-                jnp.concatenate(
-                    [(re_lo + re_hi).astype(jnp.bfloat16), (im_lo + im_hi).astype(jnp.bfloat16)],
-                    axis=1,
+
+    def make_waves(mode):
+        for first in range(0, half, chunk):
+            wave = []
+            for rows in (slice(first, first + chunk), slice(half + first, half + first + chunk)):
+                qr = probe_ref[mode, 0, rows, :]
+                qi = probe_ref[mode, 1, rows, :]
+                pr = patch_ref[0, rows, :]
+                pi = patch_ref[1, rows, :]
+                wave.append((qr * pr - qi * pi, qr * pi + qi * pr))
+            for part in range(2):
+                rows = slice(part * half + first, part * half + first + chunk)
+                low_ref[mode, 0, rows, :] = (wave[0][part] + wave[1][part]).astype(bf16)
+                low_ref[mode, 1, rows, :] = (wave[0][part] - wave[1][part]).astype(bf16)
+
+    def left(mode):
+        wide_ref[mode, 0] = mm(table_le, low_ref[mode, 0])
+        wide_ref[mode, 1] = mm(table_lo, low_ref[mode, 1])
+
+    def split_columns(mode):
+        for index in range(2):
+            for first in range(0, half, chunk):
+                rows = slice(index * half + first, index * half + first + chunk)
+                for part in range(2):
+                    source = slice(part * half + first, part * half + first + chunk)
+                    at = slice(part * half, (part + 1) * half)
+                    near = wide_ref[mode, index, source, :half]
+                    far = wide_ref[mode, index, source, half:]
+                    low_ref[mode, 2, rows, at] = (near + far).astype(bf16)
+                    low_ref[mode, 3, rows, at] = (near - far).astype(bf16)
+
+    def right(mode):
+        far_ref[mode, 0] = mm(low_ref[mode, 2], table_re)
+        far_ref[mode, 1] = mm(low_ref[mode, 3], table_ro)
+
+    def make_ratio():
+        for index in range(2):
+            for first in range(0, side, chunk):
+                rows = slice(first, first + chunk)
+                power = jnp.zeros((chunk, half), f32)
+                for mode in range(modes):
+                    re = far_ref[mode, index, rows, :half]
+                    im = far_ref[mode, index, rows, half:]
+                    power += re * re + im * im
+                at = slice(index * half, (index + 1) * half)
+                ratio_ref[rows, at] = (
+                    amp_ref[0, rows, at] * lax.rsqrt(jnp.maximum(power, 1.0)) - 1.0
                 )
-            )
-            odds.append(
-                jnp.concatenate(
-                    [(re_lo - re_hi).astype(jnp.bfloat16), (im_lo - im_hi).astype(jnp.bfloat16)],
-                    axis=1,
-                )
-            )
-        far_e = mm(jnp.concatenate(evens, axis=0), table_re)
-        far_o = mm(jnp.concatenate(odds, axis=0), table_ro)
-        far_ref[mode, 0] = far_e
-        far_ref[mode, 1] = far_o
-        power_e += far_e[:, :half] * far_e[:, :half] + far_e[:, half:] * far_e[:, half:]
-        power_o += far_o[:, :half] * far_o[:, :half] + far_o[:, half:] * far_o[:, half:]
-
-    ratio_e = amp_ref[0, :, :half] * lax.rsqrt(jnp.maximum(power_e, 1.0)) - 1.0
-    ratio_o = amp_ref[0, :, half:] * lax.rsqrt(jnp.maximum(power_o, 1.0)) - 1.0
-
-    obj = [[None, None], [None, None]]
-    for mode in range(modes):
-        far_e = far_ref[mode, 0]
-        far_o = far_ref[mode, 1]
-        diff_e = jnp.concatenate(
-            [
-                (far_e[:, :half] * ratio_e).astype(jnp.bfloat16),
-                (far_e[:, half:] * ratio_e).astype(jnp.bfloat16),
-            ],
-            axis=1,
-        )
-        diff_o = jnp.concatenate(
-            [
-                (far_o[:, :half] * ratio_o).astype(jnp.bfloat16),
-                (far_o[:, half:] * ratio_o).astype(jnp.bfloat16),
-            ],
-            axis=1,
-        )
-        u = mm(diff_e, table_le)
-        v = mm(diff_o, table_lo)
-        total = (u + v).astype(jnp.bfloat16)
-        gap = (u - v).astype(jnp.bfloat16)
-        backs = []
-        for rows in (slice(0, half), slice(half, side)):
-            backs.append(
-                jnp.concatenate(
-                    [
-                        jnp.concatenate([total[rows, :half], gap[rows, :half]], axis=1),
-                        jnp.concatenate([total[rows, half:], gap[rows, half:]], axis=1),
-                    ],
-                    axis=0,
-                )
-            )
-        p = mm(table_re, backs[0])
-        q = mm(table_ro, backs[1])
-        for index, sign in ((0, 1), (1, -1)):
-            rows = slice(index * half, (index + 1) * half)
-            if sign > 0:
-                chi_re = p[:half] + q[:half]
-                chi_im = p[half:] + q[half:]
-            else:
-                chi_re = p[:half] - q[:half]
-                chi_im = p[half:] - q[half:]
-            qr = probe_ref[mode, 0, rows, :]
-            qi = probe_ref[mode, 1, rows, :]
-            pr = patch_ref[0, rows, :]
-            pi = patch_ref[1, rows, :]
-            term_re = qr * chi_re + qi * chi_im
-            term_im = qr * chi_im - qi * chi_re
-            if mode == 0:
-                obj[index] = [term_re, term_im]
-            else:
-                obj[index][0] += term_re
-                obj[index][1] += term_im
-            probe_acc[mode, 0, rows, :] += pr * chi_re + pi * chi_im
-            probe_acc[mode, 1, rows, :] += pr * chi_im - pi * chi_re
-
-    lane_h = lax.broadcasted_iota(jnp.int32, (half, LANES), 1)
-    right_part = lane_h >= lane0
-    scale = scale_ref[0]
-    for index in range(2):
-        for part in range(2):
-            values = obj[index][part] * scale
-            rolled = [
-                pltpu.roll(values[:, j * LANES : (j + 1) * LANES], lane0, 1) for j in range(width)
-            ]
-            where = pl.ds(row + index * half, half)
-            for j in range(width + 1):
-                above = rolled[j] if j < width else jnp.zeros_like(rolled[0])
-                below = rolled[j - 1] if j > 0 else jnp.zeros_like(rolled[0])
-                acc_ref[part, tile0 + j, where, :] += jnp.where(right_part, above, below)
-
-    @pl.when(step == pl.num_programs(0) - 1)
+
+    def make_diffs(mode):
+        for index in range(2):
+            for first in range(0, side, chunk):
+                rows = slice(first, first + chunk)
+                ratio = ratio_ref[rows, index * half : (index + 1) * half]
+                for part in range(2):
+                    at = slice(part * half, (part + 1) * half)
+                    low_ref[mode, index, rows, at] = (
+                        far_ref[mode, index, rows, at] * ratio
+                    ).astype(bf16)
+
+    def right_back(mode):
+        wide_ref[mode, 0] = mm(low_ref[mode, 0], table_le)
+        wide_ref[mode, 1] = mm(low_ref[mode, 1], table_lo)
+
+    def join_columns(mode):
+        for index in range(2):
+            for first in range(0, half, chunk):
+                source = slice(index * half + first, index * half + first + chunk)
+                for part in range(2):
+                    at = slice(part * half, (part + 1) * half)
+                    rows = slice(part * half + first, part * half + first + chunk)
+                    u = wide_ref[mode, 0, source, at]
+                    v = wide_ref[mode, 1, source, at]
+                    low_ref[mode, 2 + index, rows, :half] = (u + v).astype(bf16)
+                    low_ref[mode, 2 + index, rows, half:] = (u - v).astype(bf16)
+
+    def left_back(mode):
+        far_ref[mode, 0] = mm(table_re, low_ref[mode, 2])
+        far_ref[mode, 1] = mm(table_ro, low_ref[mode, 3])
+
+    def gather_terms(mode):
+        for first in range(0, half, 8):
+            even_re = far_ref[mode, 0, first : first + 8, :]
+            odd_re = far_ref[mode, 1, first : first + 8, :]
+            even_im = far_ref[mode, 0, half + first : half + first + 8, :]
+            odd_im = far_ref[mode, 1, half + first : half + first + 8, :]
+            for index in range(2):
+                rows = slice(index * half + first, index * half + first + 8)
+                chi_re = even_re + odd_re if index == 0 else even_re - odd_re
+                chi_im = even_im + odd_im if index == 0 else even_im - odd_im
+                qr = probe_ref[mode, 0, rows, :]
+                qi = probe_ref[mode, 1, rows, :]
+                pr = patch_ref[0, rows, :]
+                pi = patch_ref[1, rows, :]
+                term_re = qr * chi_re + qi * chi_im
+                term_im = qr * chi_im - qi * chi_re
+                if mode > 0:
+                    term_re += window_ref[0, rows, :]
+                    term_im += window_ref[1, rows, :]
+                window_ref[0, rows, :] = term_re
+                window_ref[1, rows, :] = term_im
+                probe_acc[mode, 0, rows, :] += pr * chi_re + pi * chi_im
+                probe_acc[mode, 1, rows, :] += pr * chi_im - pi * chi_re
+
+    for pair in range(0, modes, 2):
+        make_waves(pair)
+        left(pair)
+        make_waves(pair + 1)
+        left(pair + 1)
+        split_columns(pair)
+        right(pair)
+        split_columns(pair + 1)
+        right(pair + 1)
+    make_ratio()
+    for pair in range(0, modes, 2):
+        make_diffs(pair)
+        right_back(pair)
+        make_diffs(pair + 1)
+        right_back(pair + 1)
+        if pair > 0:
+            gather_terms(pair - 2)
+        join_columns(pair)
+        left_back(pair)
+        join_columns(pair + 1)
+        left_back(pair + 1)
+        if pair > 0:
+            gather_terms(pair - 1)
+    gather_terms(modes - 2)
+    gather_terms(modes - 1)
+
+    after = jnp.minimum(step + 1, count - 1)
+    take_patch(ext_f32, next_ref, rows_ref[after], cols_ref[after])
+
+    @pl.when(step == count - 1)
     def _():
+        add_window(acc_ref, window_ref, rows_ref[step], cols_ref[step], scale_ref[0])
         keep_ref[...] = probe_acc[pl.ds(upper * share, share)]
         send_ref[...] = probe_acc[pl.ds((1 - upper) * share, share)].astype(send_ref.dtype)
         for part in range(2):
@@ -313,10 +358,15 @@
             scratch_shapes=[
                 pltpu.VMEM((2, tiles, ext_rows, LANES), jnp.float32),
                 pltpu.VMEM((2, side, side), jnp.float32),
-                pltpu.VMEM((modes, 2, side, side), jnp.float32),
+                pltpu.VMEM((2, side, side), jnp.float32),
+                pltpu.VMEM((2, side, side), jnp.float32),
                 pltpu.VMEM((2, tiles, ext_rows, LANES), jnp.float32),
                 pltpu.VMEM((modes, 2, side, side), jnp.float32),
                 pltpu.VMEM((modes, 2, side, side), jnp.float32),
+                pltpu.VMEM((modes, 4, side, side), jnp.bfloat16),
+                pltpu.VMEM((modes, 2, side, side), jnp.float32),
+                pltpu.VMEM((modes, 2, side, side), jnp.float32),
+                pltpu.VMEM((side, side), jnp.float32),
                 pltpu.SMEM((1,), jnp.float32),
             ],
         ),
@@ -444,11 +494,10 @@
             probe_parts = [part.reshape(split) for part in parts]
         else:
             rest = (probe_share - low_share.astype(jnp.float32)).astype(jnp.bfloat16)
-            parts = [
-                part.astype(jnp.float32) + more.astype(jnp.float32)
-                for part, more in zip(parts, join_shares(rest))
-            ]
-            probe = in_order(upper, *parts).reshape(probe_modes.shape)
+            rests = join_shares(rest)
+            low = in_order(upper, *parts).astype(jnp.float32)
+            probe = low + in_order(upper, *rests).astype(jnp.float32)
+            probe = probe.reshape(probe_modes.shape)
     return (current, probe)
 
 

time: 220 us -> 216 us (0.982)
  Pallas kernels: 52.7 us -> 49.2 us
  other arithmetic: 19.6 us -> 17.4 us
    pallas_call x2, Pallas kernels: 52.7 us -> 49.2 us  [propagate(): pl.pallas_call(propagate_body, out_shape=outs, grid_spec=pltpu.PrefetchSc...]
  transfers between devices with their start and end apart: 34 -> 34, of which waited for: 19 -> 18; matrix products, arithmetic and copies ran while one was open for 11% -> 11% of each run, Pallas kernels for 0% -> 0%
where the time goes in v3:
time: 216 us; the launch traced here: 215 us
  starting transfers between devices  65.8 us (30%)
  waiting for transfers between devices  63.6 us (29%)
  Pallas kernels  49.2 us (23%)
  other arithmetic  17.4 us (8%)
  local copies, waits for them, and re-layouts  11.9 us (6%)
  matrix products  5.38 us (2%)
    pallas_call x2, Pallas kernels, propagate(): pl.pallas_call(propagate_body, out_shape=outs, grid_spec=pltpu.PrefetchSc...  49.2 us
    ppermute x18, waiting for transfers between devices, swap_bit(): lax.ppermute(values, axis, [(i, i ^ bit) for i in range(lax.axis_size(axi...  44.9 us
    ppermute x18, starting transfers between devices, swap_bit(): lax.ppermute(values, axis, [(i, i ^ bit) for i in range(lax.axis_size(axi...  31.2 us
    ppermute x4, starting transfers between devices, shift_both(): lax.ppermute(before, axis, [(target, source) for source, target in up])  13.9 us
    ppermute x4, starting transfers between devices, shift_both(): previous = lax.ppermute(after, axis, up)  11.7 us
    ppermute x4, waiting for transfers between devices, shift_both(): previous = lax.ppermute(after, axis, up)  11.3 us
    ppermute x4, waiting for transfers between devices, shift_both(): lax.ppermute(before, axis, [(target, source) for source, target in up])  7.37 us
    ppermute x4, starting transfers between devices, swap_both(): inner = lax.ppermute(inner, axis, inner_pairs)  6.26 us
  transfers between devices with their start and end apart: 34, of which 18 were waited for; matrix products, arithmetic and copies ran while one was open for 11% of the time, Pallas kernels for 0%

profile of v3, /device:TPU:8, one launch (start us, length us, event | category | flops | bytes accessed | tf_op | source)
XLA Modules:
  0.0 214.8 jit_solution(1927366403388866489)
XLA Ops:
  2.1 3.3 %collective-permute-start.1 = (bf16[2,128,512]{2,1,0:T(8,128)(2,1)S(1)}, bf16[2,128,512]{2,1,0:T(8,128)(2,1)S(1)}, u32[]{:S(2)}, u32[]{:S(2)}) collective-permute-start(bf16[2,128,512]{2,1,0:T(8,128)(2,1)S(1)} %get-tuple-element.48), channel_id=1, source_target_pairs={{4,0},{8,4},{12,8},{16,12},{20,16},{24,20},{28,24},{5,1},{9,5},{13... | collective-permute-start | bytes 786440 | tf_op jit(solution)/shard_map/ppermute | solution.py:26
  5.4 2.6 %collective-permute-start = (bf16[2,128,512]{2,1,0:T(8,128)(2,1)S(1)}, bf16[2,128,512]{2,1,0:T(8,128)(2,1)S(1)}, u32[]{:S(2)}, u32[]{:S(2)}) collective-permute-start(bf16[2,128,512]{2,1,0:T(8,128)(2,1)S(1)} %get-tuple-element.49), channel_id=1, source_target_pairs={{0,4},{4,8},{8,12},{12,16},{16,20},{20,24},{24,28},{1,5},{5,9},{9,... | collective-permute-start | bytes 786440 | tf_op jit(solution)/shard_map/ppermute | solution.py:25
  8.0 2.7 %fusion.21 = f32[256,6,256]{2,0,1:T(8,128)S(1)} fusion(f32[256,256,1]{1,0,2:T(8,128)S(1)} %copy-done.12, f32[6,256,256]{2,1,0:T(8,128)S(1)} %copy-done), kind=kOutput, calls=%fused_computation.70 | convolution fusion | flops 1207959552 | bytes 3407872 | tf_op jit(solution)/shard_map/brc,ck->brk/dot_general | solution.py:67
  10.7 2.7 %fusion.2.amp_ref = f32[6,256,256]{2,1,0:T(8,128)} fusion(f32[256,256,1]{1,0,2:T(8,128)S(1)} %copy-done.12, f32[256,6,256]{2,0,1:T(8,128)S(1)} %fusion.21), kind=kOutput, calls=%fused_computation.5 | convolution fusion | flops 1207959552 | bytes 3407872 | tf_op jit(solution)/shard_map/rk,brc->bkc/dot_general | solution.py:71
  13.5 2.6 %dynamic-slice_convert_fusion = (bf16[1024,256]{1,0:T(8,128)(2,1)}, bf16[1024,256]{1,0:T(8,128)(2,1)}) fusion(f32[2048,256]{1,0:T(8,128)} %bitcast.65, s32[]{:T(128)S(6)} %select_n.233, s32[]{:T(128)S(6)} %select_n.232), kind=kLoop, calls=%fused_computation.12 | loop fusion | bytes 2097160 | tf_op jit(solution)/shard_map/convert_element_type | solution.py:478
  20.7 24.6 %propagate.2 = (f32[2,512,512]{2,1,0:T(8,128)}, bf16[2,512,128]{2,1,0:T(8,128)(2,1)}, bf16[2,512,128]{2,1,0:T(8,128)(2,1)}, f32[2,2,256,256]{3,2,1,0:T(8,128)}, bf16[2,2,256,256]{3,2,1,0:T(8,128)(2,1)}) custom-call(s32[6]{0:T(128)} %get-tuple-element.59.rows_ref, s32[6]{0:T(128)} %get-tuple-element.58.cols_ref, s32[2]{0:T(128)} %pad_add_fusion.flag_ref, ...), custom_call_target="tpu_custom_call" | custom-call | tf_op jit(solution)/shard_map/propagate/pallas_call | solution.py:345
  45.3 6.1 %collective-permute-start.4 = (bf16[2,512,128]{2,1,0:T(8,128)(2,1)}, bf16[2,512,128]{2,1,0:T(8,128)(2,1)S(1)}, u32[]{:S(2)}, u32[]{:S(2)}) collective-permute-start(bf16[2,512,128]{2,1,0:T(8,128)(2,1)} %get-tuple-element.13), channel_id=1, source_target_pairs={{0,1},{1,0},{2,3},{3,2},{4,5},{5,4},{6,7},{7,6},{8,9},{9,8},{10,11... | collective-permute-start | bytes 786440 | tf_op jit(solution)/shard_map/ppermute | solution.py:36
  52.1 2.5 %collective-permute-start.12 = (bf16[1024,256]{1,0:T(8,128)(2,1)}, bf16[1024,256]{1,0:T(8,128)(2,1)S(1)}, u32[]{:S(2)}, u32[]{:S(2)}) collective-permute-start(bf16[1024,256]{1,0:T(8,128)(2,1)} %bitcast.67), channel_id=1, source_target_pairs={{0,1},{1,0},{2,3},{3,2},{4,5},{5,4},{6,7},{7,6},{8,9},{9,8},{10,11... | collective-permute-start | bytes 1572872 | tf_op jit(solution)/shard_map/ppermute | solution.py:20
  57.8 4.2 %collective-permute-start.13 = (bf16[512,256]{1,0:T(8,128)(2,1)S(1)}, bf16[512,256]{1,0:T(8,128)(2,1)S(1)}, u32[]{:S(2)}, u32[]{:S(2)}) collective-permute-start(bf16[512,256]{1,0:T(8,128)(2,1)S(1)} %dynamic-slice_convert_fusion.3), channel_id=1, source_target_pairs={{0,2},{1,3},{2,0},{3,1},{4,6},{5,7},{6,4},{7,5},{8,10},{9,11},{10,... | collective-permute-start | bytes 786440 | tf_op jit(solution)/shard_map/ppermute | solution.py:20
  62.4 6.7 %collective-permute-done.13 = bf16[512,256]{1,0:T(8,128)(2,1)S(1)} collective-permute-done((bf16[512,256]{1,0:T(8,128)(2,1)S(1)}, bf16[512,256]{1,0:T(8,128)(2,1)S(1)}, u32[]{:S(2)}, u32[]{:S(2)}) %collective-permute-start.13) | collective-permute-done | bytes 262176 | tf_op jit(solution)/shard_map/ppermute | solution.py:20
  69.6 4.4 %collective-permute-start.6 = (bf16[2,128,512]{2,1,0:T(8,128)(2,1)S(1)}, bf16[2,128,512]{2,1,0:T(8,128)(2,1)S(1)}, u32[]{:S(2)}, u32[]{:S(2)}) collective-permute-start(bf16[2,128,512]{2,1,0:T(8,128)(2,1)S(1)} %get-tuple-element.32), channel_id=1, source_target_pairs={{0,4},{4,8},{8,12},{12,16},{16,20},{20,24},{24,28},{1,5},{5,9},{9,... | collective-permute-start | bytes 786440 | tf_op jit(solution)/shard_map/ppermute | solution.py:25
  74.0 2.8 %collective-permute-start.7 = (bf16[2,128,512]{2,1,0:T(8,128)(2,1)S(1)}, bf16[2,128,512]{2,1,0:T(8,128)(2,1)S(1)}, u32[]{:S(2)}, u32[]{:S(2)}) collective-permute-start(bf16[2,128,512]{2,1,0:T(8,128)(2,1)S(1)} %get-tuple-element.33), channel_id=1, source_target_pairs={{4,0},{8,4},{12,8},{16,12},{20,16},{24,20},{28,24},{5,1},{9,5},{13... | collective-permute-start | bytes 786440 | tf_op jit(solution)/shard_map/ppermute | solution.py:26
  76.8 2.3 %collective-permute-start.15 = (bf16[128,256]{1,0:T(8,128)(2,1)S(1)}, bf16[128,256]{1,0:T(8,128)(2,1)S(1)}, u32[]{:S(2)}, u32[]{:S(2)}) collective-permute-start(bf16[128,256]{1,0:T(8,128)(2,1)S(1)} %dynamic-slice_convert_fusion.7), channel_id=1, source_target_pairs={{0,16},{4,20},{8,24},{12,28},{16,0},{20,4},{24,8},{28,12},{1,17},{... | collective-permute-start | bytes 196616 | tf_op jit(solution)/shard_map/ppermute | solution.py:20
  79.1 5.1 %collective-permute-done.6 = bf16[2,128,512]{2,1,0:T(8,128)(2,1)S(1)} collective-permute-done((bf16[2,128,512]{2,1,0:T(8,128)(2,1)S(1)}, bf16[2,128,512]{2,1,0:T(8,128)(2,1)S(1)}, u32[]{:S(2)}, u32[]{:S(2)}) %collective-permute-start.6) | collective-permute-done | bytes 262176 | tf_op jit(solution)/shard_map/ppermute | solution.py:25
  84.2 3.4 %collective-permute-done.7 = bf16[2,128,512]{2,1,0:T(8,128)(2,1)S(1)} collective-permute-done((bf16[2,128,512]{2,1,0:T(8,128)(2,1)S(1)}, bf16[2,128,512]{2,1,0:T(8,128)(2,1)S(1)}, u32[]{:S(2)}, u32[]{:S(2)}) %collective-permute-start.7) | collective-permute-done | bytes 262176 | tf_op jit(solution)/shard_map/ppermute | solution.py:26
  89.6 3.9 %collective-permute-start.9 = (bf16[2,128,512]{2,1,0:T(8,128)(2,1)}, bf16[2,128,512]{2,1,0:T(8,128)(2,1)}, u32[]{:S(2)}, u32[]{:S(2)}) collective-permute-start(bf16[2,128,512]{2,1,0:T(8,128)(2,1)} %get-tuple-element.40), channel_id=1, source_target_pairs={{4,0},{8,4},{12,8},{16,12},{20,16},{24,20},{28,24},{5,1},{9,5},{13... | collective-permute-start | bytes 786440 | tf_op jit(solution)/shard_map/ppermute | solution.py:26
  102.6 2.3 %collective-permute-start.18 = (bf16[256,256]{1,0:T(8,128)(2,1)S(1)}, bf16[256,256]{1,0:T(8,128)(2,1)S(1)}, u32[]{:S(2)}, u32[]{:S(2)}) collective-permute-start(bf16[256,256]{1,0:T(8,128)(2,1)S(1)} %bitcast_select_fusion.5), channel_id=1, source_target_pairs={{0,8},{4,12},{8,0},{12,4},{16,24},{20,28},{24,16},{28,20},{1,9},{5... | collective-permute-start | bytes 393224 | tf_op jit(solution)/shard_map/ppermute | solution.py:20
  104.9 2.9 %collective-permute-done.18 = bf16[256,256]{1,0:T(8,128)(2,1)S(1)} collective-permute-done((bf16[256,256]{1,0:T(8,128)(2,1)S(1)}, bf16[256,256]{1,0:T(8,128)(2,1)S(1)}, u32[]{:S(2)}, u32[]{:S(2)}) %collective-permute-start.18) | collective-permute-done | bytes 131104 | tf_op jit(solution)/shard_map/ppermute | solution.py:20
  110.5 4.5 %collective-permute-done.19 = bf16[512,256]{1,0:T(8,128)(2,1)S(1)} collective-permute-done((bf16[512,256]{1,0:T(8,128)(2,1)S(1)}, bf16[512,256]{1,0:T(8,128)(2,1)S(1)}, u32[]{:S(2)}, u32[]{:S(2)}) %collective-permute-start.19) | collective-permute-done | bytes 262176 | tf_op jit(solution)/shard_map/ppermute | solution.py:20
  119.0 24.6 %propagate.3 = (f32[2,512,512]{2,1,0:T(8,128)}, bf16[2,512,128]{2,1,0:T(8,128)(2,1)}, bf16[2,512,128]{2,1,0:T(8,128)(2,1)}, f32[2,2,256,256]{3,2,1,0:T(8,128)}, bf16[2,2,256,256]{3,2,1,0:T(8,128)(2,1)}) custom-call(s32[6]{0:T(128)} %get-tuple-element.59.rows_ref, s32[6]{0:T(128)} %get-tuple-element.58.cols_ref, s32[2]{0:T(128)} %pad_add_fusion.flag_ref, ...), custom_call_target="tpu_custom_call" | custom-call | tf_op jit(solution)/shard_map/propagate/pallas_call | solution.py:345
  143.6 6.3 %collective-permute-start.25 = (bf16[1024,256]{1,0:T(8,128)(2,1)}, bf16[1024,256]{1,0:T(8,128)(2,1)S(1)}, u32[]{:S(2)}, u32[]{:S(2)}) collective-permute-start(bf16[1024,256]{1,0:T(8,128)(2,1)} %bitcast.68), channel_id=1, source_target_pairs={{0,1},{1,0},{2,3},{3,2},{4,5},{5,4},{6,7},{7,6},{8,9},{9,8},{10,11... | collective-permute-start | bytes 1572872 | tf_op jit(solution)/shard_map/ppermute | solution.py:20
  153.5 8.2 %collective-permute-done.26 = bf16[512,256]{1,0:T(8,128)(2,1)S(1)} collective-permute-done((bf16[512,256]{1,0:T(8,128)(2,1)S(1)}, bf16[512,256]{1,0:T(8,128)(2,1)S(1)}, u32[]{:S(2)}, u32[]{:S(2)}) %collective-permute-start.26) | collective-permute-done | bytes 262176 | tf_op jit(solution)/shard_map/ppermute | solution.py:20
  164.0 3.2 %collective-permute-done.27 = bf16[256,256]{1,0:T(8,128)(2,1)S(1)} collective-permute-done((bf16[256,256]{1,0:T(8,128)(2,1)S(1)}, bf16[256,256]{1,0:T(8,128)(2,1)S(1)}, u32[]{:S(2)}, u32[]{:S(2)}) %collective-permute-start.27) | collective-permute-done | bytes 131104 | tf_op jit(solution)/shard_map/ppermute | solution.py:20
  167.3 5.2 %collective-permute-done.28 = bf16[128,256]{1,0:T(8,128)(2,1)S(1)} collective-permute-done((bf16[128,256]{1,0:T(8,128)(2,1)S(1)}, bf16[128,256]{1,0:T(8,128)(2,1)S(1)}, u32[]{:S(2)}, u32[]{:S(2)}) %collective-permute-start.28) | collective-permute-done | bytes 65568 | tf_op jit(solution)/shard_map/ppermute | solution.py:20
  172.5 4.5 %collective-permute-start.29 = (f32[128,256]{1,0:T(8,128)S(1)}, f32[128,256]{1,0:T(8,128)S(1)}, u32[]{:S(2)}, u32[]{:S(2)}) collective-permute-start(f32[128,256]{1,0:T(8,128)S(1)} %convert_add_fusion.7), channel_id=1, source_target_pairs={{0,4},{4,0},{8,12},{12,8},{16,20},{20,16},{24,28},{28,24},{1,5},{5... | collective-permute-start | bytes 393224 | tf_op jit(solution)/shard_map/ppermute | solution.py:20
  181.5 3.7 %collective-permute-done.30 = bf16[128,256]{1,0:T(8,128)(2,1)S(1)} collective-permute-done((bf16[128,256]{1,0:T(8,128)(2,1)S(1)}, bf16[128,256]{1,0:T(8,128)(2,1)S(1)}, u32[]{:S(2)}, u32[]{:S(2)}) %collective-permute-start.30) | collective-permute-done | bytes 65568 | tf_op jit(solution)/shard_map/ppermute | solution.py:20
  187.7 3.2 %collective-permute-done.31 = bf16[256,256]{1,0:T(8,128)(2,1)S(1)} collective-permute-done((bf16[256,256]{1,0:T(8,128)(2,1)S(1)}, bf16[256,256]{1,0:T(8,128)(2,1)S(1)}, u32[]{:S(2)}, u32[]{:S(2)}) %collective-permute-start.31) | collective-permute-done | bytes 131104 | tf_op jit(solution)/shard_map/ppermute | solution.py:20
  193.2 2.8 %collective-permute-start.23 = (bf16[2,128,512]{2,1,0:T(8,128)(2,1)}, bf16[2,128,512]{2,1,0:T(8,128)(2,1)}, u32[]{:S(2)}, u32[]{:S(2)}) collective-permute-start(bf16[2,128,512]{2,1,0:T(8,128)(2,1)} %get-tuple-element.30), channel_id=1, source_target_pairs={{0,4},{4,8},{8,12},{12,16},{16,20},{20,24},{24,28},{1,5},{5,9},{9,... | collective-permute-start | bytes 786440 | tf_op jit(solution)/shard_map/ppermute | solution.py:25
  195.9 4.0 %collective-permute-start.24 = (bf16[2,128,512]{2,1,0:T(8,128)(2,1)}, bf16[2,128,512]{2,1,0:T(8,128)(2,1)}, u32[]{:S(2)}, u32[]{:S(2)}) collective-permute-start(bf16[2,128,512]{2,1,0:T(8,128)(2,1)} %get-tuple-element.31), channel_id=1, source_target_pairs={{4,0},{8,4},{12,8},{16,12},{20,16},{24,20},{28,24},{5,1},{9,5},{13... | collective-permute-start | bytes 786440 | tf_op jit(solution)/shard_map/ppermute | solution.py:26
  200.4 5.3 %collective-permute-done.23 = bf16[2,128,512]{2,1,0:T(8,128)(2,1)} collective-permute-done((bf16[2,128,512]{2,1,0:T(8,128)(2,1)}, bf16[2,128,512]{2,1,0:T(8,128)(2,1)}, u32[]{:S(2)}, u32[]{:S(2)}) %collective-permute-start.23) | collective-permute-done | bytes 262176 | tf_op jit(solution)/shard_map/ppermute | solution.py:25
  205.8 2.5 %collective-permute-done.24 = bf16[2,128,512]{2,1,0:T(8,128)(2,1)} collective-permute-done((bf16[2,128,512]{2,1,0:T(8,128)(2,1)}, bf16[2,128,512]{2,1,0:T(8,128)(2,1)}, u32[]{:S(2)}, u32[]{:S(2)}) %collective-permute-start.24) | collective-permute-done | bytes 262176 | tf_op jit(solution)/shard_map/ppermute | solution.py:26
  208.2 3.2 %fusion.5 = f32[2,256,512]{2,1,0:T(8,128)} fusion(f32[2,512,512]{2,1,0:T(8,128)} %get-tuple-element.23, bf16[2,128,512]{2,1,0:T(8,128)(2,1)} %collective-permute-done.24, bf16[2,128,512]{2,1,0:T(8,128)(2,1)} %collective-permute-done.23, f32[2,256,512]{2,1,0:T(8,128)S(1)} %copy-done.1, bf16[2,128,512]{2,1,0:T(8,128)(2,1)} %copy-done.11, ...), kind=kLoop, calls=%fused_computation.7 | loop fusion | flops 3145728 | bytes 5242880 | tf_op jit(solution)/shard_map/add | solution.py:446
  (162 shorter events, 47.3 us)
Async XLA Ops:
  2.1 15.6 %collective-permute-start.1 = (bf16[2,128,512]{2,1,0:T(8,128)(2,1)S(1)}, bf16[2,128,512]{2,1,0:T(8,128)(2,1)S(1)}, u32[]{:S(2)}, u32[]{:S(2)}) collective-permute-start(bf16[2,128,512]{2,1,0:T(8,128)(2,1)S(1)} %get-tuple-element.48), channel_id=1, source_target_pairs={{4,0},{8,4},{12,8},{16,12},{20,16},{24,20},{28,24},{5,1},{9,5},{13... | collective-permute-start | bytes 786440 | tf_op jit(solution)/shard_map/ppermute | solution.py:26
  5.4 12.3 %collective-permute-start = (bf16[2,128,512]{2,1,0:T(8,128)(2,1)S(1)}, bf16[2,128,512]{2,1,0:T(8,128)(2,1)S(1)}, u32[]{:S(2)}, u32[]{:S(2)}) collective-permute-start(bf16[2,128,512]{2,1,0:T(8,128)(2,1)S(1)} %get-tuple-element.49), channel_id=1, source_target_pairs={{0,4},{4,8},{8,12},{12,16},{16,20},{20,24},{24,28},{1,5},{5,9},{9,... | collective-permute-start | bytes 786440 | tf_op jit(solution)/shard_map/ppermute | solution.py:25
  17.9 1.9 collective-permute-start.3
  18.0 1.9 collective-permute-start.2
  45.3 9.4 %collective-permute-start.4 = (bf16[2,512,128]{2,1,0:T(8,128)(2,1)}, bf16[2,512,128]{2,1,0:T(8,128)(2,1)S(1)}, u32[]{:S(2)}, u32[]{:S(2)}) collective-permute-start(bf16[2,512,128]{2,1,0:T(8,128)(2,1)} %get-tuple-element.13), channel_id=1, source_target_pairs={{0,1},{1,0},{2,3},{3,2},{4,5},{5,4},{6,7},{7,6},{8,9},{9,8},{10,11... | collective-permute-start | bytes 786440 | tf_op jit(solution)/shard_map/ppermute | solution.py:36
  51.4 3.3 %collective-permute-start.5 = (bf16[2,512,128]{2,1,0:T(8,128)(2,1)}, bf16[2,512,128]{2,1,0:T(8,128)(2,1)S(1)}, u32[]{:S(2)}, u32[]{:S(2)}) collective-permute-start(bf16[2,512,128]{2,1,0:T(8,128)(2,1)} %get-tuple-element.14), channel_id=1, source_target_pairs={{1,2},{2,1},{5,6},{6,5},{9,10},{10,9},{13,14},{14,13},{17,18},{18,... | collective-permute-start | bytes 786440 | tf_op jit(solution)/shard_map/ppermute | solution.py:35
  52.1 4.3 %collective-permute-start.12 = (bf16[1024,256]{1,0:T(8,128)(2,1)}, bf16[1024,256]{1,0:T(8,128)(2,1)S(1)}, u32[]{:S(2)}, u32[]{:S(2)}) collective-permute-start(bf16[1024,256]{1,0:T(8,128)(2,1)} %bitcast.67), channel_id=1, source_target_pairs={{0,1},{1,0},{2,3},{3,2},{4,5},{5,4},{6,7},{7,6},{8,9},{9,8},{10,11... | collective-permute-start | bytes 1572872 | tf_op jit(solution)/shard_map/ppermute | solution.py:20
  57.8 11.3 %collective-permute-start.13 = (bf16[512,256]{1,0:T(8,128)(2,1)S(1)}, bf16[512,256]{1,0:T(8,128)(2,1)S(1)}, u32[]{:S(2)}, u32[]{:S(2)}) collective-permute-start(bf16[512,256]{1,0:T(8,128)(2,1)S(1)} %dynamic-slice_convert_fusion.3), channel_id=1, source_target_pairs={{0,2},{1,3},{2,0},{3,1},{4,6},{5,7},{6,4},{7,5},{8,10},{9,11},{10,... | collective-permute-start | bytes 786440 | tf_op jit(solution)/shard_map/ppermute | solution.py:20
  69.1 7.6 %collective-permute-start.14 = (bf16[256,256]{1,0:T(8,128)(2,1)S(1)}, bf16[256,256]{1,0:T(8,128)(2,1)S(1)}, u32[]{:S(2)}, u32[]{:S(2)}) collective-permute-start(bf16[256,256]{1,0:T(8,128)(2,1)S(1)} %dynamic-slice_convert_fusion.5), channel_id=1, source_target_pairs={{0,8},{4,12},{8,0},{12,4},{16,24},{20,28},{24,16},{28,20},{1,9},{5... | collective-permute-start | bytes 393224 | tf_op jit(solution)/shard_map/ppermute | solution.py:20
  69.6 14.6 %collective-permute-start.6 = (bf16[2,128,512]{2,1,0:T(8,128)(2,1)S(1)}, bf16[2,128,512]{2,1,0:T(8,128)(2,1)S(1)}, u32[]{:S(2)}, u32[]{:S(2)}) collective-permute-start(bf16[2,128,512]{2,1,0:T(8,128)(2,1)S(1)} %get-tuple-element.32), channel_id=1, source_target_pairs={{0,4},{4,8},{8,12},{12,16},{16,20},{20,24},{24,28},{1,5},{5,9},{9,... | collective-permute-start | bytes 786440 | tf_op jit(solution)/shard_map/ppermute | solution.py:25
  74.0 13.6 %collective-permute-start.7 = (bf16[2,128,512]{2,1,0:T(8,128)(2,1)S(1)}, bf16[2,128,512]{2,1,0:T(8,128)(2,1)S(1)}, u32[]{:S(2)}, u32[]{:S(2)}) collective-permute-start(bf16[2,128,512]{2,1,0:T(8,128)(2,1)S(1)} %get-tuple-element.33), channel_id=1, source_target_pairs={{4,0},{8,4},{12,8},{16,12},{20,16},{24,20},{28,24},{5,1},{9,5},{13... | collective-permute-start | bytes 786440 | tf_op jit(solution)/shard_map/ppermute | solution.py:26
  76.8 11.1 %collective-permute-start.15 = (bf16[128,256]{1,0:T(8,128)(2,1)S(1)}, bf16[128,256]{1,0:T(8,128)(2,1)S(1)}, u32[]{:S(2)}, u32[]{:S(2)}) collective-permute-start(bf16[128,256]{1,0:T(8,128)(2,1)S(1)} %dynamic-slice_convert_fusion.7), channel_id=1, source_target_pairs={{0,16},{4,20},{8,24},{12,28},{16,0},{20,4},{24,8},{28,12},{1,17},{... | collective-permute-start | bytes 196616 | tf_op jit(solution)/shard_map/ppermute | solution.py:20
  88.0 5.5 %collective-permute-start.16 = (f32[128,256]{1,0:T(8,128)S(1)}, f32[128,256]{1,0:T(8,128)S(1)}, u32[]{:S(2)}, u32[]{:S(2)}) collective-permute-start(f32[128,256]{1,0:T(8,128)S(1)} %convert_add_fusion.8), channel_id=1, source_target_pairs={{0,4},{4,0},{8,12},{12,8},{16,20},{20,16},{24,28},{28,24},{1,5},{5... | collective-permute-start | bytes 393224 | tf_op jit(solution)/shard_map/ppermute | solution.py:20
  89.6 19.1 %collective-permute-start.9 = (bf16[2,128,512]{2,1,0:T(8,128)(2,1)}, bf16[2,128,512]{2,1,0:T(8,128)(2,1)}, u32[]{:S(2)}, u32[]{:S(2)}) collective-permute-start(bf16[2,128,512]{2,1,0:T(8,128)(2,1)} %get-tuple-element.40), channel_id=1, source_target_pairs={{4,0},{8,4},{12,8},{16,12},{20,16},{24,20},{28,24},{5,1},{9,5},{13... | collective-permute-start | bytes 786440 | tf_op jit(solution)/shard_map/ppermute | solution.py:26
  95.1 7.3 %collective-permute-start.17 = (bf16[128,256]{1,0:T(8,128)(2,1)S(1)}, bf16[128,256]{1,0:T(8,128)(2,1)S(1)}, u32[]{:S(2)}, u32[]{:S(2)}) collective-permute-start(bf16[128,256]{1,0:T(8,128)(2,1)S(1)} %get-tuple-element.24), channel_id=1, source_target_pairs={{0,16},{4,20},{8,24},{12,28},{16,0},{20,4},{24,8},{28,12},{1,17},{... | collective-permute-start | bytes 196616 | tf_op jit(solution)/shard_map/ppermute | solution.py:20
  98.7 11.8 %collective-permute-start.8 = (bf16[2,128,512]{2,1,0:T(8,128)(2,1)}, bf16[2,128,512]{2,1,0:T(8,128)(2,1)S(1)}, u32[]{:S(2)}, u32[]{:S(2)}) collective-permute-start(bf16[2,128,512]{2,1,0:T(8,128)(2,1)} %get-tuple-element.41), channel_id=1, source_target_pairs={{0,4},{4,8},{8,12},{12,16},{16,20},{20,24},{24,28},{1,5},{5,9},{9,... | collective-permute-start | bytes 786440 | tf_op jit(solution)/shard_map/ppermute | solution.py:25
  102.6 5.2 %collective-permute-start.18 = (bf16[256,256]{1,0:T(8,128)(2,1)S(1)}, bf16[256,256]{1,0:T(8,128)(2,1)S(1)}, u32[]{:S(2)}, u32[]{:S(2)}) collective-permute-start(bf16[256,256]{1,0:T(8,128)(2,1)S(1)} %bitcast_select_fusion.5), channel_id=1, source_target_pairs={{0,8},{4,12},{8,0},{12,4},{16,24},{20,28},{24,16},{28,20},{1,9},{5... | collective-permute-start | bytes 393224 | tf_op jit(solution)/shard_map/ppermute | solution.py:20
  108.6 6.4 %collective-permute-start.19 = (bf16[512,256]{1,0:T(8,128)(2,1)S(1)}, bf16[512,256]{1,0:T(8,128)(2,1)S(1)}, u32[]{:S(2)}, u32[]{:S(2)}) collective-permute-start(bf16[512,256]{1,0:T(8,128)(2,1)S(1)} %bitcast_select_fusion.3), channel_id=1, source_target_pairs={{0,2},{1,3},{2,0},{3,1},{4,6},{5,7},{6,4},{7,5},{8,10},{9,11},{10,... | collective-permute-start | bytes 786440 | tf_op jit(solution)/shard_map/ppermute | solution.py:20
  115.3 2.7 %collective-permute-start.20 = (bf16[1024,256]{1,0:T(8,128)(2,1)S(1)}, bf16[1024,256]{1,0:T(8,128)(2,1)S(1)}, u32[]{:S(2)}, u32[]{:S(2)}) collective-permute-start(bf16[1024,256]{1,0:T(8,128)(2,1)S(1)} %bitcast_select_fusion.1), channel_id=1, source_target_pairs={{0,1},{1,0},{2,3},{3,2},{4,5},{5,4},{6,7},{7,6},{8,9},{9,8},{10,11... | collective-permute-start | bytes 1572872 | tf_op jit(solution)/shard_map/ppermute | solution.py:20
  143.6 8.1 %collective-permute-start.25 = (bf16[1024,256]{1,0:T(8,128)(2,1)}, bf16[1024,256]{1,0:T(8,128)(2,1)S(1)}, u32[]{:S(2)}, u32[]{:S(2)}) collective-permute-start(bf16[1024,256]{1,0:T(8,128)(2,1)} %bitcast.68), channel_id=1, source_target_pairs={{0,1},{1,0},{2,3},{3,2},{4,5},{5,4},{6,7},{7,6},{8,9},{9,8},{10,11... | collective-permute-start | bytes 1572872 | tf_op jit(solution)/shard_map/ppermute | solution.py:20
  153.1 8.7 %collective-permute-start.26 = (bf16[512,256]{1,0:T(8,128)(2,1)S(1)}, bf16[512,256]{1,0:T(8,128)(2,1)S(1)}, u32[]{:S(2)}, u32[]{:S(2)}) collective-permute-start(bf16[512,256]{1,0:T(8,128)(2,1)S(1)} %dynamic-slice_convert_fusion.2), channel_id=1, source_target_pairs={{0,2},{1,3},{2,0},{3,1},{4,6},{5,7},{6,4},{7,5},{8,10},{9,11},{10,... | collective-permute-start | bytes 786440 | tf_op jit(solution)/shard_map/ppermute | solution.py:20
  161.8 5.3 %collective-permute-start.27 = (bf16[256,256]{1,0:T(8,128)(2,1)S(1)}, bf16[256,256]{1,0:T(8,128)(2,1)S(1)}, u32[]{:S(2)}, u32[]{:S(2)}) collective-permute-start(bf16[256,256]{1,0:T(8,128)(2,1)S(1)} %dynamic-slice_convert_fusion.4), channel_id=1, source_target_pairs={{0,8},{4,12},{8,0},{12,4},{16,24},{20,28},{24,16},{28,20},{1,9},{5... | collective-permute-start | bytes 393224 | tf_op jit(solution)/shard_map/ppermute | solution.py:20
  167.2 5.3 %collective-permute-start.28 = (bf16[128,256]{1,0:T(8,128)(2,1)S(1)}, bf16[128,256]{1,0:T(8,128)(2,1)S(1)}, u32[]{:S(2)}, u32[]{:S(2)}) collective-permute-start(bf16[128,256]{1,0:T(8,128)(2,1)S(1)} %dynamic-slice_convert_fusion.6), channel_id=1, source_target_pairs={{0,16},{4,20},{8,24},{12,28},{16,0},{20,4},{24,8},{28,12},{1,17},{... | collective-permute-start | bytes 196616 | tf_op jit(solution)/shard_map/ppermute | solution.py:20
  172.5 7.4 %collective-permute-start.29 = (f32[128,256]{1,0:T(8,128)S(1)}, f32[128,256]{1,0:T(8,128)S(1)}, u32[]{:S(2)}, u32[]{:S(2)}) collective-permute-start(f32[128,256]{1,0:T(8,128)S(1)} %convert_add_fusion.7), channel_id=1, source_target_pairs={{0,4},{4,0},{8,12},{12,8},{16,20},{20,16},{24,28},{28,24},{1,5},{5... | collective-permute-start | bytes 393224 | tf_op jit(solution)/shard_map/ppermute | solution.py:20
  176.9 4.5 %collective-permute-start.21 = (bf16[2,512,128]{2,1,0:T(8,128)(2,1)S(1)}, bf16[2,512,128]{2,1,0:T(8,128)(2,1)S(1)}, u32[]{:S(2)}, u32[]{:S(2)}) collective-permute-start(bf16[2,512,128]{2,1,0:T(8,128)(2,1)S(1)} %copy-done.28), channel_id=1, source_target_pairs={{0,1},{1,0},{2,3},{3,2},{4,5},{5,4},{6,7},{7,6},{8,9},{9,8},{10,11... | collective-permute-start | bytes 786440 | tf_op jit(solution)/shard_map/ppermute | solution.py:36
  177.0 4.5 %collective-permute-start.22 = (bf16[2,512,128]{2,1,0:T(8,128)(2,1)S(1)}, bf16[2,512,128]{2,1,0:T(8,128)(2,1)S(1)}, u32[]{:S(2)}, u32[]{:S(2)}) collective-permute-start(bf16[2,512,128]{2,1,0:T(8,128)(2,1)S(1)} %copy-done.27), channel_id=1, source_target_pairs={{1,2},{2,1},{5,6},{6,5},{9,10},{10,9},{13,14},{14,13},{17,18},{18,... | collective-permute-start | bytes 786440 | tf_op jit(solution)/shard_map/ppermute | solution.py:35
  179.9 5.2 %collective-permute-start.30 = (bf16[128,256]{1,0:T(8,128)(2,1)S(1)}, bf16[128,256]{1,0:T(8,128)(2,1)S(1)}, u32[]{:S(2)}, u32[]{:S(2)}) collective-permute-start(bf16[128,256]{1,0:T(8,128)(2,1)S(1)} %subtract_convert_fusion), channel_id=1, source_target_pairs={{0,16},{4,20},{8,24},{12,28},{16,0},{20,4},{24,8},{28,12},{1,17},{... | collective-permute-start | bytes 196616 | tf_op jit(solution)/shard_map/ppermute | solution.py:20
  185.3 5.6 %collective-permute-start.31 = (bf16[256,256]{1,0:T(8,128)(2,1)S(1)}, bf16[256,256]{1,0:T(8,128)(2,1)S(1)}, u32[]{:S(2)}, u32[]{:S(2)}) collective-permute-start(bf16[256,256]{1,0:T(8,128)(2,1)S(1)} %bitcast_select_fusion.4), channel_id=1, source_target_pairs={{0,8},{4,12},{8,0},{12,4},{16,24},{20,28},{24,16},{28,20},{1,9},{5... | collective-permute-start | bytes 393224 | tf_op jit(solution)/shard_map/ppermute | solution.py:20
  191.1 8.9 %collective-permute-start.32 = (bf16[512,256]{1,0:T(8,128)(2,1)S(1)}, bf16[512,256]{1,0:T(8,128)(2,1)S(1)}, u32[]{:S(2)}, u32[]{:S(2)}) collective-permute-start(bf16[512,256]{1,0:T(8,128)(2,1)S(1)} %bitcast_select_fusion.2), channel_id=1, source_target_pairs={{0,2},{1,3},{2,0},{3,1},{4,6},{5,7},{6,4},{7,5},{8,10},{9,11},{10,... | collective-permute-start | bytes 786440 | tf_op jit(solution)/shard_map/ppermute | solution.py:20
  193.2 12.6 %collective-permute-start.23 = (bf16[2,128,512]{2,1,0:T(8,128)(2,1)}, bf16[2,128,512]{2,1,0:T(8,128)(2,1)}, u32[]{:S(2)}, u32[]{:S(2)}) collective-permute-start(bf16[2,128,512]{2,1,0:T(8,128)(2,1)} %get-tuple-element.30), channel_id=1, source_target_pairs={{0,4},{4,8},{8,12},{12,16},{16,20},{20,24},{24,28},{1,5},{5,9},{9,... | collective-permute-start | bytes 786440 | tf_op jit(solution)/shard_map/ppermute | solution.py:25
  195.9 12.3 %collective-permute-start.24 = (bf16[2,128,512]{2,1,0:T(8,128)(2,1)}, bf16[2,128,512]{2,1,0:T(8,128)(2,1)}, u32[]{:S(2)}, u32[]{:S(2)}) collective-permute-start(bf16[2,128,512]{2,1,0:T(8,128)(2,1)} %get-tuple-element.31), channel_id=1, source_target_pairs={{4,0},{8,4},{12,8},{16,12},{20,16},{24,20},{28,24},{5,1},{9,5},{13... | collective-permute-start | bytes 786440 | tf_op jit(solution)/shard_map/ppermute | solution.py:26
  200.1 11.3 %collective-permute-start.33 = (bf16[1024,256]{1,0:T(8,128)(2,1)S(1)}, bf16[1024,256]{1,0:T(8,128)(2,1)}, u32[]{:S(2)}, u32[]{:S(2)}) collective-permute-start(bf16[1024,256]{1,0:T(8,128)(2,1)S(1)} %bitcast_select_fusion), channel_id=1, source_target_pairs={{0,1},{1,0},{2,3},{3,2},{4,5},{5,4},{6,7},{7,6},{8,9},{9,8},{10,11... | collective-permute-start | bytes 1572872 | tf_op jit(solution)/shard_map/ppermute | solution.py:20
  (31 other events, 367.4 us)
